TPU v7x, 32 devices: a whole 2x2x4 slice. The times are simulated.
32 devices in a mesh: gx: 8 (over y, x, core), gy: 4 (over z).
Axes of the slice: x: 2, y: 2, z: 4, core: 2. Of those that a mesh axis runs over, the one named last changes fastest.
Arguments:
- state_field: float32 [32, 32, 2304], P('gx', 'gy'), may hold values from -6 to 6
- conv_first: float32 [3, 3, 36, 108], replicated, may hold values from -0.1875 to 0.1875
- conv_second: float32 [3, 3, 36, 108], replicated, may hold values from -0.1875 to 0.1875
- spec_real: float32 [32, 32, 36, 432], P('gx', 'gy'), may hold values from -12 to 12
- spec_imag: float32 [32, 32, 36, 432], P('gx', 'gy'), may hold values from -12 to 12
Outputs:
- layer_out: float32 [32, 32, 2304], P('gx', 'gy')
All inputs are finite; a program needn't handle non-finite values.
Results may differ from a plain program's by a relative error of at most 0.00007.
Values sent between devices are 32-bit elements; how exact they have to be, the bound alone decides.
No kernel may reach another device: no remote copies, remote signals or barrier semaphores. Data moves between devices by JAX's collectives and lax.ppermute only.
A program may use at most 128 MiB of HBM per device.

v0:
```python
import jax
import jax.numpy as jnp
from jax import lax
from jax.sharding import PartitionSpec as P

C = 36
Z = 64
MX = 16
MY = 16
MZ = 12


highest = lax.Precision.HIGHEST
two_pi = 6.283185307179586


def with_halo(cells, sides, width):
    for axis, dim in sides:
        count = lax.axis_size(axis)
        ends = count - 1
        head = lax.slice_in_dim(cells, 0, width, axis=dim)
        tail = lax.slice_in_dim(cells, cells.shape[dim] - width, cells.shape[dim], axis=dim)
        cells = jnp.concatenate(
            [
                lax.ppermute(tail, axis, [(i, (i + 1) % count) for i in range(ends)]),
                cells,
                lax.ppermute(head, axis, [((i + 1) % count, i) for i in range(ends)]),
            ],
            axis=dim,
        )
    return cells


def matmul(left, right):
    return jnp.dot(left, right, precision=highest)


def kept_modes(mode_count, length):
    places = jnp.arange(2 * mode_count, dtype=jnp.int32)
    return jnp.where(places < mode_count, places, places + length - 2 * mode_count)


def angle_table(first_index, second_index, length):
    product = first_index[:, None] * second_index[None, :] % length
    angles = product.astype(jnp.float32) * (two_pi / length)
    return (jnp.cos(angles), jnp.sin(angles))


def convolve(extended, kernel, rows_out, cols_out):
    shaped = extended.reshape(rows_out + 2, cols_out + 2, C, Z)
    moved = jnp.transpose(shaped, (2, 0, 1, 3))
    padded = jnp.pad(moved, ((0, 0), (0, 0), (0, 0), (1, 1)))
    summed = jnp.zeros((C, rows_out * cols_out * Z), jnp.float32)
    for shift_x in range(3):
        for shift_y in range(3):
            for shift_z in range(3):
                window = padded[
                    :,
                    shift_x : shift_x + rows_out,
                    shift_y : shift_y + cols_out,
                    shift_z : shift_z + Z,
                ]
                block = kernel[shift_x, shift_y, :, shift_z * C : (shift_z + 1) * C]
                summed = summed + matmul(block, window.reshape(C, rows_out * cols_out * Z))
    return jnp.transpose(summed.reshape(C, rows_out, cols_out, Z), (1, 2, 0, 3))


def on_device(state_field, conv_first, conv_second, spec_real, spec_imag):
    rows_here = state_field.shape[0]
    cols_here = state_field.shape[1]
    total_x = rows_here * lax.axis_size("gx")
    total_y = cols_here * lax.axis_size("gy")
    row_start = lax.axis_index("gx") * rows_here
    col_start = lax.axis_index("gy") * cols_here
    chan_modes = C * MZ
    width_q = cols_here * chan_modes
    extended = with_halo(state_field, (("gx", 0), ("gy", 1)), 1)
    hidden_field = jax.nn.gelu(
        convolve(extended, conv_first, rows_here, cols_here), approximate=False
    )
    hidden_rim = with_halo(
        hidden_field.reshape(rows_here, cols_here, C * Z), (("gx", 0), ("gy", 1)), 1
    )
    conv_out = convolve(hidden_rim, conv_second, rows_here, cols_here)
    z_cells = jnp.arange(Z, dtype=jnp.int32)
    z_freqs = jnp.arange(MZ, dtype=jnp.int32)
    z_cosine, z_sine = angle_table(z_cells, z_freqs, Z)
    flat_cells = state_field.reshape(rows_here * cols_here * C, Z)
    z_real = matmul(flat_cells, z_cosine).reshape(rows_here, width_q)
    z_imag = -matmul(flat_cells, z_sine).reshape(rows_here, width_q)
    x_freqs = kept_modes(MX, total_x)
    local_x = row_start + jnp.arange(rows_here, dtype=jnp.int32)
    frequency = x_freqs
    cosine, sine_part = angle_table(frequency, local_x, total_x)
    term_real = matmul(cosine, z_real) + matmul(sine_part, z_imag)
    term_imag = matmul(cosine, z_imag) - matmul(sine_part, z_real)
    joined = lax.psum_scatter(
        jnp.concatenate([term_real, term_imag], axis=1), "gx", scatter_dimension=0, tiled=True
    )
    mode_real = joined[:, :width_q]
    mode_imag = joined[:, width_q:]
    kxd_rows = mode_real.shape[0]
    y_real = mode_real.reshape(kxd_rows, cols_here, chan_modes)
    y_imag = mode_imag.reshape(kxd_rows, cols_here, chan_modes)
    y_freqs = kept_modes(MY, total_y)
    local_y = col_start + jnp.arange(cols_here, dtype=jnp.int32)
    frequency = y_freqs
    cosine, sine_part = angle_table(frequency, local_y, total_y)
    term_real = jnp.einsum("my,ayq->maq", cosine, y_real, precision=highest) + jnp.einsum(
        "my,ayq->maq", sine_part, y_imag, precision=highest
    )
    term_imag = jnp.einsum("my,ayq->maq", cosine, y_imag, precision=highest) - jnp.einsum(
        "my,ayq->maq", sine_part, y_real, precision=highest
    )
    owned = lax.psum_scatter(
        jnp.concatenate([term_real, term_imag], axis=2), "gy", scatter_dimension=0, tiled=True
    )
    kyd_rows = owned.shape[0]
    owned_real = owned[..., :chan_modes].reshape(kyd_rows, kxd_rows, C, MZ)
    owned_imag = owned[..., chan_modes:].reshape(kyd_rows, kxd_rows, C, MZ)
    weight_real = spec_real.reshape(kxd_rows, kyd_rows, C, MZ, C)
    weight_imag = spec_imag.reshape(kxd_rows, kyd_rows, C, MZ, C)
    mixed_real = jnp.einsum(
        "baik,abiko->baok", owned_real, weight_real, precision=highest
    ) - jnp.einsum("baik,abiko->baok", owned_imag, weight_imag, precision=highest)
    mixed_imag = jnp.einsum(
        "baik,abiko->baok", owned_real, weight_imag, precision=highest
    ) + jnp.einsum("baik,abiko->baok", owned_imag, weight_real, precision=highest)
    mixed = jnp.concatenate(
        [
            mixed_real.reshape(kyd_rows, kxd_rows, chan_modes),
            mixed_imag.reshape(kyd_rows, kxd_rows, chan_modes),
        ],
        axis=2,
    )
    shard_piece = lax.all_gather(mixed, "gy", axis=0, tiled=True)
    frequency = y_freqs
    cosine, sine_part = angle_table(local_y, frequency, total_y)
    piece_real = shard_piece[..., :chan_modes]
    piece_imag = shard_piece[..., chan_modes:]
    add_real = jnp.einsum("ym,maq->ayq", cosine, piece_real, precision=highest) - jnp.einsum(
        "ym,maq->ayq", sine_part, piece_imag, precision=highest
    )
    add_imag = jnp.einsum("ym,maq->ayq", cosine, piece_imag, precision=highest) + jnp.einsum(
        "ym,maq->ayq", sine_part, piece_real, precision=highest
    )
    returned = jnp.concatenate([add_real, add_imag], axis=2)
    back_real = returned[..., :chan_modes].reshape(kxd_rows, width_q)
    back_imag = returned[..., chan_modes:].reshape(kxd_rows, width_q)
    joined_back = jnp.concatenate([back_real, back_imag], axis=1)
    shard_piece = lax.all_gather(joined_back, "gx", axis=0, tiled=True)
    frequency = x_freqs
    cosine, sine_part = angle_table(local_x, frequency, total_x)
    piece_real = shard_piece[:, :width_q]
    piece_imag = shard_piece[:, width_q:]
    add_real = matmul(cosine, piece_real) - matmul(sine_part, piece_imag)
    add_imag = matmul(cosine, piece_imag) + matmul(sine_part, piece_real)
    gathered = jnp.concatenate([add_real, add_imag], axis=1)
    cell_real = gathered[:, :width_q]
    cell_imag = gathered[:, width_q:]
    scaling = 1.0 / (total_x * total_y * Z)
    factors = jnp.where(z_freqs == 0, 1.0, 2.0).astype(jnp.float32) * scaling
    back_cosine, back_sine = angle_table(z_freqs, z_cells, Z)
    back_cosine = back_cosine * factors[:, None]
    back_sine = back_sine * factors[:, None]
    spectral = matmul(cell_real.reshape(rows_here * cols_here * C, MZ), back_cosine) - matmul(
        cell_imag.reshape(rows_here * cols_here * C, MZ), back_sine
    )
    spectral = spectral.reshape(rows_here, cols_here, C, Z)
    layer_out = jax.nn.gelu(spectral + conv_out, approximate=False)
    return layer_out.reshape(rows_here, cols_here, C * Z)


def solution(mesh):
    in_specs = (P("gx", "gy", None), P(), P(), P("gx", "gy", None, None), P("gx", "gy", None, None))
    out_specs = P("gx", "gy", None)
    return jax.shard_map(
        on_device, mesh=mesh, in_specs=in_specs, out_specs=out_specs, check_vma=False
    )
```

profile of v0, /device:TPU:0, one launch (start us, length us, event | category | flops | bytes accessed | tf_op | source)
XLA Modules:
  0.0 326.7 jit_solution(6536752744020171497)
XLA Ops:
  7.5 2.4 collective-permute-start
  18.9 4.9 %collective-permute-start.2 = (f32[6,1,2304]{2,1,0:T(1,128)S(1)}, f32[6,1,2304]{2,1,0:T(1,128)S(1)}, u32[]{:S(2)}, u32[]{:S(2)}) collective-permute-start(f32[6,1,2304]{2,1,0:T(1,128)S(1)} %get-tuple-element.71), channel_id=1, source_target_pairs={{0,1},{1,2},{2,3},{4,5},{5,6},{6,7},{8,9},{9,10},{10,11},{12,13},{... | collective-permute-start | bytes 165896 | tf_op jit(solution)/shard_map/ppermute | solution.py:25
  26.6 3.5 %fusion.337 = (f32[36,4,8,64]{3,0,1,2:T(8,128)S(1)}, f32[36,4,8,64]{3,0,1,2:T(8,128)S(1)}, f32[36,4,8,64]{3,0,1,2:T(8,128)S(1)}, f32[36,4,8,64]{3,0,1,2:T(8,128)...) fusion(f32[36,6,10,64]{3,0,1,2:T(8,128)S(1)} %bitcast.554), kind=kLoop, calls=%fused_computation.473 | loop fusion | bytes 6438912 | tf_op jit(solution)/shard_map/slice | solution.py:57
  30.0 4.4 %pad_slice_fusion.24 = (f32[36,4,8,64]{3,0,1,2:T(8,128)}, f32[36,4,8,64]{3,0,1,2:T(8,128)}, f32[36,4,8,64]{3,0,1,2:T(8,128)}, f32[36,4,8,64]{3,0,1,2:T(8,128)}, ...) fusion(f32[36,6,10,64]{3,0,1,2:T(8,128)S(1)} %bitcast.555), kind=kLoop, calls=%fused_computation.459 | loop fusion | bytes 4833280 | tf_op jit(solution)/shard_map/slice | solution.py:57
  34.4 2.1 fusion.338
  38.8 2.2 convolution_bitcast_fusion.10
  46.9 2.2 convolution_bitcast_fusion.13
  50.4 2.2 convolution_bitcast_fusion.14
  57.2 2.2 convolution_bitcast_fusion.16
  60.7 2.2 convolution_bitcast_fusion.17
  118.5 3.8 %collective-permute-start.4 = (f32[1,8,2304]{2,1,0:T(8,128)}, f32[1,8,2304]{2,1,0:T(8,128)S(1)}, u32[]{:S(2)}, u32[]{:S(2)}) collective-permute-start(f32[1,8,2304]{2,1,0:T(8,128)} %slice.463), channel_id=1, source_target_pairs={{0,4},{4,8},{8,12},{12,16},{16,20},{20,24},{24,28},{1,5},{5,9},{9,... | collective-permute-start | bytes 221192 | tf_op jit(solution)/shard_map/ppermute | solution.py:25
  124.0 4.1 %collective-permute-done.5 = f32[1,8,2304]{2,1,0:T(8,128)S(1)} collective-permute-done((f32[1,8,2304]{2,1,0:T(8,128)S(1)}, f32[1,8,2304]{2,1,0:T(8,128)S(1)}, u32[]{:S(2)}, u32[]{:S(2)}) %collective-permute-start.5) | collective-permute-done | bytes 73760 | tf_op jit(solution)/shard_map/ppermute | solution.py:27
  129.5 5.0 %collective-permute-start.6 = (f32[6,1,2304]{2,1,0:T(1,128)S(1)}, f32[6,1,2304]{2,1,0:T(1,128)S(1)}, u32[]{:S(2)}, u32[]{:S(2)}) collective-permute-start(f32[6,1,2304]{2,1,0:T(1,128)S(1)} %get-tuple-element.69), channel_id=1, source_target_pairs={{0,1},{1,2},{2,3},{4,5},{5,6},{6,7},{8,9},{9,10},{10,11},{12,13},{... | collective-permute-start | bytes 165896 | tf_op jit(solution)/shard_map/ppermute | solution.py:25
  134.5 6.6 %reshape.275 = f32[4,8,36,12,36]{4,3,1,2,0:T(8,128)} reshape(f32[4,8,36,432]{3,1,2,0:T(8,128)S(1)} %copy-done.40) | data formatting | bytes 3981312 | tf_op jit(solution)/shard_map/reshape | solution.py:121
  141.1 8.1 %reshape.277 = f32[4,8,36,12,36]{4,3,1,2,0:T(8,128)} reshape(f32[4,8,36,432]{3,1,2,0:T(8,128)} %param.9) | data formatting | bytes 3981312 | tf_op jit(solution)/shard_map/reshape | solution.py:122
  151.4 3.8 %fusion.335 = (f32[36,4,8,64]{3,0,1,2:T(8,128)S(1)}, f32[36,4,8,64]{3,0,1,2:T(8,128)}, f32[36,4,8,64]{3,0,1,2:T(8,128)S(1)}, f32[36,4,8,64]{3,0,1,2:T(8,128)}, f...) fusion(f32[36,6,10,64]{3,0,1,2:T(8,128)S(1)} %bitcast.557), kind=kLoop, calls=%fused_computation.471 | loop fusion | bytes 6438912 | tf_op jit(solution)/shard_map/slice | solution.py:57
  155.2 4.1 %pad_slice_fusion.6 = (f32[36,4,8,64]{3,0,1,2:T(8,128)S(1)}, f32[36,4,8,64]{3,0,1,2:T(8,128)}, f32[36,4,8,64]{3,0,1,2:T(8,128)}, f32[36,4,8,64]{3,0,1,2:T(8,128)...) fusion(f32[36,6,10,64]{3,0,1,2:T(8,128)S(1)} %bitcast.558), kind=kLoop, calls=%fused_computation.441 | loop fusion | bytes 4833280 | tf_op jit(solution)/shard_map/slice | solution.py:57
  159.3 2.1 fusion.336
  164.0 2.2 convolution_bitcast_fusion
  166.2 2.2 convolution_bitcast_fusion.1
  254.8 16.6 %reduce-scatter.2.cloned.1.call-done = f32[8,4,864]{2,0,1:T(8,128)} async-done(((f32[32,4,864]{2,0,1:T(8,128)}), f32[8,4,864]{2,0,1:T(8,128)}) %reduce-scatter.2.cloned.1.call-update) | async-done | bytes 110608 | tf_op jit(solution)/shard_map/reduce_scatter | solution.py:115
  273.2 9.2 %multiply_reduce_fusion.3 = (f32[8,4,12,36]{3,2,0,1:T(8,128)S(1)}, f32[8,4,12,36]{3,2,0,1:T(8,128)S(1)}, f32[8,4,12,36]{3,2,0,1:T(8,128)S(1)}, f32[8,4,12,36]{3,2,0,1:T(8,128)S(1)}) fusion(f32[4,8,36,12,36]{4,3,1,2,0:T(8,128)} %reshape.275, f32[8,4,12,36]{2,0,3,1:T(8,128)S(1)} %copy.166, f32[8,4,12,36]{2,0,3,1:T(8,128)S(1)} %copy.167, ...), kind=kLoop, calls=%fused_computation.3 | loop fusion | flops 3926016 | bytes 4313088
  284.4 14.8 %all_gather.6 = f32[32,4,864]{2,0,1:T(8,128)S(1)} all-gather(f32[8,4,864]{2,0,1:T(8,128)S(1)} %pad_maximum_fusion.4), channel_id=1, replica_groups=mesh['gx'=8,'gy'=4] {'gy'}, dimensions={0}, use_global_device_ids=true | all-gather | bytes 552960 | tf_op jit(solution)/shard_map/all_gather | solution.py:136
  300.9 11.0 %all-gather = f32[8,4,6912]{2,1,0:T(4,128)S(1)} all-gather(f32[1,4,6912]{2,1,0:T(4,128)S(1)} %maximum_bitcast_fusion), channel_id=1, replica_groups=mesh['gx'=8,'gy'=4] {'gx'}, dimensions={0}, use_global_device_ids=true | all-gather | bytes 995328 | tf_op jit(solution)/shard_map/all_gather | solution.py:151
  (434 shorter events, 189.1 us)
Async XLA Ops:
  6.5 235.4 %all-reduce.5.cloned.1.call-start = ((), (), s32[]{:S(2)}) async-start(), calls=%async_computation.2 | async-start | bytes 1769472
  7.5 10.0 %collective-permute-start = (f32[1,8,2304]{2,1,0:T(8,128)S(1)}, f32[1,8,2304]{2,1,0:T(8,128)S(1)}, u32[]{:S(2)}, u32[]{:S(2)}) collective-permute-start(f32[1,8,2304]{2,1,0:T(8,128)S(1)} %get-tuple-element.76), channel_id=1, source_target_pairs={{0,4},{4,8},{8,12},{12,16},{16,20},{20,24},{24,28},{1,5},{5,9},{9,... | collective-permute-start | bytes 221192 | tf_op jit(solution)/shard_map/ppermute | solution.py:25
  9.9 7.6 %collective-permute-start.1 = (f32[1,8,2304]{2,1,0:T(8,128)S(1)}, f32[1,8,2304]{2,1,0:T(8,128)S(1)}, u32[]{:S(2)}, u32[]{:S(2)}) collective-permute-start(f32[1,8,2304]{2,1,0:T(8,128)S(1)} %get-tuple-element.75), channel_id=1, source_target_pairs={{4,0},{8,4},{12,8},{16,12},{20,16},{24,20},{28,24},{5,1},{9,5},{13... | collective-permute-start | bytes 221192 | tf_op jit(solution)/shard_map/ppermute | solution.py:27
  17.6 7.5 %collective-permute-start.3 = (f32[6,1,2304]{2,1,0:T(1,128)S(1)}, f32[6,1,2304]{2,1,0:T(1,128)S(1)}, u32[]{:S(2)}, u32[]{:S(2)}) collective-permute-start(f32[6,1,2304]{2,1,0:T(1,128)S(1)} %get-tuple-element.72), channel_id=1, source_target_pairs={{1,0},{2,1},{3,2},{5,4},{6,5},{7,6},{9,8},{10,9},{11,10},{13,12},{... | collective-permute-start | bytes 165896 | tf_op jit(solution)/shard_map/ppermute | solution.py:27
  18.9 6.7 %collective-permute-start.2 = (f32[6,1,2304]{2,1,0:T(1,128)S(1)}, f32[6,1,2304]{2,1,0:T(1,128)S(1)}, u32[]{:S(2)}, u32[]{:S(2)}) collective-permute-start(f32[6,1,2304]{2,1,0:T(1,128)S(1)} %get-tuple-element.71), channel_id=1, source_target_pairs={{0,1},{1,2},{2,3},{4,5},{5,6},{6,7},{8,9},{9,10},{10,11},{12,13},{... | collective-permute-start | bytes 165896 | tf_op jit(solution)/shard_map/ppermute | solution.py:25
  24.9 246.6 %reduce-scatter.2.cloned.1.call-start = ((), (), s32[]{:S(2)}) async-start(), calls=%async_computation.1 | async-start | bytes 573440 | tf_op jit(solution)/shard_map/reduce_scatter | solution.py:115
  38.8 3.4 %copy-start.36 = (f32[36,4,8,64]{3,0,1,2:T(8,128)S(1)}, f32[36,4,8,64]{3,0,1,2:T(8,128)}, u32[]{:S(2)}) copy-start(f32[36,4,8,64]{3,0,1,2:T(8,128)} %get-tuple-element.55) | copy-start | bytes 884740
  62.9 4.6 %copy-start.27 = (f32[36,4,8,64]{3,0,1,2:T(8,128)S(1)}, f32[36,4,8,64]{3,0,1,2:T(8,128)}, u32[]{:S(2)}) copy-start(f32[36,4,8,64]{3,0,1,2:T(8,128)} %get-tuple-element.64) | copy-start | bytes 884740
  67.4 3.6 %copy-start.23 = (f32[36,4,8,64]{3,0,1,2:T(8,128)S(1)}, f32[36,4,8,64]{3,0,1,2:T(8,128)}, u32[]{:S(2)}) copy-start(f32[36,4,8,64]{3,0,1,2:T(8,128)} %get-tuple-element.63) | copy-start | bytes 884740
  117.8 16.7 %copy-start.40 = (f32[4,8,36,432]{3,1,2,0:T(8,128)S(1)}, f32[4,8,36,432]{3,1,2,0:T(8,128)}, u32[]{:S(2)}) copy-start(f32[4,8,36,432]{3,1,2,0:T(8,128)} %param.8) | copy-start | bytes 5971972
  118.5 5.4 %collective-permute-start.4 = (f32[1,8,2304]{2,1,0:T(8,128)}, f32[1,8,2304]{2,1,0:T(8,128)S(1)}, u32[]{:S(2)}, u32[]{:S(2)}) collective-permute-start(f32[1,8,2304]{2,1,0:T(8,128)} %slice.463), channel_id=1, source_target_pairs={{0,4},{4,8},{8,12},{12,16},{16,20},{20,24},{24,28},{1,5},{5,9},{9,... | collective-permute-start | bytes 221192 | tf_op jit(solution)/shard_map/ppermute | solution.py:25
  122.7 5.5 %collective-permute-start.5 = (f32[1,8,2304]{2,1,0:T(8,128)S(1)}, f32[1,8,2304]{2,1,0:T(8,128)S(1)}, u32[]{:S(2)}, u32[]{:S(2)}) collective-permute-start(f32[1,8,2304]{2,1,0:T(8,128)S(1)} %slice.465), channel_id=1, source_target_pairs={{4,0},{8,4},{12,8},{16,12},{20,16},{24,20},{28,24},{5,1},{9,5},{13... | collective-permute-start | bytes 221192 | tf_op jit(solution)/shard_map/ppermute | solution.py:27
  128.2 22.3 %collective-permute-start.7 = (f32[6,1,2304]{2,1,0:T(1,128)S(1)}, f32[6,1,2304]{2,1,0:T(1,128)S(1)}, u32[]{:S(2)}, u32[]{:S(2)}) collective-permute-start(f32[6,1,2304]{2,1,0:T(1,128)S(1)} %get-tuple-element.70), channel_id=1, source_target_pairs={{1,0},{2,1},{3,2},{5,4},{6,5},{7,6},{9,8},{10,9},{11,10},{13,12},{... | collective-permute-start | bytes 165896 | tf_op jit(solution)/shard_map/ppermute | solution.py:27
  129.5 21.0 %collective-permute-start.6 = (f32[6,1,2304]{2,1,0:T(1,128)S(1)}, f32[6,1,2304]{2,1,0:T(1,128)S(1)}, u32[]{:S(2)}, u32[]{:S(2)}) collective-permute-start(f32[6,1,2304]{2,1,0:T(1,128)S(1)} %get-tuple-element.69), channel_id=1, source_target_pairs={{0,1},{1,2},{2,3},{4,5},{5,6},{6,7},{8,9},{9,10},{10,11},{12,13},{... | collective-permute-start | bytes 165896 | tf_op jit(solution)/shard_map/ppermute | solution.py:25
  141.1 8.1 %copy-start.90 = (u32[32]{0:T(128)S(1)}, u32[32]{0:T(128)}, u32[]{:S(2)}) copy-start(u32[32]{0:T(128)} %constant.167) | copy-start | bytes 388
  163.1 5.3 %copy-start.37 = (f32[36,4,8,64]{3,0,1,2:T(8,128)S(1)}, f32[36,4,8,64]{3,0,1,2:T(8,128)}, u32[]{:S(2)}) copy-start(f32[36,4,8,64]{3,0,1,2:T(8,128)} %get-tuple-element.28) | copy-start | bytes 884740
  168.4 3.6 %copy-start.35 = (f32[36,4,8,64]{3,0,1,2:T(8,128)S(1)}, f32[36,4,8,64]{3,0,1,2:T(8,128)}, u32[]{:S(2)}) copy-start(f32[36,4,8,64]{3,0,1,2:T(8,128)} %get-tuple-element.27) | copy-start | bytes 884740
  172.0 3.6 %copy-start.33 = (f32[36,4,8,64]{3,0,1,2:T(8,128)S(1)}, f32[36,4,8,64]{3,0,1,2:T(8,128)}, u32[]{:S(2)}) copy-start(f32[36,4,8,64]{3,0,1,2:T(8,128)} %get-tuple-element.30) | copy-start | bytes 884740
  175.6 3.7 %copy-start.31 = (f32[36,4,8,64]{3,0,1,2:T(8,128)S(1)}, f32[36,4,8,64]{3,0,1,2:T(8,128)}, u32[]{:S(2)}) copy-start(f32[36,4,8,64]{3,0,1,2:T(8,128)} %get-tuple-element.26) | copy-start | bytes 884740
  179.3 3.6 %copy-start.28 = (f32[36,4,8,64]{3,0,1,2:T(8,128)S(1)}, f32[36,4,8,64]{3,0,1,2:T(8,128)}, u32[]{:S(2)}) copy-start(f32[36,4,8,64]{3,0,1,2:T(8,128)} %get-tuple-element.25) | copy-start | bytes 884740
  182.9 3.7 %copy-start.24 = (f32[36,4,8,64]{3,0,1,2:T(8,128)S(1)}, f32[36,4,8,64]{3,0,1,2:T(8,128)}, u32[]{:S(2)}) copy-start(f32[36,4,8,64]{3,0,1,2:T(8,128)} %get-tuple-element.31) | copy-start | bytes 884740
  192.9 3.8 %copy-start.25 = (f32[36,4,8,64]{3,0,1,2:T(8,128)S(1)}, f32[36,4,8,64]{3,0,1,2:T(8,128)}, u32[]{:S(2)}) copy-start(f32[36,4,8,64]{3,0,1,2:T(8,128)} %get-tuple-element.36) | copy-start | bytes 884740
  213.7 3.3 copy-start.10
  249.6 3.3 copy-start.50
  (77 other events, 153.3 us)
Sparse Core Ops, SparseCore 0:
  25.0 59.2 all-reduce.4
  246.4 25.0 reduce-scatter.1
where the time goes:
time: 333 us; the launch traced here: 327 us
  local copies, waits for them, and re-layouts  162 us (49%)
  matrix products  65.8 us (20%)
  blocking collectives  25.8 us (8%)
  starting transfers between devices  21.5 us (6%)
  waiting for transfers between devices  21.3 us (6%)
  between operations  15.8 us (5%)
  other arithmetic  14.9 us (4%)
    reshape x54, local copies, waits for them, and re-layouts, convolve(): summed = summed + matmul(block, window.reshape(C, rows_out * cols_out * Z))  64.9 us
    slice x60, local copies, waits for them, and re-layouts, convolve(): padded[:, shift_x:shift_x + rows_out, shift_y:shift_y + cols_out, shift_z...  64.8 us
    dot_general x66, matrix products, matmul(): return jnp.dot(left, right, precision=highest)  62.4 us
    reduce_scatter x1, waiting for transfers between devices, on_device(): lax.psum_scatter(jnp.concatenate([term_real, term_imag], axis=2), 'gy', s...  16.6 us
    ppermute x4, starting transfers between devices, with_halo(): lax.ppermute(tail, axis, [(i, (i + 1) % count) for i in range(ends)])  16.1 us
    all_gather x1, blocking collectives, on_device(): shard_piece = lax.all_gather(mixed, 'gy', axis=0, tiled=True)  14.8 us
    all_gather x1, blocking collectives, on_device(): shard_piece = lax.all_gather(joined_back, 'gx', axis=0, tiled=True)  11 us
    unnamed x2, other arithmetic  9.24 us
  transfers between devices with their start and end apart: 10, of which 3 were waited for; matrix products, arithmetic and copies ran while one was open for 65% of the time, Pallas kernels for 0%

commit v1 on v0

--- a/solution.py
+++ b/solution.py
@@ -1,6 +1,8 @@
 import jax
 import jax.numpy as jnp
 from jax import lax
+from jax.experimental import pallas as pl
+from jax.experimental.pallas import tpu as pltpu
 from jax.sharding import PartitionSpec as P
 
 C = 36
@@ -10,6 +12,7 @@
 MZ = 12
 
 
+BF = jnp.bfloat16
 highest = lax.Precision.HIGHEST
 two_pi = 6.283185307179586
 
@@ -46,23 +49,84 @@
     return (jnp.cos(angles), jnp.sin(angles))
 
 
-def convolve(extended, kernel, rows_out, cols_out):
-    shaped = extended.reshape(rows_out + 2, cols_out + 2, C, Z)
-    moved = jnp.transpose(shaped, (2, 0, 1, 3))
-    padded = jnp.pad(moved, ((0, 0), (0, 0), (0, 0), (1, 1)))
-    summed = jnp.zeros((C, rows_out * cols_out * Z), jnp.float32)
-    for shift_x in range(3):
-        for shift_y in range(3):
-            for shift_z in range(3):
-                window = padded[
-                    :,
-                    shift_x : shift_x + rows_out,
-                    shift_y : shift_y + cols_out,
-                    shift_z : shift_z + Z,
-                ]
-                block = kernel[shift_x, shift_y, :, shift_z * C : (shift_z + 1) * C]
-                summed = summed + matmul(block, window.reshape(C, rows_out * cols_out * Z))
-    return jnp.transpose(summed.reshape(C, rows_out, cols_out, Z), (1, 2, 0, 3))
+def gelu(x):
+    return 0.5*x*(1.0+lax.erf(x*0.7071067811865476))
+
+def split(x):
+    hi=x.astype(BF)
+    return hi,(x-hi.astype(jnp.float32)).astype(BF)
+
+def conv_body(ext_ref, w1_ref, w2_ref, mask_ref, out_ref, t_ref, d_ref, w_ref, wh_ref, wl_ref):
+    f32=jnp.float32
+    zb=4
+    m=zb*C
+    top=40
+    rows=Z*C
+    d_ref[0:top,:]=jnp.zeros((top,128),f32)
+    d_ref[top+rows:,:]=jnp.zeros((d_ref.shape[0]-top-rows,128),f32)
+    for j in range(C//2):
+        x=ext_ref[:,:,j*128:(j+1)*128].reshape(128,128)
+        t_ref[j*128:(j+1)*128,:]=x.T
+    for z in range(Z):
+        d_ref[top+z*C:top+(z+1)*C,:]=t_ref[pl.ds(z,C,stride=Z),:]
+    kk=224
+    def load_w(wr):
+        w_ref[...]=jnp.zeros_like(w_ref)
+        for s in range(9):
+            w=wr[s//3,s%3]
+            for zo in range(zb):
+                w_ref[s*m+zo*C:s*m+(zo+1)*C, 4+C*zo:4+C*zo+3*C]=w
+        h,l=split(w_ref[...])
+        wh_ref[...]=h
+        wl_ref[...]=l
+    def conv(store):
+        def step(g,_):
+            r0=pl.multiple_of(g*2*m,8)
+            a=d_ref[pl.ds(r0,kk),:]
+            b=d_ref[pl.ds(pl.multiple_of(r0+m,8),kk),:]
+            x=jnp.concatenate([a,b],axis=1)
+            xh,xl=split(x)
+            acc=None
+            for s in range(9):
+                wh=wh_ref[s*m:(s+1)*m,:]
+                wl=wl_ref[s*m:(s+1)*m,:]
+                p=jnp.dot(wh,xh,preferred_element_type=f32)+(jnp.dot(wl,xh,preferred_element_type=f32)+jnp.dot(wh,xl,preferred_element_type=f32))
+                off=(s//3)*16+s%3
+                if off:
+                    p=[pltpu.roll(p[:,h*128:(h+1)*128],128-off,1) for h in range(2)]
+                else:
+                    p=[p[:,h*128:(h+1)*128] for h in range(2)]
+                acc=p if acc is None else [u+v for u,v in zip(acc,p)]
+            store(r0,acc)
+            return 0
+        lax.fori_loop(0,Z//(2*zb),step,0)
+    load_w(w1_ref)
+    mask=mask_ref[0:1,:]
+    def store1(r0,acc):
+        for h in range(2):
+            t_ref[pl.ds(pl.multiple_of(r0+h*m,8),m),:]=gelu(acc[h])*mask
+    conv(store1)
+    d_ref[top:top+rows,:]=t_ref[...]
+    load_w(w2_ref)
+    def store2(r0,acc):
+        for h in range(2):
+            t_ref[pl.ds(pl.multiple_of(r0+h*m,8),m),:]=acc[h]
+    conv(store2)
+    for j in range(C//2):
+        x=jnp.concatenate([t_ref[pl.ds(2*j+e,Z,stride=C),:] for e in range(2)],axis=0)
+        y=x.T
+        for xx in range(4):
+            out_ref[xx,:,j*128:(j+1)*128]=y[16*xx:16*xx+8,:]
+
+def conv_call(ext,w1,w2,mask):
+    return pl.pallas_call(conv_body,
+        out_shape=jax.ShapeDtypeStruct((4,8,C*Z),jnp.float32),
+        in_specs=[pl.BlockSpec(memory_space=pltpu.VMEM)]*4,
+        out_specs=pl.BlockSpec(memory_space=pltpu.VMEM),
+        scratch_shapes=[pltpu.VMEM((Z*C,128),jnp.float32),pltpu.VMEM((Z*C+80,128),jnp.float32),
+            pltpu.VMEM((1296,224),jnp.float32),pltpu.VMEM((1296,224),BF),pltpu.VMEM((1296,224),BF)],
+        name="conv_pair",
+    )(ext,w1,w2,mask)
 
 
 def on_device(state_field, conv_first, conv_second, spec_real, spec_imag):
@@ -74,14 +138,14 @@
     col_start = lax.axis_index("gy") * cols_here
     chan_modes = C * MZ
     width_q = cols_here * chan_modes
-    extended = with_halo(state_field, (("gx", 0), ("gy", 1)), 1)
-    hidden_field = jax.nn.gelu(
-        convolve(extended, conv_first, rows_here, cols_here), approximate=False
-    )
-    hidden_rim = with_halo(
-        hidden_field.reshape(rows_here, cols_here, C * Z), (("gx", 0), ("gy", 1)), 1
-    )
-    conv_out = convolve(hidden_rim, conv_second, rows_here, cols_here)
+    extended = with_halo(state_field, (("gx", 0), ("gy", 1)), 2)
+    extended = jnp.pad(extended, ((0, 0), (0, 4), (0, 0)))
+    lanes = jnp.arange(128, dtype=jnp.int32)[None, :]
+    cell_x = row_start - 1 + lanes // 16
+    cell_y = col_start - 1 + lanes % 16
+    inside = (cell_x >= 0) & (cell_x < total_x) & (cell_y >= 0) & (cell_y < total_y)
+    mask = jnp.broadcast_to(inside.astype(jnp.float32), (8, 128))
+    conv_out = conv_call(extended, conv_first, conv_second, mask).reshape(rows_here, cols_here, C, Z)
     z_cells = jnp.arange(Z, dtype=jnp.int32)
     z_freqs = jnp.arange(MZ, dtype=jnp.int32)
     z_cosine, z_sine = angle_table(z_cells, z_freqs, Z)

time: 333 us -> 174 us (0.52); the launches traced: 327 us -> 174 us
  local copies, waits for them, and re-layouts: 162 us -> 26.2 us
  matrix products: 65.8 us -> 10.8 us
  waiting for transfers between devices: 21.3 us -> 56.2 us
  Pallas kernels: 0 us -> 16.7 us
  starting transfers between devices: 21.5 us -> 8.53 us
    reshape x59 -> x0, local copies, waits for them, and re-layouts: 67 us -> none  [the longest x54 64.9 us: convolve(): summed = summed + matmul(block, window.reshape(C, rows_out * cols_out * Z))]
    slice x60 -> x0, local copies, waits for them, and re-layouts: 64.8 us -> none  [convolve(): padded[:, shift_x:shift_x + rows_out, shift_y:shift_y + cols_out, shift_z...]
    dot_general x66 -> x12, matrix products: 62.4 us -> 7.27 us  [matmul(): return jnp.dot(left, right, precision=highest)]
    unnamed x3, waiting for transfers between devices: 0.03 us -> 53.4 us
    pallas_call x0 -> x1, Pallas kernels: none -> 16.7 us  [conv_call(): pl.pallas_call(conv_body, out_shape=jax.ShapeDtypeStruct((4, 8, C * Z), j...]
    reduce_scatter x1, waiting for transfers between devices: 16.6 us -> 0.01 us  [on_device(): lax.psum_scatter(jnp.concatenate([term_real, term_imag], axis=2), 'gy', s...]
    ppermute x4 -> x2, starting transfers between devices: 16.1 us -> 5.72 us  [with_halo(): lax.ppermute(tail, axis, [(i, (i + 1) % count) for i in range(ends)])]
  transfers between devices with their start and end apart: 10 -> 6, of which waited for: 3 -> 2; matrix products, arithmetic and copies ran while one was open for 65% -> 14% of each run, Pallas kernels for 0% -> 10%
where the time goes in v1:
time: 174 us
  waiting for transfers between devices  56.2 us (32%)
  blocking collectives  26.7 us (15%)
  local copies, waits for them, and re-layouts  26.2 us (15%)
  Pallas kernels  16.7 us (10%)
  between operations  14.5 us (8%)
  other arithmetic  14 us (8%)
  matrix products  10.8 us (6%)
  starting transfers between devices  8.53 us (5%)
    unnamed x3, waiting for transfers between devices  53.4 us
    pallas_call x1, Pallas kernels, conv_call(): pl.pallas_call(conv_body, out_shape=jax.ShapeDtypeStruct((4, 8, C * Z), j...  16.7 us
    all_gather x1, blocking collectives, on_device(): shard_piece = lax.all_gather(mixed, 'gy', axis=0, tiled=True)  15.9 us
    all_gather x1, blocking collectives, on_device(): shard_piece = lax.all_gather(joined_back, 'gx', axis=0, tiled=True)  10.7 us
    unnamed x2, other arithmetic  9.24 us
    reshape x1, local copies, waits for them, and re-layouts, on_device(): weight_imag = spec_imag.reshape(kxd_rows, kyd_rows, C, MZ, C)  8.04 us
    dot_general x12, matrix products, matmul(): return jnp.dot(left, right, precision=highest)  7.27 us
    reshape x1, local copies, waits for them, and re-layouts, on_device(): weight_real = spec_real.reshape(kxd_rows, kyd_rows, C, MZ, C)  6.56 us
  transfers between devices with their start and end apart: 6, of which 2 were waited for; matrix products, arithmetic and copies ran while one was open for 14% of the time, Pallas kernels for 10%

profile of v1, /device:TPU:0, one launch (start us, length us, event | category | flops | bytes accessed | tf_op | source)
XLA Modules:
  0.0 173.6 jit_solution(2250339118622589596)
XLA Ops:
  6.5 1.0 fusion.190
  7.5 2.4 %collective-permute-start = (f32[2,8,2304]{2,1,0:T(8,128)S(1)}, f32[2,8,2304]{2,1,0:T(8,128)S(1)}, u32[]{:S(2)}, u32[]{:S(2)}) collective-permute-start(f32[2,8,2304]{2,1,0:T(8,128)S(1)} %get-tuple-element.16), channel_id=1, source_target_pairs={{0,4},{4,8},{8,12},{12,16},{16,20},{20,24},{24,28},{1,5},{5,9},{9,... | collective-permute-start | bytes 442376 | tf_op jit(solution)/shard_map/ppermute | solution.py:28
  10.0 1.1 reshape.159
  11.1 0.8 convolution_bitcast_fusion
  11.9 0.8 fusion
  16.2 1.0 pad_maximum_fusion
  17.3 1.3 collective-permute-start.1
  19.9 2.7 %collective-permute-done.1 = f32[2,8,2304]{2,1,0:T(8,128)S(1)} collective-permute-done((f32[2,8,2304]{2,1,0:T(8,128)S(1)}, f32[2,8,2304]{2,1,0:T(8,128)S(1)}, u32[]{:S(2)}, u32[]{:S(2)}) %collective-permute-start.1) | collective-permute-done | bytes 147488 | tf_op jit(solution)/shard_map/ppermute | solution.py:30
  22.7 53.4 %all-reduce.4.cloned.1.call-done = f32[32,6912]{1,0:T(8,128)} async-done(((f32[32,6912]{1,0:T(8,128)}), f32[32,6912]{1,0:T(8,128)}) %all-reduce.4.cloned.1.call-update) | async-done | bytes 884752
  76.1 1.0 constant_dynamic-slice_fusion
  79.5 0.9 pad_maximum_fusion.1
  80.5 3.3 %collective-permute-start.2 = (f32[8,2,2304]{2,1,0:T(2,128)S(1)}, f32[8,2,2304]{2,1,0:T(2,128)S(1)}, u32[]{:S(2)}, u32[]{:S(2)}) collective-permute-start(f32[8,2,2304]{2,1,0:T(2,128)S(1)} %get-tuple-element.13), channel_id=1, source_target_pairs={{0,1},{1,2},{2,3},{4,5},{5,6},{6,7},{8,9},{9,10},{10,11},{12,13},{... | collective-permute-start | bytes 442376 | tf_op jit(solution)/shard_map/ppermute | solution.py:28
  83.9 1.5 collective-permute-start.3
  85.4 6.6 %reshape.164 = f32[4,8,36,12,36]{4,3,1,2,0:T(8,128)} reshape(f32[4,8,36,432]{3,1,2,0:T(8,128)S(1)} %copy-done.1) | data formatting | bytes 3981312 | tf_op jit(solution)/shard_map/reshape | solution.py:185
  91.9 8.0 %reshape.166 = f32[4,8,36,12,36]{4,3,1,2,0:T(8,128)} reshape(f32[4,8,36,432]{3,1,2,0:T(8,128)} %param.9) | data formatting | bytes 3981312 | tf_op jit(solution)/shard_map/reshape | solution.py:186
  100.0 1.3 select_maximum_fusion.ext_ref
  101.9 16.7 %conv_pair.1 = f32[4,8,2304]{2,1,0:T(8,128)} custom-call(f32[8,16,2304]{2,1,0:T(8,128)} %select_maximum_fusion.ext_ref, f32[3,3,36,108]{3,2,1,0:T(8,128)} %w1_ref.1, f32[3,3,36,108]{3,2,1,0:T(8,128)} %w2_ref.1, f32[8,128]{1,0:T(8,128)} %broadcast_in_dim.10.mask_ref), custom_call_target="tpu_custom_call" | custom-call | tf_op jit(solution)/shard_map/conv_pair/pallas_call | solution.py:122
  118.6 1.0 fusion.191
  120.3 9.2 %multiply_reduce_fusion.3 = (f32[8,4,12,36]{3,2,0,1:T(8,128)S(1)}, f32[8,4,12,36]{3,2,0,1:T(8,128)S(1)}, f32[8,4,12,36]{3,2,0,1:T(8,128)S(1)}, f32[8,4,12,36]{3,2,0,1:T(8,128)S(1)}) fusion(f32[4,8,36,12,36]{4,3,1,2,0:T(8,128)} %reshape.164, f32[8,4,12,36]{2,0,3,1:T(8,128)S(1)} %copy.45, f32[8,4,12,36]{2,0,3,1:T(8,128)S(1)} %copy.46, ...), kind=kLoop, calls=%fused_computation.3 | loop fusion | flops 3926016 | bytes 4313088
  131.6 15.9 %all_gather.6 = f32[32,4,864]{2,0,1:T(8,128)S(1)} all-gather(f32[8,4,864]{2,0,1:T(8,128)S(1)} %pad_maximum_fusion.2), channel_id=1, replica_groups=mesh['gx'=8,'gy'=4] {'gy'}, dimensions={0}, use_global_device_ids=true | all-gather | bytes 552960 | tf_op jit(solution)/shard_map/all_gather | solution.py:200
  149.2 10.7 %all-gather = f32[8,4,6912]{2,1,0:T(4,128)S(1)} all-gather(f32[1,4,6912]{2,1,0:T(4,128)S(1)} %maximum_bitcast_fusion), channel_id=1, replica_groups=mesh['gx'=8,'gy'=4] {'gx'}, dimensions={0}, use_global_device_ids=true | all-gather | bytes 995328 | tf_op jit(solution)/shard_map/all_gather | solution.py:215
  163.2 0.9 fusion.45
  164.1 0.9 convolution_subtract_fusion.2
  165.4 1.4 fusion.10
  (69 shorter events, 15.2 us)
Async XLA Ops:
  6.5 69.5 %all-reduce.4.cloned.1.call-start = ((), (), s32[]{:S(2)}) async-start(), calls=%async_computation.2 | async-start | bytes 1769472
  7.5 12.3 %collective-permute-start = (f32[2,8,2304]{2,1,0:T(8,128)S(1)}, f32[2,8,2304]{2,1,0:T(8,128)S(1)}, u32[]{:S(2)}, u32[]{:S(2)}) collective-permute-start(f32[2,8,2304]{2,1,0:T(8,128)S(1)} %get-tuple-element.16), channel_id=1, source_target_pairs={{0,4},{4,8},{8,12},{12,16},{16,20},{20,24},{24,28},{1,5},{5,9},{9,... | collective-permute-start | bytes 442376 | tf_op jit(solution)/shard_map/ppermute | solution.py:28
  15.0 3.6 %copy-start.3 = (u32[32]{0:T(128)S(1)}, u32[32]{0:T(128)}, u32[]{:S(2)}) copy-start(u32[32]{0:T(128)} %constant.199) | copy-start | bytes 388
  15.0 4.8 %copy-start = (f32[4,8,2304]{2,1,0:T(8,128)S(1)}, f32[4,8,2304]{2,1,0:T(8,128)}, u32[]{:S(2)}) copy-start(f32[4,8,2304]{2,1,0:T(8,128)} %param.5) | copy-start | bytes 884740
  17.2 101.4 %reduce-scatter.2.cloned.1.call-start = ((), (), s32[]{:S(2)}) async-start(), calls=%async_computation.1 | async-start | bytes 573440 | tf_op jit(solution)/shard_map/reduce_scatter | solution.py:179
  17.3 5.4 %collective-permute-start.1 = (f32[2,8,2304]{2,1,0:T(8,128)S(1)}, f32[2,8,2304]{2,1,0:T(8,128)S(1)}, u32[]{:S(2)}, u32[]{:S(2)}) collective-permute-start(f32[2,8,2304]{2,1,0:T(8,128)S(1)} %get-tuple-element.15), channel_id=1, source_target_pairs={{4,0},{8,4},{12,8},{16,12},{20,16},{24,20},{28,24},{5,1},{9,5},{13... | collective-permute-start | bytes 442376 | tf_op jit(solution)/shard_map/ppermute | solution.py:30
  19.9 65.4 %copy-start.1 = (f32[4,8,36,432]{3,1,2,0:T(8,128)S(1)}, f32[4,8,36,432]{3,1,2,0:T(8,128)}, u32[]{:S(2)}) copy-start(f32[4,8,36,432]{3,1,2,0:T(8,128)} %param.8) | copy-start | bytes 5971972
  80.5 19.4 %collective-permute-start.2 = (f32[8,2,2304]{2,1,0:T(2,128)S(1)}, f32[8,2,2304]{2,1,0:T(2,128)S(1)}, u32[]{:S(2)}, u32[]{:S(2)}) collective-permute-start(f32[8,2,2304]{2,1,0:T(2,128)S(1)} %get-tuple-element.13), channel_id=1, source_target_pairs={{0,1},{1,2},{2,3},{4,5},{5,6},{6,7},{8,9},{9,10},{10,11},{12,13},{... | collective-permute-start | bytes 442376 | tf_op jit(solution)/shard_map/ppermute | solution.py:28
  83.9 16.1 %collective-permute-start.3 = (f32[8,2,2304]{2,1,0:T(2,128)S(1)}, f32[8,2,2304]{2,1,0:T(2,128)S(1)}, u32[]{:S(2)}, u32[]{:S(2)}) collective-permute-start(f32[8,2,2304]{2,1,0:T(2,128)S(1)} %get-tuple-element.14), channel_id=1, source_target_pairs={{1,0},{2,1},{3,2},{5,4},{6,5},{7,6},{9,8},{10,9},{11,10},{13,12},{... | collective-permute-start | bytes 442376 | tf_op jit(solution)/shard_map/ppermute | solution.py:30
  162.6 2.9 %copy-start.2 = (f32[4,8,2304]{2,1,0:T(8,128)S(1)}, f32[4,8,2304]{2,1,0:T(8,128)}, u32[]{:S(2)}) copy-start(f32[4,8,2304]{2,1,0:T(8,128)} %conv_pair.1) | copy-start | bytes 884740
Sparse Core Ops, SparseCore 0:
  17.4 58.6 all-reduce.3
  80.6 21.9 reduce-scatter.1

commit v2 on v1

v2 whole, which is shorter than its diff:
```python
import numpy as np
import jax
import jax.numpy as jnp
from jax import lax
from jax.experimental import pallas as pl
from jax.experimental.pallas import tpu as pltpu
from jax.sharding import PartitionSpec as P

C = 36
Z = 64
MX = 16
MY = 16
MZ = 12
BF = jnp.bfloat16
highest = lax.Precision.HIGHEST


def with_halo(cells, sides, width):
    for axis, dim in sides:
        count = lax.axis_size(axis)
        ends = count - 1
        head = lax.slice_in_dim(cells, 0, width, axis=dim)
        tail = lax.slice_in_dim(cells, cells.shape[dim] - width, cells.shape[dim], axis=dim)
        cells = jnp.concatenate(
            [
                lax.ppermute(tail, axis, [(i, (i + 1) % count) for i in range(ends)]),
                cells,
                lax.ppermute(head, axis, [((i + 1) % count, i) for i in range(ends)]),
            ],
            axis=dim,
        )
    return cells


def gelu(x):
    return 0.5*x*(1.0+lax.erf(x*0.7071067811865476))

def split(x):
    hi=x.astype(BF)
    return hi,(x-hi.astype(jnp.float32)).astype(BF)

def conv_body(ext_ref, w1_ref, w2_ref, mask_ref, out_ref, t_ref, d_ref, w_ref, wh_ref, wl_ref):
    f32=jnp.float32
    zb=4
    m=zb*C
    top=40
    rows=Z*C
    d_ref[0:top,:]=jnp.zeros((top,128),f32)
    d_ref[top+rows:,:]=jnp.zeros((d_ref.shape[0]-top-rows,128),f32)
    for j in range(C//2):
        x=ext_ref[:,:,j*128:(j+1)*128].reshape(128,128)
        t_ref[j*128:(j+1)*128,:]=x.T
    for z in range(Z):
        d_ref[top+z*C:top+(z+1)*C,:]=t_ref[pl.ds(z,C,stride=Z),:]
    kk=224
    def load_w(wr):
        w_ref[...]=jnp.zeros_like(w_ref)
        for s in range(9):
            w=wr[s//3,s%3]
            for zo in range(zb):
                w_ref[s*m+zo*C:s*m+(zo+1)*C, 4+C*zo:4+C*zo+3*C]=w
        h,l=split(w_ref[...])
        wh_ref[...]=h
        wl_ref[...]=l
    def conv(store):
        def step(g,_):
            r0=pl.multiple_of(g*2*m,8)
            a=d_ref[pl.ds(r0,kk),:]
            b=d_ref[pl.ds(pl.multiple_of(r0+m,8),kk),:]
            x=jnp.concatenate([a,b],axis=1)
            xh,xl=split(x)
            acc=None
            for s in range(9):
                wh=wh_ref[s*m:(s+1)*m,:]
                wl=wl_ref[s*m:(s+1)*m,:]
                p=jnp.dot(wh,xh,preferred_element_type=f32)+(jnp.dot(wl,xh,preferred_element_type=f32)+jnp.dot(wh,xl,preferred_element_type=f32))
                off=(s//3)*16+s%3
                if off:
                    p=[pltpu.roll(p[:,h*128:(h+1)*128],128-off,1) for h in range(2)]
                else:
                    p=[p[:,h*128:(h+1)*128] for h in range(2)]
                acc=p if acc is None else [u+v for u,v in zip(acc,p)]
            store(r0,acc)
            return 0
        lax.fori_loop(0,Z//(2*zb),step,0)
    load_w(w1_ref)
    mask=mask_ref[0:1,:]
    def store1(r0,acc):
        for h in range(2):
            t_ref[pl.ds(pl.multiple_of(r0+h*m,8),m),:]=gelu(acc[h])*mask
    conv(store1)
    d_ref[top:top+rows,:]=t_ref[...]
    load_w(w2_ref)
    def store2(r0,acc):
        for h in range(2):
            t_ref[pl.ds(pl.multiple_of(r0+h*m,8),m),:]=acc[h]
    conv(store2)
    for j in range(C//2):
        x=jnp.concatenate([t_ref[pl.ds(2*j+e,Z,stride=C),:] for e in range(2)],axis=0)
        y=x.T
        for xx in range(4):
            out_ref[xx,:,j*128:(j+1)*128]=y[16*xx:16*xx+8,:]

def conv_call(ext,w1,w2,mask):
    return pl.pallas_call(conv_body,
        out_shape=jax.ShapeDtypeStruct((4,8,C*Z),jnp.float32),
        in_specs=[pl.BlockSpec(memory_space=pltpu.VMEM)]*4,
        out_specs=pl.BlockSpec(memory_space=pltpu.VMEM),
        scratch_shapes=[pltpu.VMEM((Z*C,128),jnp.float32),pltpu.VMEM((Z*C+80,128),jnp.float32),
            pltpu.VMEM((1296,224),jnp.float32),pltpu.VMEM((1296,224),BF),pltpu.VMEM((1296,224),BF)],
        name="conv_pair",
    )(ext,w1,w2,mask)


def dft_wave(freqs, length, sign):
    angle = sign * 2.0 * np.pi * np.outer(freqs, np.arange(length)) / length
    return np.cos(angle) + 1j * np.sin(angle)


def mode_freqs(kept, length):
    places = np.arange(2 * kept)
    return np.where(places < kept, places, places + length - 2 * kept)


def line_table(wave, outer, inner, outer_to, inner_to):
    shaped = wave.reshape(outer_to, inner_to, outer, inner)
    parts = np.stack([shaped.real, shaped.imag])
    table = np.einsum("cbqal,jk->lajcqbk", parts, np.eye(4))
    return table.reshape(inner * outer * 4, 2 * inner_to * outer_to * 4).astype(np.float32)


def plane_table(wave, outer, inner, outer_to, inner_to, order):
    shaped = wave.reshape(outer_to, inner_to, outer, inner)
    turned = np.stack([np.stack([shaped * 1j ** (c + r) for r in range(2)]) for c in range(2)])
    parts = np.stack([turned.real, turned.imag])
    table = np.einsum("ecrpmal->" + order + "carl", parts)
    return table.reshape(2 * outer_to * inner_to, 4 * outer * inner).astype(np.float32)


def dot(left, right):
    return jnp.dot(left, right, precision=highest, preferred_element_type=jnp.float32)


def swap_lanes(tiles, low):
    tiles = list(tiles)
    lane = lax.broadcasted_iota(jnp.int32, (8, 128), 1)
    bit = 1
    while bit < len(tiles):
        width = low * bit
        upper = (lane & width) != 0
        for at in range(len(tiles)):
            if at & bit == 0:
                first, second = tiles[at], tiles[at | bit]
                tiles[at] = jnp.where(upper, pltpu.roll(second, width, 1), first)
                tiles[at | bit] = jnp.where(upper, second, pltpu.roll(first, 128 - width, 1))
        bit *= 2
    return tiles


def swap_halves(tile):
    row = lax.broadcasted_iota(jnp.int32, (8, 128), 0)
    lane = lax.broadcasted_iota(jnp.int32, (8, 128), 1)
    same = (row >= 4) == (lane >= 64)
    return jnp.where(same, tile, pltpu.roll(pltpu.roll(tile, 4, 0), 64, 1))


def forward_z_body(cells_ref, table_ref, out_ref, rows_ref):
    groups = C // 4
    stacked = jnp.concatenate(
        [cells_ref[:, :, g * 256 : (g + 1) * 256].reshape(32, 256) for g in range(groups)], axis=0
    )
    rows_ref[0 : 32 * groups, :] = dot(stacked, table_ref[...])
    rows_ref[32 * groups :, :] = jnp.zeros((32, 128), jnp.float32)
    for pair in range((groups + 1) // 2):
        tiles = [
            swap_halves(rows_ref[pl.ds(64 * pair + y, 8, stride=8), :]) for y in range(8)
        ]
        tiles = swap_lanes(tiles, 16)
        for slot in range(8):
            group, part = 2 * pair + slot // 4, slot % 4
            if group < groups and part < 3:
                out_ref[group * 3 + part] = tiles[slot]
    for spare in range(3 * groups, out_ref.shape[0]):
        out_ref[spare] = jnp.zeros((8, 128), jnp.float32)


def planes(in_ref, line_ref, plane_ref, rows_ref, outer, inner):
    for a in range(outer):
        tiles = swap_lanes([in_ref[a * inner + b] for b in range(inner)], 4)
        for k in range(4):
            rows_ref[k * 8 * outer + a * 8 : k * 8 * outer + a * 8 + 8, :] = tiles[k]
    lines = dot(rows_ref[...], line_ref[...])
    results = []
    for k in range(4):
        part = lines[k * 8 * outer : (k + 1) * 8 * outer]
        stacked = jnp.concatenate([part[:, :128], part[:, 128:]], axis=0)
        results.append(dot(plane_ref[...], stacked))
    return results


def forward_xy_body(in_ref, line_ref, plane_ref, out_ref, rows_ref, turn_ref):
    outer, inner = 8, 4
    results = planes(in_ref, line_ref, plane_ref, rows_ref, outer, inner)
    for k in range(4):
        turn_ref[pl.ds(k, 8 * outer, stride=4), :] = results[k]
    for a in range(outer):
        tiles = swap_lanes([turn_ref[a * 32 + m * 8 : a * 32 + m * 8 + 8, :] for m in range(4)], 4)
        for b in range(inner):
            out_ref[a * inner + b] = tiles[b]


def inverse_xy_body(in_ref, line_ref, plane_ref, out_ref, rows_ref):
    outer, inner = 8, 4
    results = planes(in_ref, line_ref, plane_ref, rows_ref, outer, inner)
    for a in range(outer):
        tiles = swap_lanes([results[k][a * 8 : a * 8 + 8] for k in range(4)], 4)
        for b in range(inner):
            out_ref[a * inner + b] = tiles[b]


def mix_body(in_ref, real_ref, imag_ref, spread_ref, order_ref, out_ref, left_ref, mixed_ref):
    groups = C // 4
    pairs = (groups + 1) // 2
    row = lax.broadcasted_iota(jnp.int32, (8, 128), 0)
    low = row < 4
    zero = jnp.zeros((8, 128), jnp.float32)
    for t in range(pairs):
        real_parts, imag_parts = [], []
        for part in range(3):
            first = in_ref[2 * t * 3 + part]
            second = in_ref[(2 * t + 1) * 3 + part] if 2 * t + 1 < groups else zero
            real_parts.append(jnp.where(low, first, pltpu.roll(second, 4, 0)))
            imag_parts.append(jnp.where(low, pltpu.roll(first, 4, 0), second))
        for e, parts in enumerate((real_parts, imag_parts)):
            tiles = swap_lanes(parts + [zero], 4)
            for m in range(4):
                at = ((e * 4 + m) * pairs + t) * 8
                left_ref[at : at + 8, :] = tiles[m]
    hi, lo = split(left_ref[...])
    left = jnp.concatenate([hi, lo], axis=1)

    def step(q, carry):
        table = spread_ref[q]
        spread = jnp.dot(
            left, jnp.concatenate([table, table], axis=0), preferred_element_type=jnp.float32
        )
        for m in range(4):
            re = spread[m * 8 * pairs : m * 8 * pairs + C]
            im = spread[(4 + m) * 8 * pairs : (4 + m) * 8 * pairs + C]
            wr = real_ref[m, q]
            wi = imag_ref[m, q]
            at = q * 8 + m
            mixed_ref[pl.ds(at, 1), :] = jnp.sum(re * wr - im * wi, axis=0, keepdims=True)
            mixed_ref[pl.ds(at + 4, 1), :] = jnp.sum(re * wi + im * wr, axis=0, keepdims=True)
        return carry

    lax.fori_loop(0, 8, step, 0)
    mixed = mixed_ref[...]
    hi = mixed.astype(BF)
    rest = mixed - hi.astype(jnp.float32)
    mid, lo = split(rest)
    placed = jnp.dot(
        jnp.concatenate([hi, mid, lo], axis=0), order_ref[...], preferred_element_type=jnp.float32
    )
    placed = placed[0:64] + (placed[64:128] + placed[128:192])
    for block in range(out_ref.shape[0] // 8):
        tiles = [placed[8 * q : 8 * q + 8, block * 128 : (block + 1) * 128] for q in range(8)]
        tiles = swap_lanes(tiles, 16)
        for slot in range(8):
            out_ref[block * 8 + slot] = tiles[slot]


def inverse_z_body(in_ref, table_ref, conv_ref, out_ref, rows_ref, cells_ref):
    groups = C // 4
    zero = jnp.zeros((8, 128), jnp.float32)
    pairs = (groups + 1) // 2
    for pair in range(pairs):
        tiles = []
        for slot in range(8):
            group, part = 2 * pair + slot // 4, slot % 4
            tiles.append(in_ref[group * 3 + part] if group < groups and part < 3 else zero)
        tiles = swap_lanes(tiles, 16)
        for y in range(8):
            rows_ref[64 * pair + 8 * y : 64 * pair + 8 * y + 8, :] = swap_halves(tiles[y])
    for half in range(2):
        cells_ref[half] = dot(rows_ref[...], table_ref[:, half * 128 : (half + 1) * 128])
    for x in range(4):
        for group in range(groups):
            at = 64 * (group // 2) + 4 * (group % 2) + x
            for half in range(2):
                lanes = slice(group * 256 + half * 128, group * 256 + half * 128 + 128)
                spectral = cells_ref[half, pl.ds(at, 8, stride=8), :]
                out_ref[x, :, lanes] = gelu(spectral + conv_ref[x, :, lanes])


def local_call(body, out_shape, scratch, name, *operands):
    return pl.pallas_call(
        body,
        out_shape=jax.ShapeDtypeStruct(out_shape, jnp.float32),
        in_specs=[pl.BlockSpec(memory_space=pltpu.VMEM)] * len(operands),
        out_specs=pl.BlockSpec(memory_space=pltpu.VMEM),
        scratch_shapes=scratch,
        name=name,
    )(*operands)


def complex_product(spec, table, real, imag):
    cosine = jnp.asarray(table.real.astype(np.float32))
    sine = jnp.asarray(table.imag.astype(np.float32))

    def product(left, right):
        return jnp.einsum(spec, left, right, precision=highest)

    return (
        product(cosine, real) - product(sine, imag),
        product(cosine, imag) + product(sine, real),
    )


def transform(wave_x, wave_y, parts, split_to):
    a, b, _, x, y, _, _ = parts.shape
    shaped = jnp.transpose(parts, (2, 0, 3, 1, 4, 5, 6)).reshape(2, a * x, b * y, 4, 4)
    real, imag = complex_product("qy,xykj->xqkj", wave_y, shaped[0], shaped[1])
    real, imag = complex_product("px,xqkj->pqkj", wave_x, real, imag)
    return jnp.stack([real, imag]).reshape((2,) + split_to + (4, 4))


def on_device(state_field, conv_first, conv_second, spec_real, spec_imag):
    rows_here, cols_here = state_field.shape[:2]
    kept_x, kept_y = spec_real.shape[:2]
    count_x, count_y = lax.axis_size("gx"), lax.axis_size("gy")
    devices = count_x * count_y
    total_x, total_y = rows_here * count_x, cols_here * count_y
    groups, thirds = C // 4, MZ // 4
    owners = groups * thirds
    if (rows_here, cols_here) != (4, 8) or owners > devices:
        raise ValueError("unsupported block")
    both = ("gx", "gy")
    row_start = lax.axis_index("gx") * rows_here
    col_start = lax.axis_index("gy") * cols_here
    f32 = jnp.float32

    wave_z = dft_wave(np.arange(MZ), Z, -1.0).reshape(thirds, 4, Z)
    wave_z = np.concatenate([wave_z, np.zeros((1, 4, Z))])
    parts_z = np.stack([wave_z.real, wave_z.imag])
    forward_z = np.einsum("egrz,ck->czegkr", parts_z, np.eye(4)).reshape(4 * Z, 128)
    gains = np.where(np.arange(16) == 0, 1.0, 2.0).reshape(4, 4) / (total_x * total_y * Z)
    inverse_z = np.einsum("egrz,gr,ck->egcrkz", parts_z, gains, np.eye(4)).reshape(128, 4 * Z)
    forward_x = dft_wave(mode_freqs(MX, total_x), total_x, -1.0)
    forward_y = dft_wave(mode_freqs(MY, total_y), total_y, -1.0)
    inverse_x, inverse_y = np.conj(forward_x).T, np.conj(forward_y).T

    extended = with_halo(state_field, (("gx", 0), ("gy", 1)), 2)
    extended = jnp.pad(extended, ((0, 0), (0, 4), (0, 0)))
    lanes = jnp.arange(128, dtype=jnp.int32)[None, :]
    cell_x = row_start - 1 + lanes // 16
    cell_y = col_start - 1 + lanes % 16
    inside = (cell_x >= 0) & (cell_x < total_x) & (cell_y >= 0) & (cell_y < total_y)
    mask = jnp.broadcast_to(inside.astype(f32), (8, 128))
    conv_out = conv_call(extended, conv_first, conv_second, mask)

    columns = local_call(
        forward_z_body,
        (devices, 8, 128),
        [pltpu.VMEM((32 * (groups + 1), 128), f32)],
        "forward_z",
        state_field,
        jnp.asarray(forward_z.astype(np.float32)),
    )
    columns = lax.all_to_all(columns, both, 0, 0, tiled=True)
    fast = (count_x, count_y, kept_x, kept_y) == (8, 4, 4, 8)
    if fast:
        pairs = (groups + 1) // 2
        modes = local_call(
            forward_xy_body,
            (devices, 8, 128),
            [pltpu.VMEM((256, 128), f32)] * 2,
            "forward_xy",
            columns,
            line_table(forward_y, count_y, cols_here, count_y, kept_y),
            plane_table(forward_x, count_x, rows_here, count_x, kept_x, "pme"),
        )
        modes = lax.all_to_all(modes, both, 0, 0, tiled=True)
        spread = np.zeros((kept_y, kept_y, 16, MZ, C))
        for q in range(kept_y):
            for r in range(MZ):
                spread[q, q, r, r, :] = 1.0
        order = np.zeros((MZ, C, devices, 16))
        for r in range(MZ):
            for o in range(C):
                order[r, o, (o // 4) * thirds + r // 4, (o % 4) * 4 + r % 4] = 1.0
        mixed = local_call(
            mix_body,
            (devices, 8, 128),
            [pltpu.VMEM((2 * 4 * pairs * 8, 128), f32), pltpu.VMEM((64, MZ * C), f32)],
            "mix",
            modes,
            spec_real,
            spec_imag,
            jnp.asarray(spread.reshape(kept_y, 128, MZ * C), BF),
            jnp.asarray(order.reshape(MZ * C, devices * 16), BF),
        )
        mixed = lax.all_to_all(mixed, both, 0, 0, tiled=True)
        back = local_call(
            inverse_xy_body,
            (devices, 8, 128),
            [pltpu.VMEM((256, 128), f32)],
            "inverse_xy",
            mixed,
            line_table(inverse_y, count_y, kept_y, count_y, cols_here),
            plane_table(inverse_x, count_x, kept_x, count_x, rows_here, "pem"),
        )
    else:
        parts = columns.reshape(count_x, count_y, 2, rows_here, cols_here, 4, 4)
        modes = transform(
            forward_x, forward_y, parts, (count_x, kept_x, count_y, kept_y)
        )
        modes = jnp.transpose(modes, (1, 3, 0, 5, 4, 2, 6))
        modes = modes.reshape(devices, 8, kept_y * kept_x * 4)
        modes = lax.all_to_all(modes, both, 0, 0, tiled=True)[:owners]
        modes = modes.reshape(groups, thirds, 2, 4, kept_y, kept_x, 4)
        modes = jnp.transpose(modes, (2, 5, 4, 0, 3, 1, 6))
        modes = modes.reshape(2, kept_x, kept_y, C, MZ)
        weight_real = spec_real.reshape(kept_x, kept_y, C, MZ, C)
        weight_imag = spec_imag.reshape(kept_x, kept_y, C, MZ, C)

        def product(left, right):
            return jnp.einsum("abik,abiko->abok", left, right, precision=highest)

        mixed = jnp.stack(
            [
                product(modes[0], weight_real) - product(modes[1], weight_imag),
                product(modes[0], weight_imag) + product(modes[1], weight_real),
            ]
        ).reshape(2, kept_x, kept_y, groups, 4, thirds, 4)
        mixed = jnp.transpose(mixed, (3, 5, 0, 1, 2, 4, 6))
        mixed = mixed.reshape(owners, 2 * kept_x, kept_y * 16)
        mixed = jnp.pad(mixed, ((0, devices - owners), (0, 0), (0, 0)))
        mixed = lax.all_to_all(mixed, both, 0, 0, tiled=True)
        parts = mixed.reshape(count_x, count_y, 2, kept_x, kept_y, 4, 4)
        back = transform(
            inverse_x, inverse_y, parts, (count_x, rows_here, count_y, cols_here)
        )
        back = jnp.transpose(back, (1, 3, 0, 2, 4, 5, 6)).reshape(devices, 8, 128)
    back = lax.all_to_all(back, both, 0, 0, tiled=True)
    return local_call(
        inverse_z_body,
        (rows_here, cols_here, C * Z),
        [pltpu.VMEM((64 * ((groups + 1) // 2), 128), f32), pltpu.VMEM((2, 64 * ((groups + 1) // 2), 128), f32)],
        "inverse_z",
        back,
        jnp.asarray(inverse_z.astype(np.float32)),
        conv_out,
    )


def solution(mesh):
    in_specs = (P("gx", "gy", None), P(), P(), P("gx", "gy", None, None), P("gx", "gy", None, None))
    out_specs = P("gx", "gy", None)
    return jax.shard_map(
        on_device, mesh=mesh, in_specs=in_specs, out_specs=out_specs, check_vma=False
    )
```

time: 174 us -> 87.6 us (0.50)
  waiting for transfers between devices: 56.2 us -> 10.8 us
  blocking collectives: 26.7 us -> 0 us
  starting transfers between devices: 8.53 us -> 28.5 us
  Pallas kernels: 16.7 us -> 34.4 us
  between operations: 14.5 us -> 0.18 us
  local copies, waits for them, and re-layouts: 26.2 us -> 11.9 us
  other arithmetic: 14 us -> 1.31 us
  matrix products: 10.8 us -> 0 us
    unnamed x3 -> x0, waiting for transfers between devices: 53.4 us -> none
    all_gather x2 -> x0, blocking collectives: 26.7 us -> none  [the longest x1 15.9 us: on_device(): shard_piece = lax.all_gather(mixed, 'gy', axis=0, tiled=True)]
    all_to_all x0 -> x4, starting transfers between devices: none -> 19 us  [the longest x1 7.11 us: on_device(): columns = lax.all_to_all(columns, both, 0, 0, tiled=True)]
    reshape x15 -> x0, local copies, waits for them, and re-layouts: 18.9 us -> none  [the longest x1 8.04 us: on_device(): weight_imag = spec_imag.reshape(kxd_rows, kyd_rows, C, MZ, C)]
    pallas_call x0 -> x5, Pallas kernels: none -> 17.7 us  [local_call(): pl.pallas_call(body, out_shape=jax.ShapeDtypeStruct(out_shape, jnp.float3...]
    all_to_all x0 -> x4, waiting for transfers between devices: none -> 10.8 us  [the longest x1 8.35 us: on_device(): modes = lax.all_to_all(modes, both, 0, 0, tiled=True)]
    dot_general x20 -> x0, matrix products: 10.8 us -> none  [the longest x12 7.27 us: matmul(): return jnp.dot(left, right, precision=highest)]
    unnamed x2 -> x0, other arithmetic: 9.24 us -> none
  transfers between devices with their start and end apart: 6 -> 8, of which waited for: 2 -> 2; matrix products, arithmetic and copies ran while one was open for 14% -> 11% of each run, Pallas kernels for 10% -> 29%
where the time goes in v2:
time: 87.6 us; the launch traced here: 87.1 us
  Pallas kernels  34.4 us (39%)
  starting transfers between devices  28.5 us (33%)
  local copies, waits for them, and re-layouts  11.9 us (14%)
  waiting for transfers between devices  10.8 us (12%)
  other arithmetic  1.31 us (1%)
    pallas_call x5, Pallas kernels, local_call(): pl.pallas_call(body, out_shape=jax.ShapeDtypeStruct(out_shape, jnp.float3...  17.7 us
    pallas_call x1, Pallas kernels, conv_call(): pl.pallas_call(conv_body, out_shape=jax.ShapeDtypeStruct((4, 8, C * Z), j...  16.7 us
    unnamed x16, local copies, waits for them, and re-layouts  10.2 us
    all_to_all x1, waiting for transfers between devices, on_device(): modes = lax.all_to_all(modes, both, 0, 0, tiled=True)  8.35 us
    all_to_all x1, starting transfers between devices, on_device(): columns = lax.all_to_all(columns, both, 0, 0, tiled=True)  7.11 us
    ppermute x2, starting transfers between devices, with_halo(): lax.ppermute(tail, axis, [(i, (i + 1) % count) for i in range(ends)])  6.96 us
    all_to_all x1, starting transfers between devices, on_device(): modes = lax.all_to_all(modes, both, 0, 0, tiled=True)  6.72 us
    ppermute x2, starting transfers between devices, with_halo(): lax.ppermute(head, axis, [((i + 1) % count, i) for i in range(ends)])  2.58 us
  transfers between devices with their start and end apart: 8, of which 2 were waited for; matrix products, arithmetic and copies ran while one was open for 11% of the time, Pallas kernels for 29%

profile of v2, /device:TPU:0, one launch (start us, length us, event | category | flops | bytes accessed | tf_op | source)
XLA Modules:
  0.0 87.1 jit_solution(16607147851328059064)
XLA Ops:
  0.0 1.0 %fusion.3 = (f32[2,8,2304]{2,1,0:T(8,128)S(1)}, f32[2,8,2304]{2,1,0:T(8,128)S(1)}) fusion(f32[4,8,2304]{2,1,0:T(8,128)} %cells_ref.1), kind=kLoop, calls=%fused_computation.15 | loop fusion | bytes 589824 | tf_op jit(solution)/shard_map/slice | solution.py:22
  1.0 2.4 %collective-permute-start = (f32[2,8,2304]{2,1,0:T(8,128)S(1)}, f32[2,8,2304]{2,1,0:T(8,128)S(1)}, u32[]{:S(2)}, u32[]{:S(2)}) collective-permute-start(f32[2,8,2304]{2,1,0:T(8,128)S(1)} %get-tuple-element.8), channel_id=1, source_target_pairs={{0,4},{4,8},{8,12},{12,16},{16,20},{20,24},{24,28},{1,5},{5,9},{9,... | collective-permute-start | bytes 442376 | tf_op jit(solution)/shard_map/ppermute | solution.py:26
  3.4 2.3 %forward_z.1 = f32[32,8,128]{2,1,0:T(8,128)} custom-call(f32[4,8,2304]{2,1,0:T(8,128)} %cells_ref.1, f32[256,128]{1,0:T(8,128)} %constant.68.clone.table_ref), custom_call_target="tpu_custom_call" | custom-call | tf_op jit(solution)/shard_map/forward_z/pallas_call | solution.py:297
  5.8 7.1 %all-to-all-start = ((f32[32,8,128]{2,1,0:T(8,128)}), f32[32,8,128]{2,1,0:T(8,128)S(1)}, u32[]{:S(2)}, u32[]{:S(2)}) async-start(f32[32,8,128]{2,1,0:T(8,128)} %forward_z.1), calls=%async_computation | async-start | bytes 262144 | tf_op jit(solution)/shard_map/all_to_all | solution.py:370
  12.9 1.3 %collective-permute-start.1 = (f32[2,8,2304]{2,1,0:T(8,128)S(1)}, f32[2,8,2304]{2,1,0:T(8,128)S(1)}, u32[]{:S(2)}, u32[]{:S(2)}) collective-permute-start(f32[2,8,2304]{2,1,0:T(8,128)S(1)} %get-tuple-element.7), channel_id=1, source_target_pairs={{4,0},{8,4},{12,8},{16,12},{20,16},{24,20},{28,24},{5,1},{9,5},{13... | collective-permute-start | bytes 442376 | tf_op jit(solution)/shard_map/ppermute | solution.py:28
  14.2 4.7 %copy.14.real_ref = f32[4,8,36,432]{3,2,1,0:T(8,128)} copy(f32[4,8,36,432]{3,1,2,0:T(8,128)} %param.16) | data formatting | bytes 3981312 | tf_op args[3]
  18.9 2.9 %copy.15.imag_ref = f32[4,8,36,432]{3,2,1,0:T(8,128)} copy(f32[4,8,36,432]{3,1,2,0:T(8,128)S(1)} %copy-done.1) | data formatting | bytes 3981312 | tf_op args[4]
  21.9 0.6 copy-done.4
  22.5 2.9 %forward_xy.1 = f32[32,8,128]{2,1,0:T(8,128)} custom-call(f32[32,8,128]{2,1,0:T(8,128)} %copy-done.4, f32[128,256]{1,0:T(8,128)} %constant.69.clone.line_ref, f32[64,128]{1,0:T(8,128)} %constant.70.clone.plane_ref), custom_call_target="tpu_custom_call" | custom-call | tf_op jit(solution)/shard_map/forward_xy/pallas_call | solution.py:297
  25.4 6.7 %all-to-all-start.1 = ((f32[32,8,128]{2,1,0:T(8,128)}), f32[32,8,128]{2,1,0:T(8,128)S(1)}, u32[]{:S(2)}, u32[]{:S(2)}) async-start(f32[32,8,128]{2,1,0:T(8,128)} %forward_xy.1), calls=%async_computation.1 | async-start | bytes 262144 | tf_op jit(solution)/shard_map/all_to_all | solution.py:383
  32.2 8.3 %all-to-all-done.1.in_ref = f32[32,8,128]{2,1,0:T(8,128)S(1)} async-done(((f32[32,8,128]{2,1,0:T(8,128)}), f32[32,8,128]{2,1,0:T(8,128)S(1)}, u32[]{:S(2)}, u32[]{:S(2)}) %all-to-all-start.1) | async-done | bytes 131104 | tf_op jit(solution)/shard_map/all_to_all | solution.py:383
  40.6 0.7 copy-done.2
  41.2 6.9 %mix.1 = f32[32,8,128]{2,1,0:T(8,128)} custom-call(f32[32,8,128]{2,1,0:T(8,128)} %copy-done.2, f32[4,8,36,432]{3,2,1,0:T(8,128)} %copy.14.real_ref, f32[4,8,36,432]{3,2,1,0:T(8,128)} %copy.15.imag_ref, bf16[8,128,432]{2,1,0:T(8,128)(2,1)} %constant.71.clone.spread_ref, bf16[432,512]{1,0:T(8,128)(2,1)} %constant.72.clone.order_ref), custom_call_target="tpu_custom_call" | custom-call | tf_op jit(solution)/shard_map/mix/pallas_call | solution.py:297
  48.2 2.6 %all-to-all-start.2 = ((f32[32,8,128]{2,1,0:T(8,128)}), f32[32,8,128]{2,1,0:T(8,128)S(1)}, u32[]{:S(2)}, u32[]{:S(2)}) async-start(f32[32,8,128]{2,1,0:T(8,128)} %mix.1), calls=%async_computation.2 | async-start | bytes 262144 | tf_op jit(solution)/shard_map/all_to_all | solution.py:403
  50.8 1.3 %collective-permute-start.3 = (f32[8,2,2304]{2,1,0:T(2,128)S(1)}, f32[8,2,2304]{2,1,0:T(2,128)S(1)}, u32[]{:S(2)}, u32[]{:S(2)}) collective-permute-start(f32[8,2,2304]{2,1,0:T(2,128)S(1)} %get-tuple-element.6), channel_id=1, source_target_pairs={{1,0},{2,1},{3,2},{5,4},{6,5},{7,6},{9,8},{10,9},{11,10},{13,12},{... | collective-permute-start | bytes 442376 | tf_op jit(solution)/shard_map/ppermute | solution.py:28
  52.1 4.6 %collective-permute-start.2 = (f32[8,2,2304]{2,1,0:T(2,128)S(1)}, f32[8,2,2304]{2,1,0:T(2,128)S(1)}, u32[]{:S(2)}, u32[]{:S(2)}) collective-permute-start(f32[8,2,2304]{2,1,0:T(2,128)S(1)} %get-tuple-element.5), channel_id=1, source_target_pairs={{0,1},{1,2},{2,3},{4,5},{5,6},{6,7},{8,9},{9,10},{10,11},{12,13},{... | collective-permute-start | bytes 442376 | tf_op jit(solution)/shard_map/ppermute | solution.py:26
  56.7 2.4 %all-to-all-done.2.in_ref = f32[32,8,128]{2,1,0:T(8,128)S(1)} async-done(((f32[32,8,128]{2,1,0:T(8,128)}), f32[32,8,128]{2,1,0:T(8,128)S(1)}, u32[]{:S(2)}, u32[]{:S(2)}) %all-to-all-start.2) | async-done | bytes 131104 | tf_op jit(solution)/shard_map/all_to_all | solution.py:403
  59.1 0.7 copy-done.3
  59.8 2.9 %inverse_xy.1 = f32[32,8,128]{2,1,0:T(8,128)} custom-call(f32[32,8,128]{2,1,0:T(8,128)} %copy-done.3, f32[128,256]{1,0:T(8,128)} %constant.73.clone.line_ref, f32[64,128]{1,0:T(8,128)} %constant.74.clone.plane_ref), custom_call_target="tpu_custom_call" | custom-call | tf_op jit(solution)/shard_map/inverse_xy/pallas_call | solution.py:297
  62.7 2.6 %all-to-all-start.3 = ((f32[32,8,128]{2,1,0:T(8,128)}), f32[32,8,128]{2,1,0:T(8,128)S(1)}, u32[]{:S(2)}, u32[]{:S(2)}) async-start(f32[32,8,128]{2,1,0:T(8,128)} %inverse_xy.1), calls=%async_computation.3 | async-start | bytes 262144 | tf_op jit(solution)/shard_map/all_to_all | solution.py:445
  65.3 1.3 %select_maximum_fusion.ext_ref = f32[8,16,2304]{2,1,0:T(8,128)} fusion(f32[8,2,2304]{2,1,0:T(2,128)S(1)} %collective-permute-done.3, f32[8,8,2304]{2,1,0:T(8,128)S(1)} %constant_dynamic-update-slice_fusion, f32[8,2,2304]{2,1,0:T(2,128)S(1)} %collective-permute-done.2), kind=kLoop, calls=%fused_computation | loop fusion | flops 1769472 | bytes 2064384 | tf_op jit(solution)/shard_map/concatenate | solution.py:24
  67.2 16.7 %conv_pair.1.conv_ref = f32[4,8,2304]{2,1,0:T(8,128)} custom-call(f32[8,16,2304]{2,1,0:T(8,128)} %select_maximum_fusion.ext_ref, f32[3,3,36,108]{3,2,1,0:T(8,128)} %w1_ref.1, f32[3,3,36,108]{3,2,1,0:T(8,128)} %w2_ref.1, f32[8,128]{1,0:T(8,128)} %broadcast_in_dim.2.mask_ref), custom_call_target="tpu_custom_call" | custom-call | tf_op jit(solution)/shard_map/conv_pair/pallas_call | solution.py:105
  83.9 0.7 copy-done.5
  84.5 2.6 %inverse_z.1 = f32[4,8,2304]{2,1,0:T(8,128)} custom-call(f32[32,8,128]{2,1,0:T(8,128)} %copy-done.5, f32[128,256]{1,0:T(8,128)} %constant.75.clone.table_ref, f32[4,8,2304]{2,1,0:T(8,128)} %conv_pair.1.conv_ref), custom_call_target="tpu_custom_call" | custom-call | tf_op jit(solution)/shard_map/inverse_z/pallas_call | solution.py:297
  (20 shorter events, 0.8 us)
Async XLA Ops:
  1.0 20.8 %collective-permute-start = (f32[2,8,2304]{2,1,0:T(8,128)S(1)}, f32[2,8,2304]{2,1,0:T(8,128)S(1)}, u32[]{:S(2)}, u32[]{:S(2)}) collective-permute-start(f32[2,8,2304]{2,1,0:T(8,128)S(1)} %get-tuple-element.8), channel_id=1, source_target_pairs={{0,4},{4,8},{8,12},{12,16},{16,20},{20,24},{24,28},{1,5},{5,9},{9,... | collective-permute-start | bytes 442376 | tf_op jit(solution)/shard_map/ppermute | solution.py:26
  5.8 16.1 %all-to-all-start = ((f32[32,8,128]{2,1,0:T(8,128)}), f32[32,8,128]{2,1,0:T(8,128)S(1)}, u32[]{:S(2)}, u32[]{:S(2)}) async-start(f32[32,8,128]{2,1,0:T(8,128)} %forward_z.1), calls=%async_computation | async-start | bytes 262144 | tf_op jit(solution)/shard_map/all_to_all | solution.py:370
  12.9 19.3 %collective-permute-start.1 = (f32[2,8,2304]{2,1,0:T(8,128)S(1)}, f32[2,8,2304]{2,1,0:T(8,128)S(1)}, u32[]{:S(2)}, u32[]{:S(2)}) collective-permute-start(f32[2,8,2304]{2,1,0:T(8,128)S(1)} %get-tuple-element.7), channel_id=1, source_target_pairs={{4,0},{8,4},{12,8},{16,12},{20,16},{24,20},{28,24},{5,1},{9,5},{13... | collective-permute-start | bytes 442376 | tf_op jit(solution)/shard_map/ppermute | solution.py:28
  14.2 4.7 %copy-start.1 = (f32[4,8,36,432]{3,1,2,0:T(8,128)S(1)}, f32[4,8,36,432]{3,1,2,0:T(8,128)}, u32[]{:S(2)}) copy-start(f32[4,8,36,432]{3,1,2,0:T(8,128)} %param.17) | copy-start | bytes 5971972
  18.9 2.9 %copy-start = (f32[4,8,2304]{2,1,0:T(8,128)S(1)}, f32[4,8,2304]{2,1,0:T(8,128)}, u32[]{:S(2)}) copy-start(f32[4,8,2304]{2,1,0:T(8,128)} %cells_ref.1) | copy-start | bytes 884740
  21.9 0.7 copy-start.4
  25.4 15.1 %all-to-all-start.1 = ((f32[32,8,128]{2,1,0:T(8,128)}), f32[32,8,128]{2,1,0:T(8,128)S(1)}, u32[]{:S(2)}, u32[]{:S(2)}) async-start(f32[32,8,128]{2,1,0:T(8,128)} %forward_xy.1), calls=%async_computation.1 | async-start | bytes 262144 | tf_op jit(solution)/shard_map/all_to_all | solution.py:383
  40.5 0.7 copy-start.2
  48.2 11.0 %all-to-all-start.2 = ((f32[32,8,128]{2,1,0:T(8,128)}), f32[32,8,128]{2,1,0:T(8,128)S(1)}, u32[]{:S(2)}, u32[]{:S(2)}) async-start(f32[32,8,128]{2,1,0:T(8,128)} %mix.1), calls=%async_computation.2 | async-start | bytes 262144 | tf_op jit(solution)/shard_map/all_to_all | solution.py:403
  50.8 14.4 %collective-permute-start.3 = (f32[8,2,2304]{2,1,0:T(2,128)S(1)}, f32[8,2,2304]{2,1,0:T(2,128)S(1)}, u32[]{:S(2)}, u32[]{:S(2)}) collective-permute-start(f32[8,2,2304]{2,1,0:T(2,128)S(1)} %get-tuple-element.6), channel_id=1, source_target_pairs={{1,0},{2,1},{3,2},{5,4},{6,5},{7,6},{9,8},{10,9},{11,10},{13,12},{... | collective-permute-start | bytes 442376 | tf_op jit(solution)/shard_map/ppermute | solution.py:28
  52.1 13.1 %collective-permute-start.2 = (f32[8,2,2304]{2,1,0:T(2,128)S(1)}, f32[8,2,2304]{2,1,0:T(2,128)S(1)}, u32[]{:S(2)}, u32[]{:S(2)}) collective-permute-start(f32[8,2,2304]{2,1,0:T(2,128)S(1)} %get-tuple-element.5), channel_id=1, source_target_pairs={{0,1},{1,2},{2,3},{4,5},{5,6},{6,7},{8,9},{9,10},{10,11},{12,13},{... | collective-permute-start | bytes 442376 | tf_op jit(solution)/shard_map/ppermute | solution.py:26
  59.1 0.7 copy-start.3
  62.7 21.2 %all-to-all-start.3 = ((f32[32,8,128]{2,1,0:T(8,128)}), f32[32,8,128]{2,1,0:T(8,128)S(1)}, u32[]{:S(2)}, u32[]{:S(2)}) async-start(f32[32,8,128]{2,1,0:T(8,128)} %inverse_xy.1), calls=%async_computation.3 | async-start | bytes 262144 | tf_op jit(solution)/shard_map/all_to_all | solution.py:445
  83.9 0.7 copy-start.5

commit v3 on v0

v3 whole, which is shorter than its diff:
```python
import numpy as np
import jax
import jax.numpy as jnp
from jax import lax
from jax.experimental import pallas as pl
from jax.experimental.pallas import tpu as pltpu
from jax.sharding import PartitionSpec as P


C = 36
Z = 64
MX = 16
MY = 16
MZ = 12
BF = jnp.bfloat16
highest = lax.Precision.HIGHEST


def gelu(x):
    return 0.5 * x * (1.0 + lax.erf(x * 0.7071067811865476))


def split(x):
    hi = x.astype(BF)
    return hi, (x - hi.astype(jnp.float32)).astype(BF)


STEP = 4
TOP = 40
DEPTH = 224
ROWS = Z * C
BLOCK = STEP * C


def load_filters(filter_ref, wide_ref, hi_ref, lo_ref):
    wide_ref[...] = jnp.zeros_like(wide_ref)
    for s in range(9):
        taps = filter_ref[s // 3, s % 3]
        for z in range(STEP):
            at = s * BLOCK + z * C
            lane = TOP - C + C * z
            wide_ref[at : at + C, lane : lane + 3 * C] = taps
    hi_ref[...], lo_ref[...] = split(wide_ref[...])


def convolve(data_ref, hi_ref, lo_ref, store):
    f32 = jnp.float32

    def step(g, carry):
        at = pl.multiple_of(g * 2 * BLOCK, 8)
        window = jnp.concatenate(
            [data_ref[pl.ds(pl.multiple_of(at + h * BLOCK, 8), DEPTH), :] for h in range(2)], axis=1
        )
        data_hi, data_lo = split(window)
        total = None
        for s in range(9):
            hi = hi_ref[s * BLOCK : (s + 1) * BLOCK, :]
            lo = lo_ref[s * BLOCK : (s + 1) * BLOCK, :]
            part = jnp.dot(hi, data_hi, preferred_element_type=f32) + (
                jnp.dot(lo, data_hi, preferred_element_type=f32)
                + jnp.dot(hi, data_lo, preferred_element_type=f32)
            )
            halves = [part[:, :128], part[:, 128:]]
            shift = (s // 3 - 1) * 16 + s % 3 - 1
            if shift:
                halves = [pltpu.roll(half, -shift % 128, 1) for half in halves]
            total = halves if total is None else [u + v for u, v in zip(total, halves)]
        for h in range(2):
            store(pl.multiple_of(at + h * BLOCK, 8), total[h])
        return carry

    lax.fori_loop(0, Z // (2 * STEP), step, 0)


def first_conv_body(
    cells_ref, top_ref, bottom_ref, left_ref, right_ref, filter_ref, mask_ref,
    out_ref, frame_ref, turn_ref, data_ref, wide_ref, hi_ref, lo_ref,
):
    f32 = jnp.float32
    frame_ref[:, 8:16, :] = jnp.zeros((8, 8, C * Z), f32)
    frame_ref[0:2, 0:8, :] = top_ref[...]
    frame_ref[2:6, 0:8, :] = cells_ref[...]
    frame_ref[6:8, 0:8, :] = bottom_ref[...]
    for x in range(8):
        frame_ref[x, 8:10, :] = right_ref[x]
        frame_ref[(x + 7) % 8, 14:16, :] = left_ref[x]
    data_ref[0:TOP, :] = jnp.zeros((TOP, 128), f32)
    data_ref[TOP + ROWS :, :] = jnp.zeros((TOP, 128), f32)
    for j in range(C * Z // 128):
        lanes = slice(j * 128, (j + 1) * 128)
        turn_ref[lanes, :] = frame_ref[:, :, lanes].reshape(128, 128).T
    for z in range(Z):
        data_ref[TOP + z * C : TOP + (z + 1) * C, :] = turn_ref[pl.ds(z, C, stride=Z), :]
    load_filters(filter_ref, wide_ref, hi_ref, lo_ref)
    mask = mask_ref[0:1, :]

    def store(at, total):
        turn_ref[pl.ds(at, BLOCK), :] = gelu(total) * mask

    convolve(data_ref, hi_ref, lo_ref, store)
    out_ref[0:TOP, :] = jnp.zeros((TOP, 128), f32)
    out_ref[TOP + ROWS :, :] = jnp.zeros((TOP, 128), f32)
    out_ref[TOP : TOP + ROWS, :] = turn_ref[...]


def second_conv_body(data_ref, filter_ref, out_ref, turn_ref, wide_ref, hi_ref, lo_ref):
    load_filters(filter_ref, wide_ref, hi_ref, lo_ref)

    def store(at, total):
        turn_ref[pl.ds(at, BLOCK), :] = total

    convolve(data_ref, hi_ref, lo_ref, store)
    for j in range(C * Z // 128):
        pieces = [turn_ref[pl.ds(2 * j + e, Z, stride=C), :] for e in range(2)]
        turned = jnp.concatenate(pieces, axis=0).T
        for x in range(4):
            out_ref[x, :, j * 128 : (j + 1) * 128] = turned[16 * x + 32 : 16 * x + 40, :]


def dft_wave(freqs, length, sign):
    angle = sign * 2.0 * np.pi * np.outer(freqs, np.arange(length)) / length
    return np.cos(angle) + 1j * np.sin(angle)


def mode_freqs(kept, length):
    places = np.arange(2 * kept)
    return np.where(places < kept, places, places + length - 2 * kept)


def halves(table):
    hi = table.astype(BF)
    lo = (table - hi.astype(np.float64)).astype(BF)
    return hi, lo


def line_table(wave, outer_to, inner_to, outer, inner):
    shaped = wave.reshape(outer_to, inner_to, outer, inner)
    turned = np.stack([shaped, shaped * 1j])
    parts = np.stack([turned.real, turned.imag])
    table = np.einsum("crAmal,uv->rlaucmAv", parts, np.eye(2))
    return table.reshape(4 * inner * outer, 4 * inner_to * outer_to)


def plane_table(lines, wave):
    cross = np.concatenate([wave.real, wave.imag])
    cross = np.pad(cross, ((0, 0), (0, lines.shape[1] - cross.shape[1])))
    return np.stack(halves(np.concatenate([lines, cross])))


def dot(left, right_hi, right_lo):
    f32 = jnp.float32
    hi, lo = split(left)
    return jnp.dot(hi, right_hi, preferred_element_type=f32) + (
        jnp.dot(lo, right_hi, preferred_element_type=f32)
        + jnp.dot(hi, right_lo, preferred_element_type=f32)
    )


def swap_lanes(tiles, low):
    tiles = list(tiles)
    lane = lax.broadcasted_iota(jnp.int32, (8, 128), 1)
    bit = 1
    while bit < len(tiles):
        width = low * bit
        upper = (lane & width) != 0
        for at in range(len(tiles)):
            if at & bit == 0:
                first, second = tiles[at], tiles[at | bit]
                tiles[at] = jnp.where(upper, pltpu.roll(second, width, 1), first)
                tiles[at | bit] = jnp.where(upper, second, pltpu.roll(first, 128 - width, 1))
        bit *= 2
    return tiles


def forward_z_body(field_ref, waves_ref, out_ref, head_ref, tail_ref, cells_ref, table_ref, sems):
    groups = C // 4
    copies = [
        pltpu.make_async_copy(field_ref, cells_ref, sems.at[0]),
        pltpu.make_async_copy(waves_ref, table_ref, sems.at[1]),
    ]
    for copy in copies:
        copy.start()
    for copy in copies:
        copy.wait()
    rows = cells_ref.shape[0]
    head_ref[...] = cells_ref[0:2]
    tail_ref[...] = cells_ref[rows - 2 : rows]
    stacked = jnp.concatenate(
        [cells_ref[:, :, g * 256 : (g + 1) * 256].reshape(32, 256) for g in range(groups)], axis=0
    )
    waves = dot(stacked, table_ref[0], table_ref[1])
    for group in range(groups):
        at = 32 * group
        tiles = swap_lanes([waves[at + 8 * x : at + 8 * x + 8] for x in range(4)], 16)
        for part in range(3):
            out_ref[group * 3 + part] = tiles[part]
    for spare in range(3 * groups, out_ref.shape[0]):
        out_ref[spare] = jnp.zeros((8, 128), jnp.float32)


def plane_body(in_ref, table_ref, out_ref, rows_ref):
    f32 = jnp.float32
    outer, inner = 8, 4
    for b in range(inner):
        tiles = swap_lanes([in_ref[a * inner + b] for a in range(outer)], 2)
        for g in range(8):
            rows_ref[g * 32 + b * 8 : g * 32 + b * 8 + 8, :] = tiles[g]
    lines = dot(rows_ref[...], table_ref[0, 0:128, :], table_ref[1, 0:128, :])
    minus = lax.broadcasted_iota(jnp.int32, (32, 128), 1) < 64
    results = []
    cross_hi, cross_lo = table_ref[0, 128:192, 0:32], table_ref[1, 128:192, 0:32]
    for g in range(0, 8, 2):
        part = jnp.concatenate([lines[g * 32 : g * 32 + 32], lines[g * 32 + 32 : g * 32 + 64]], axis=1)
        hi, lo = split(part)
        both = jnp.dot(cross_hi, hi, preferred_element_type=f32) + (
            jnp.dot(cross_lo, hi, preferred_element_type=f32)
            + jnp.dot(cross_hi, lo, preferred_element_type=f32)
        )
        for h in range(2):
            turned = pltpu.roll(both[32:, h * 128 : h * 128 + 128], 64, 1)
            plain = both[:32, h * 128 : h * 128 + 128]
            results.append(jnp.where(minus, plain - turned, plain + turned))
    for b in range(inner):
        tiles = swap_lanes([results[g][b * 8 : b * 8 + 8] for g in range(8)], 2)
        for a in range(outer):
            out_ref[a * inner + b] = tiles[a]


def mode_of(place):
    return jnp.floor((place.astype(jnp.float32) + 0.5) * (1.0 / C)).astype(jnp.int32)


def mix_body(in_ref, real_hbm, imag_hbm, out_ref, left_ref, real_ref, imag_ref, sems):
    f32 = jnp.float32
    groups = C // 4
    copies = [
        [
            pltpu.make_async_copy(source.at[:, :, k], held.at[k], sems.at[k, e])
            for e, (source, held) in enumerate(((real_hbm, real_ref), (imag_hbm, imag_ref)))
        ]
        for k in range(4)
    ]
    for pair in copies:
        for copy in pair:
            copy.start()
    width = MZ * C
    lane = lax.broadcasted_iota(jnp.int32, (256, width), 0) & 127
    mode = mode_of(lax.broadcasted_iota(jnp.int32, (1, width), 1))
    wanted = lane - ((mode >> 2) * 16 + (mode & 3))
    place = lax.broadcasted_iota(jnp.int32, (width, 1), 0)
    mode = mode_of(place)
    channel = place - mode * C
    column = ((channel >> 2) * 3 + (mode >> 2)) * 16 + (channel & 3) * 4 + (mode & 3)
    slots = lax.broadcasted_iota(jnp.int32, (width, out_ref.shape[0] * 16), 1)
    order = jnp.where(slots == column, 1.0, 0.0).astype(BF)
    zero = jnp.zeros((8, 128), f32)
    for group in range(groups):
        tiles = swap_lanes([in_ref[group * 3 + part] for part in range(3)] + [zero], 16)
        for m in range(4):
            at = (m * groups + group) * 8
            left_ref[at : at + 8, :] = tiles[m]
    hi, lo = split(left_ref[...])
    left = jnp.concatenate([hi, lo], axis=1)
    real = [jnp.zeros((8, MZ * C), f32) for _ in range(4)]
    imag = [jnp.zeros((8, MZ * C), f32) for _ in range(4)]
    for k in range(4):
        sides = []
        for e in range(2):
            table = jnp.where(wanted == e * 64 + k * 4, 1.0, 0.0).astype(BF)
            sides.append(jnp.dot(left, table, preferred_element_type=f32))
        for copy in copies[k]:
            copy.wait()
        for m in range(4):
            for group in range(groups):
                at = (m * groups + group) * 8
                re = sides[0][at : at + 8]
                im = sides[1][at : at + 8]
                wr = real_ref[k, m, group]
                wi = imag_ref[k, m, group]
                real[m] = real[m] + (re * wr - im * wi)
                imag[m] = imag[m] + (re * wi + im * wr)
    hi, lo = split(jnp.concatenate(real + imag, axis=0))
    placed = jnp.dot(jnp.concatenate([hi, lo], axis=0), order, preferred_element_type=f32)
    placed = placed[0:64] + placed[64:128]
    for block in range(out_ref.shape[0] // 8):
        tiles = [placed[8 * m : 8 * m + 8, block * 128 : (block + 1) * 128] for m in range(8)]
        tiles = swap_lanes(tiles, 16)
        for slot in range(8):
            out_ref[block * 8 + slot] = tiles[slot]


def inverse_z_body(in_ref, hi_ref, lo_ref, conv_ref, out_ref, rows_ref):
    groups = C // 4
    zero = jnp.zeros((8, 128), jnp.float32)
    for group in range(groups):
        tiles = swap_lanes([in_ref[group * 3 + part] for part in range(3)] + [zero], 16)
        for x in range(4):
            rows_ref[32 * group + 8 * x : 32 * group + 8 * x + 8, :] = tiles[x]
    cells = dot(rows_ref[...], hi_ref[...], lo_ref[...])
    for group in range(groups):
        lanes = slice(group * 256, (group + 1) * 256)
        for x in range(4):
            at = 32 * group + 8 * x
            out_ref[x, :, lanes] = gelu(cells[at : at + 8] + conv_ref[x, :, lanes])


def on_chip(value):
    return pltpu.with_memory_space_constraint(value, pltpu.VMEM)


def local_call(body, out_shape, scratch, *operands, keep=True, remote=(), more=()):
    shapes = [out_shape, *more]
    kinds = [pltpu.VMEM if keep else jax.ShapeDtypeStruct] + [pltpu.VMEM] * len(more)
    inside = pl.BlockSpec(memory_space=pltpu.VMEM)
    outside = pl.BlockSpec(memory_space=pltpu.HBM)
    results = pl.pallas_call(
        body,
        out_shape=[kind(shape, jnp.float32) for kind, shape in zip(kinds, shapes)],
        in_specs=[outside if at in remote else inside for at in range(len(operands))],
        out_specs=[inside] * len(shapes),
        scratch_shapes=scratch,
        compiler_params=pltpu.CompilerParams(vmem_limit_bytes=(62 if remote else 24) << 20),
    )(*operands)
    return results if more else results[0]


def complex_product(spec, table, real, imag):
    cosine = jnp.asarray(table.real.astype(np.float32))
    sine = jnp.asarray(table.imag.astype(np.float32))

    def product(left, right):
        return jnp.einsum(spec, left, right, precision=highest)

    return (
        product(cosine, real) - product(sine, imag),
        product(cosine, imag) + product(sine, real),
    )


def transform(wave_x, wave_y, parts, split_to):
    a, b, y, _, x, _, _ = parts.shape
    shaped = jnp.transpose(parts, (3, 0, 4, 1, 2, 5, 6)).reshape(2, a * x, b * y, 4, 4)
    real, imag = complex_product("qy,xykj->xqkj", wave_y, shaped[0], shaped[1])
    real, imag = complex_product("px,xqkj->pqkj", wave_x, real, imag)
    return jnp.stack([real, imag]).reshape((2,) + split_to + (4, 4))


def on_device(state_field, conv_first, conv_second, spec_real, spec_imag):
    rows_here, cols_here = state_field.shape[:2]
    kept_x, kept_y = spec_real.shape[:2]
    count_x, count_y = lax.axis_size("gx"), lax.axis_size("gy")
    devices = count_x * count_y
    total_x, total_y = rows_here * count_x, cols_here * count_y
    groups, thirds = C // 4, MZ // 4
    owners = groups * thirds
    if (rows_here, cols_here) != (4, 8) or owners > devices:
        raise ValueError("unsupported block")
    both = ("gx", "gy")
    row_start = lax.axis_index("gx") * rows_here
    col_start = lax.axis_index("gy") * cols_here
    f32 = jnp.float32

    wave_z = dft_wave(np.arange(MZ), Z, -1.0).reshape(thirds, 4, Z)
    wave_z = np.concatenate([wave_z, np.zeros((1, 4, Z))])
    parts_z = np.stack([wave_z.real, wave_z.imag])
    forward_z = np.einsum("egrz,ck->czegkr", parts_z, np.eye(4)).reshape(4 * Z, 128)
    gains = np.where(np.arange(16) == 0, 1.0, 2.0).reshape(4, 4) / (total_x * total_y * Z)
    inverse_z = np.einsum("egrz,gr,ck->egcrkz", parts_z, gains, np.eye(4)).reshape(128, 4 * Z)
    forward_x = dft_wave(mode_freqs(MX, total_x), total_x, -1.0)
    forward_y = dft_wave(mode_freqs(MY, total_y), total_y, -1.0)
    inverse_x, inverse_y = np.conj(forward_x).T, np.conj(forward_y).T

    def trade(block):
        return lax.all_to_all(block, both, 0, 0, tiled=True)

    def shift(block, axis, ahead):
        steps = range(lax.axis_size(axis) - 1)
        return lax.ppermute(block, axis, [(i, i + 1) if ahead else (i + 1, i) for i in steps])

    fast = (count_x, count_y, kept_x, kept_y) == (8, 4, 4, 8)

    edge = (2, cols_here, C * Z)
    columns, head, tail = local_call(
        forward_z_body,
        (devices, 8, 128),
        [
            pltpu.VMEM((rows_here, cols_here, C * Z), f32),
            pltpu.VMEM((2, 4 * Z, 128), BF),
            pltpu.SemaphoreType.DMA((2,)),
        ],
        state_field,
        np.stack(halves(forward_z)),
        keep=False,
        remote=(0, 1),
        more=(edge, edge),
    )
    columns = trade(columns)
    top, bottom = shift(tail, "gx", True), shift(head, "gx", False)

    if fast:
        modes = local_call(
            plane_body,
            (devices, 8, 128),
            [pltpu.VMEM((256, 128), f32)],
            on_chip(columns),
            plane_table(line_table(forward_x, count_x, kept_x, count_x, rows_here), forward_y),
            keep=False,
        )
    else:
        parts = columns.reshape(count_x, count_y, cols_here, 2, rows_here, 4, 4)
        modes = transform(forward_x, forward_y, parts, (count_x, kept_x, count_y, kept_y))
        modes = jnp.transpose(modes, (1, 3, 4, 0, 2, 5, 6))
        modes = modes.reshape(devices, kept_y, 2 * kept_x * 16)
    modes = trade(modes)
    parts = (top, state_field, bottom)
    last = jnp.concatenate([part[:, cols_here - 2 :] for part in parts], axis=0)
    first = jnp.concatenate([part[:, :2] for part in parts], axis=0)
    left, right = shift(last, "gy", True), shift(first, "gy", False)
    places = jnp.arange(128, dtype=jnp.int32)[None, :] + 2
    cell_x = row_start - 2 + places // 16
    cell_y = col_start - 2 + places % 16
    inside = (cell_x >= 0) & (cell_x < total_x) & (cell_y >= 0) & (cell_y < total_y)
    mask = inside.astype(f32)

    if fast:
        mixed = local_call(
            mix_body,
            (devices, 8, 128),
            [pltpu.VMEM((32 * groups, 128), f32)]
            + [pltpu.VMEM((4, kept_x, groups, kept_y, MZ * C), f32)] * 2
            + [pltpu.SemaphoreType.DMA((4, 2))],
            on_chip(modes),
            *[
                jnp.transpose(spec, (0, 2, 1, 3)).reshape(kept_x, groups, 4, kept_y, MZ * C)
                for spec in (spec_real, spec_imag)
            ],
            keep=False,
            remote=(1, 2),
        )
    else:
        modes = modes[:owners].reshape(groups, thirds, kept_y, 2, kept_x, 4, 4)
        modes = jnp.transpose(modes, (3, 4, 2, 0, 5, 1, 6))
        modes = modes.reshape(2, kept_x, kept_y, C, MZ)
        weight_real = spec_real.reshape(kept_x, kept_y, C, MZ, C)
        weight_imag = spec_imag.reshape(kept_x, kept_y, C, MZ, C)

        def product(left, right):
            return jnp.einsum("abik,abiko->abok", left, right, precision=highest)

        mixed = jnp.stack(
            [
                product(modes[0], weight_real) - product(modes[1], weight_imag),
                product(modes[0], weight_imag) + product(modes[1], weight_real),
            ]
        ).reshape(2, kept_x, kept_y, groups, 4, thirds, 4)
        mixed = jnp.transpose(mixed, (3, 5, 2, 0, 1, 4, 6))
        mixed = mixed.reshape(owners, kept_y, 2 * kept_x * 16)
        mixed = jnp.pad(mixed, ((0, devices - owners), (0, 0), (0, 0)))
    mixed = trade(mixed)
    filters = [pltpu.VMEM((9 * BLOCK, DEPTH), f32)] + [pltpu.VMEM((9 * BLOCK, DEPTH), BF)] * 2
    hidden = local_call(
        first_conv_body,
        (ROWS + 2 * TOP, 128),
        [
            pltpu.VMEM((8, 16, C * Z), f32),
            pltpu.VMEM((ROWS, 128), f32),
            pltpu.VMEM((ROWS + 2 * TOP, 128), f32),
        ]
        + filters,
        state_field,
        top,
        bottom,
        left,
        right,
        conv_first,
        mask,
    )

    if fast:
        back = local_call(
            plane_body,
            (devices, 8, 128),
            [pltpu.VMEM((256, 128), f32)],
            on_chip(mixed),
            plane_table(line_table(inverse_x, count_x, rows_here, count_x, kept_x), inverse_y),
            keep=False,
        )
    else:
        parts = mixed.reshape(count_x, count_y, kept_y, 2, kept_x, 4, 4)
        back = transform(inverse_x, inverse_y, parts, (count_x, rows_here, count_y, cols_here))
        back = jnp.transpose(back, (1, 3, 4, 0, 2, 5, 6)).reshape(devices, 8, 128)
    back = trade(back)
    conv_out = local_call(
        second_conv_body,
        (rows_here, cols_here, C * Z),
        [pltpu.VMEM((ROWS, 128), f32)] + filters,
        on_chip(hidden),
        conv_second,
    )
    return local_call(
        inverse_z_body,
        (rows_here, cols_here, C * Z),
        [pltpu.VMEM((32 * groups, 128), f32)],
        on_chip(back),
        *halves(inverse_z),
        on_chip(conv_out),
        keep=False,
    )


def solution(mesh):
    in_specs = (P("gx", "gy", None), P(), P(), P("gx", "gy", None, None), P("gx", "gy", None, None))
    out_specs = P("gx", "gy", None)
    return jax.shard_map(on_device, mesh=mesh, in_specs=in_specs, out_specs=out_specs, check_vma=False)
```

time: 333 us -> 77.8 us (0.23); the launches traced: 327 us -> 77.3 us
  local copies, waits for them, and re-layouts: 162 us -> 2.07 us
  matrix products: 65.8 us -> 0 us
  blocking collectives: 25.8 us -> 0 us
  Pallas kernels: 0 us -> 25.4 us
  between operations: 15.8 us -> 0.21 us
  other arithmetic: 14.9 us -> 0.14 us
  starting transfers between devices: 21.5 us -> 25.3 us
    reshape x74 -> x0, local copies, waits for them, and re-layouts: 85.9 us -> none  [the longest x54 64.9 us: convolve(): summed = summed + matmul(block, window.reshape(C, rows_out * cols_out * Z))]
    slice x68 -> x3, local copies, waits for them, and re-layouts: 68.7 us -> 1.15 us  [on_device(): first = jnp.concatenate([part[:, :2] for part in parts], axis=0)]
    dot_general x74 -> x0, matrix products: 65.8 us -> none  [the longest x66 62.4 us: matmul(): return jnp.dot(left, right, precision=highest)]
    all_gather x2 -> x0, blocking collectives: 25.8 us -> none  [the longest x1 14.8 us: on_device(): shard_piece = lax.all_gather(mixed, 'gy', axis=0, tiled=True)]
    pallas_call x0 -> x7, Pallas kernels: none -> 25.4 us  [local_call(): pl.pallas_call(body, out_shape=[kind(shape, jnp.float32) for kind, shape...]
    all_to_all x0 -> x4, starting transfers between devices: none -> 17 us  [trade(): return lax.all_to_all(block, both, 0, 0, tiled=True)]
    all_to_all x0 -> x4, waiting for transfers between devices: none -> 16.8 us  [trade(): return lax.all_to_all(block, both, 0, 0, tiled=True)]
    reduce_scatter x1 -> x0, waiting for transfers between devices: 16.6 us -> none  [on_device(): lax.psum_scatter(jnp.concatenate([term_real, term_imag], axis=2), 'gy', s...]
  transfers between devices with their start and end apart: 10 -> 8, of which waited for: 3 -> 4; matrix products, arithmetic and copies ran while one was open for 65% -> 2% of each run, Pallas kernels for 0% -> 23%
where the time goes in v3:
time: 77.8 us; the launch traced here: 77.3 us
  Pallas kernels  25.4 us (33%)
  starting transfers between devices  25.3 us (33%)
  waiting for transfers between devices  24.2 us (31%)
  local copies, waits for them, and re-layouts  2.07 us (3%)
    pallas_call x7, Pallas kernels, local_call(): pl.pallas_call(body, out_shape=[kind(shape, jnp.float32) for kind, shape...  25.4 us
    all_to_all x4, starting transfers between devices, trade(): return lax.all_to_all(block, both, 0, 0, tiled=True)  17 us
    all_to_all x4, waiting for transfers between devices, trade(): return lax.all_to_all(block, both, 0, 0, tiled=True)  16.8 us
    ppermute x4, starting transfers between devices, shift(): lax.ppermute(block, axis, [(i, i + 1) if ahead else (i + 1, i) for i in s...  8.35 us
    ppermute x4, waiting for transfers between devices, shift(): lax.ppermute(block, axis, [(i, i + 1) if ahead else (i + 1, i) for i in s...  7.37 us
  transfers between devices with their start and end apart: 8, of which 4 were waited for; matrix products, arithmetic and copies ran while one was open for 2% of the time, Pallas kernels for 23%

profile of v3, /device:TPU:0, one launch (start us, length us, event | category | flops | bytes accessed | tf_op | source)
XLA Modules:
  0.0 77.3 jit_solution(16564675210979593613)
XLA Ops:
  0.0 2.1 %shard_map.100 = (f32[32,8,128]{2,1,0:T(8,128)}, f32[2,8,2304]{2,1,0:T(8,128)S(1)}, f32[2,8,2304]{2,1,0:T(8,128)S(1)}) custom-call(f32[4,8,2304]{2,1,0:T(8,128)} %cells_ref.1, bf16[2,256,128]{2,1,0:T(8,128)(2,1)} %constant.59.clone.waves_ref), custom_call_target="tpu_custom_call" | custom-call | tf_op jit(solution)/shard_map/pallas_call | solution.py:316
  2.1 7.3 %all-to-all-start = ((f32[32,8,128]{2,1,0:T(8,128)}), f32[32,8,128]{2,1,0:T(8,128)S(1)}, u32[]{:S(2)}, u32[]{:S(2)}) async-start(f32[32,8,128]{2,1,0:T(8,128)} %get-tuple-element.8), calls=%async_computation | async-start | bytes 262144 | tf_op jit(solution)/shard_map/all_to_all | solution.py:374
  9.5 2.2 %collective-permute-start = (f32[2,8,2304]{2,1,0:T(8,128)S(1)}, f32[2,8,2304]{2,1,0:T(8,128)S(1)}, u32[]{:S(2)}, u32[]{:S(2)}) collective-permute-start(f32[2,8,2304]{2,1,0:T(8,128)S(1)} %get-tuple-element.9), channel_id=1, source_target_pairs={{0,4},{4,8},{8,12},{12,16},{16,20},{20,24},{24,28},{1,5},{5,9},{9,... | collective-permute-start | bytes 442376 | tf_op jit(solution)/shard_map/ppermute | solution.py:378
  11.6 1.3 %collective-permute-start.1 = (f32[2,8,2304]{2,1,0:T(8,128)S(1)}, f32[2,8,2304]{2,1,0:T(8,128)S(1)}, u32[]{:S(2)}, u32[]{:S(2)}) collective-permute-start(f32[2,8,2304]{2,1,0:T(8,128)S(1)} %get-tuple-element.10), channel_id=1, source_target_pairs={{4,0},{8,4},{12,8},{16,12},{20,16},{24,20},{28,24},{5,1},{9,5},{13... | collective-permute-start | bytes 442376 | tf_op jit(solution)/shard_map/ppermute | solution.py:378
  12.9 1.1 %fusion.1 = (f32[4,2,2304]{2,1,0:T(2,128)S(1)}, f32[4,2,2304]{2,1,0:T(2,128)S(1)}) fusion(f32[4,8,2304]{2,1,0:T(8,128)} %cells_ref.1), kind=kLoop, calls=%fused_computation.9 | loop fusion | bytes 294912 | tf_op jit(solution)/shard_map/slice | solution.py:417
  14.1 3.8 %all-to-all-done.in_ref = f32[32,8,128]{2,1,0:T(8,128)S(1)} async-done(((f32[32,8,128]{2,1,0:T(8,128)}), f32[32,8,128]{2,1,0:T(8,128)S(1)}, u32[]{:S(2)}, u32[]{:S(2)}) %all-to-all-start) | async-done | bytes 131104 | tf_op jit(solution)/shard_map/all_to_all | solution.py:374
  17.8 0.9 %copy-done.4 = bf16[2,192,128]{2,1,0:T(8,128)(2,1)S(1)} copy-done((bf16[2,192,128]{2,1,0:T(8,128)(2,1)S(1)}, bf16[2,192,128]{2,1,0:T(8,128)(2,1)}, u32[]{:S(2)}) %copy-start.4) | copy-done | bytes 98328
  18.7 1.6 %shard_map.101 = f32[32,8,128]{2,1,0:T(8,128)} custom-call(f32[32,8,128]{2,1,0:T(8,128)S(1)} %all-to-all-done.in_ref, bf16[2,192,128]{2,1,0:T(8,128)(2,1)S(1)} %copy-done.4), custom_call_target="tpu_custom_call" | custom-call | tf_op jit(solution)/shard_map/pallas_call | solution.py:316
  20.4 4.2 %all-to-all-start.1 = ((f32[32,8,128]{2,1,0:T(8,128)}), f32[32,8,128]{2,1,0:T(8,128)S(1)}, u32[]{:S(2)}, u32[]{:S(2)}) async-start(f32[32,8,128]{2,1,0:T(8,128)} %shard_map.101), calls=%async_computation.1 | async-start | bytes 262144 | tf_op jit(solution)/shard_map/all_to_all | solution.py:374
  24.6 8.3 %all-to-all-done.1.in_ref = f32[32,8,128]{2,1,0:T(8,128)S(1)} async-done(((f32[32,8,128]{2,1,0:T(8,128)}), f32[32,8,128]{2,1,0:T(8,128)S(1)}, u32[]{:S(2)}, u32[]{:S(2)}) %all-to-all-start.1) | async-done | bytes 131104 | tf_op jit(solution)/shard_map/all_to_all | solution.py:374
  32.9 4.2 %shard_map.102 = f32[32,8,128]{2,1,0:T(8,128)} custom-call(f32[32,8,128]{2,1,0:T(8,128)S(1)} %all-to-all-done.1.in_ref, f32[4,9,4,8,432]{4,3,2,1,0:T(8,128)} %bitcast.6, f32[4,9,4,8,432]{4,3,2,1,0:T(8,128)} %bitcast.7), custom_call_target="tpu_custom_call" | custom-call | tf_op jit(solution)/shard_map/pallas_call | solution.py:316
  37.2 2.7 %all-to-all-start.2 = ((f32[32,8,128]{2,1,0:T(8,128)}), f32[32,8,128]{2,1,0:T(8,128)S(1)}, u32[]{:S(2)}, u32[]{:S(2)}) async-start(f32[32,8,128]{2,1,0:T(8,128)} %shard_map.102), calls=%async_computation.2 | async-start | bytes 262144 | tf_op jit(solution)/shard_map/all_to_all | solution.py:374
  39.9 0.1 pad_maximum_fusion
  40.0 3.6 %collective-permute-start.2 = (f32[8,2,2304]{2,1,0:T(2,128)S(1)}, f32[8,2,2304]{2,1,0:T(2,128)S(1)}, u32[]{:S(2)}, u32[]{:S(2)}) collective-permute-start(f32[8,2,2304]{2,1,0:T(2,128)S(1)} %pad_maximum_fusion), channel_id=1, source_target_pairs={{0,1},{1,2},{2,3},{4,5},{5,6},{6,7},{8,9},{9,10},{10,11},{12,13},{... | collective-permute-start | bytes 442376 | tf_op jit(solution)/shard_map/ppermute | solution.py:378
  43.6 4.7 %all-to-all-done.2.in_ref = f32[32,8,128]{2,1,0:T(8,128)S(1)} async-done(((f32[32,8,128]{2,1,0:T(8,128)}), f32[32,8,128]{2,1,0:T(8,128)S(1)}, u32[]{:S(2)}, u32[]{:S(2)}) %all-to-all-start.2) | async-done | bytes 131104 | tf_op jit(solution)/shard_map/all_to_all | solution.py:374
  48.3 1.6 %shard_map.103 = f32[32,8,128]{2,1,0:T(8,128)} custom-call(f32[32,8,128]{2,1,0:T(8,128)S(1)} %all-to-all-done.2.in_ref, bf16[2,192,128]{2,1,0:T(8,128)(2,1)S(1)} %copy-done.3), custom_call_target="tpu_custom_call" | custom-call | tf_op jit(solution)/shard_map/pallas_call | solution.py:316
  50.0 2.7 %all-to-all-start.3 = ((f32[32,8,128]{2,1,0:T(8,128)}), f32[32,8,128]{2,1,0:T(8,128)S(1)}, u32[]{:S(2)}, u32[]{:S(2)}) async-start(f32[32,8,128]{2,1,0:T(8,128)} %shard_map.103), calls=%async_computation.3 | async-start | bytes 262144 | tf_op jit(solution)/shard_map/all_to_all | solution.py:374
  52.7 0.1 pad_maximum_fusion.1
  52.7 1.3 %collective-permute-start.3 = (f32[8,2,2304]{2,1,0:T(2,128)S(1)}, f32[8,2,2304]{2,1,0:T(2,128)S(1)}, u32[]{:S(2)}, u32[]{:S(2)}) collective-permute-start(f32[8,2,2304]{2,1,0:T(2,128)S(1)} %pad_maximum_fusion.1), channel_id=1, source_target_pairs={{1,0},{2,1},{3,2},{5,4},{6,5},{7,6},{9,8},{10,9},{11,10},{13,12},{... | collective-permute-start | bytes 442376 | tf_op jit(solution)/shard_map/ppermute | solution.py:378
  54.1 7.4 %collective-permute-done.3.right_ref = f32[8,2,2304]{2,1,0:T(2,128)S(1)} collective-permute-done((f32[8,2,2304]{2,1,0:T(2,128)S(1)}, f32[8,2,2304]{2,1,0:T(2,128)S(1)}, u32[]{:S(2)}, u32[]{:S(2)}) %collective-permute-start.3) | collective-permute-done | bytes 147488 | tf_op jit(solution)/shard_map/ppermute | solution.py:378
  61.4 7.7 %shard_map.104.data_ref = f32[2384,128]{1,0:T(8,128)S(1)} custom-call(f32[4,8,2304]{2,1,0:T(8,128)S(1)} %copy-done, f32[2,8,2304]{2,1,0:T(8,128)S(1)} %collective-permute-done.top_ref, f32[2,8,2304]{2,1,0:T(8,128)S(1)} %collective-permute-done.1.bottom_ref, f32[8,2,2304]{2,1,0:T(2,128)S(1)} %collective-permute-done.2.left_ref, ...), custom_call_target="tpu_custom_call" | custom-call | tf_op jit(solution)/shard_map/pallas_call | solution.py:316
  69.2 6.9 %shard_map.105.conv_ref = f32[4,8,2304]{2,1,0:T(8,128)S(1)} custom-call(f32[2384,128]{1,0:T(8,128)S(1)} %shard_map.104.data_ref, f32[3,3,36,108]{3,2,1,0:T(8,128)S(1)} %copy-done.1), custom_call_target="tpu_custom_call" | custom-call | tf_op jit(solution)/shard_map/pallas_call | solution.py:316
  76.1 0.0 all-to-all-done.3.in_ref
  76.1 1.1 %shard_map.106 = f32[4,8,2304]{2,1,0:T(8,128)} custom-call(f32[32,8,128]{2,1,0:T(8,128)S(1)} %all-to-all-done.3.in_ref, bf16[128,256]{1,0:T(8,128)(2,1)S(1)} %copy-done.6, bf16[128,256]{1,0:T(8,128)(2,1)S(1)} %copy-done.5, f32[4,8,2304]{2,1,0:T(8,128)S(1)} %shard_map.105.conv_ref), custom_call_target="tpu_custom_call" | custom-call | tf_op jit(solution)/shard_map/pallas_call | solution.py:316
  (19 shorter events, 0.1 us)
Async XLA Ops:
  2.1 15.7 %all-to-all-start = ((f32[32,8,128]{2,1,0:T(8,128)}), f32[32,8,128]{2,1,0:T(8,128)S(1)}, u32[]{:S(2)}, u32[]{:S(2)}) async-start(f32[32,8,128]{2,1,0:T(8,128)} %get-tuple-element.8), calls=%async_computation | async-start | bytes 262144 | tf_op jit(solution)/shard_map/all_to_all | solution.py:374
  9.5 4.6 %collective-permute-start = (f32[2,8,2304]{2,1,0:T(8,128)S(1)}, f32[2,8,2304]{2,1,0:T(8,128)S(1)}, u32[]{:S(2)}, u32[]{:S(2)}) collective-permute-start(f32[2,8,2304]{2,1,0:T(8,128)S(1)} %get-tuple-element.9), channel_id=1, source_target_pairs={{0,4},{4,8},{8,12},{12,16},{16,20},{20,24},{24,28},{1,5},{5,9},{9,... | collective-permute-start | bytes 442376 | tf_op jit(solution)/shard_map/ppermute | solution.py:378
  11.6 12.9 %collective-permute-start.1 = (f32[2,8,2304]{2,1,0:T(8,128)S(1)}, f32[2,8,2304]{2,1,0:T(8,128)S(1)}, u32[]{:S(2)}, u32[]{:S(2)}) collective-permute-start(f32[2,8,2304]{2,1,0:T(8,128)S(1)} %get-tuple-element.10), channel_id=1, source_target_pairs={{4,0},{8,4},{12,8},{16,12},{20,16},{24,20},{28,24},{5,1},{9,5},{13... | collective-permute-start | bytes 442376 | tf_op jit(solution)/shard_map/ppermute | solution.py:378
  17.8 0.9 %copy-start.4 = (bf16[2,192,128]{2,1,0:T(8,128)(2,1)S(1)}, bf16[2,192,128]{2,1,0:T(8,128)(2,1)}, u32[]{:S(2)}) copy-start(bf16[2,192,128]{2,1,0:T(8,128)(2,1)} %constant.60.clone.table_ref) | copy-start | bytes 294916
  20.4 12.6 %all-to-all-start.1 = ((f32[32,8,128]{2,1,0:T(8,128)}), f32[32,8,128]{2,1,0:T(8,128)S(1)}, u32[]{:S(2)}, u32[]{:S(2)}) async-start(f32[32,8,128]{2,1,0:T(8,128)} %shard_map.101), calls=%async_computation.1 | async-start | bytes 262144 | tf_op jit(solution)/shard_map/all_to_all | solution.py:374
  32.9 15.4 %copy-start.3 = (bf16[2,192,128]{2,1,0:T(8,128)(2,1)S(1)}, bf16[2,192,128]{2,1,0:T(8,128)(2,1)}, u32[]{:S(2)}) copy-start(bf16[2,192,128]{2,1,0:T(8,128)(2,1)} %constant.61.clone.table_ref) | copy-start | bytes 294916
  32.9 28.5 %copy-start = (f32[4,8,2304]{2,1,0:T(8,128)S(1)}, f32[4,8,2304]{2,1,0:T(8,128)}, u32[]{:S(2)}) copy-start(f32[4,8,2304]{2,1,0:T(8,128)} %cells_ref.1) | copy-start | bytes 884740
  32.9 28.5 %copy-start.2 = (f32[3,3,36,108]{3,2,1,0:T(8,128)S(1)}, f32[3,3,36,108]{3,2,1,0:T(8,128)}, u32[]{:S(2)}) copy-start(f32[3,3,36,108]{3,2,1,0:T(8,128)} %filter_ref.2) | copy-start | bytes 419908
  37.2 32.0 %copy-start.1 = (f32[3,3,36,108]{3,2,1,0:T(8,128)S(1)}, f32[3,3,36,108]{3,2,1,0:T(8,128)}, u32[]{:S(2)}) copy-start(f32[3,3,36,108]{3,2,1,0:T(8,128)} %filter_ref.3) | copy-start | bytes 419908
  37.2 11.1 %all-to-all-start.2 = ((f32[32,8,128]{2,1,0:T(8,128)}), f32[32,8,128]{2,1,0:T(8,128)S(1)}, u32[]{:S(2)}, u32[]{:S(2)}) async-start(f32[32,8,128]{2,1,0:T(8,128)} %shard_map.102), calls=%async_computation.2 | async-start | bytes 262144 | tf_op jit(solution)/shard_map/all_to_all | solution.py:374
  40.0 14.1 %collective-permute-start.2 = (f32[8,2,2304]{2,1,0:T(2,128)S(1)}, f32[8,2,2304]{2,1,0:T(2,128)S(1)}, u32[]{:S(2)}, u32[]{:S(2)}) collective-permute-start(f32[8,2,2304]{2,1,0:T(2,128)S(1)} %pad_maximum_fusion), channel_id=1, source_target_pairs={{0,1},{1,2},{2,3},{4,5},{5,6},{6,7},{8,9},{9,10},{10,11},{12,13},{... | collective-permute-start | bytes 442376 | tf_op jit(solution)/shard_map/ppermute | solution.py:378
  50.0 26.2 %copy-start.5 = (bf16[128,256]{1,0:T(8,128)(2,1)S(1)}, bf16[128,256]{1,0:T(8,128)(2,1)}, u32[]{:S(2)}) copy-start(bf16[128,256]{1,0:T(8,128)(2,1)} %constant.63.clone.lo_ref) | copy-start | bytes 196612
  50.0 26.2 %copy-start.6 = (bf16[128,256]{1,0:T(8,128)(2,1)S(1)}, bf16[128,256]{1,0:T(8,128)(2,1)}, u32[]{:S(2)}) copy-start(bf16[128,256]{1,0:T(8,128)(2,1)} %constant.62.clone.hi_ref) | copy-start | bytes 196612
  50.0 26.2 %all-to-all-start.3 = ((f32[32,8,128]{2,1,0:T(8,128)}), f32[32,8,128]{2,1,0:T(8,128)S(1)}, u32[]{:S(2)}, u32[]{:S(2)}) async-start(f32[32,8,128]{2,1,0:T(8,128)} %shard_map.103), calls=%async_computation.3 | async-start | bytes 262144 | tf_op jit(solution)/shard_map/all_to_all | solution.py:374
  52.7 8.7 %collective-permute-start.3 = (f32[8,2,2304]{2,1,0:T(2,128)S(1)}, f32[8,2,2304]{2,1,0:T(2,128)S(1)}, u32[]{:S(2)}, u32[]{:S(2)}) collective-permute-start(f32[8,2,2304]{2,1,0:T(2,128)S(1)} %pad_maximum_fusion.1), channel_id=1, source_target_pairs={{1,0},{2,1},{3,2},{5,4},{6,5},{7,6},{9,8},{10,9},{11,10},{13,12},{... | collective-permute-start | bytes 442376 | tf_op jit(solution)/shard_map/ppermute | solution.py:378

commit v4 on v3

--- a/solution.py
+++ b/solution.py
@@ -72,15 +72,28 @@
     lax.fori_loop(0, Z // (2 * STEP), step, 0)
 
 
+def odd_row():
+    return (lax.axis_index("gx") & 1) == 1
+
+
 def first_conv_body(
-    cells_ref, top_ref, bottom_ref, left_ref, right_ref, filter_ref, mask_ref,
+    cells_ref, near_ref, far_ref, left_ref, right_ref, filter_ref, mask_ref,
     out_ref, frame_ref, turn_ref, data_ref, wide_ref, hi_ref, lo_ref,
 ):
     f32 = jnp.float32
     frame_ref[:, 8:16, :] = jnp.zeros((8, 8, C * Z), f32)
-    frame_ref[0:2, 0:8, :] = top_ref[...]
     frame_ref[2:6, 0:8, :] = cells_ref[...]
-    frame_ref[6:8, 0:8, :] = bottom_ref[...]
+
+    @pl.when(odd_row())
+    def _():
+        frame_ref[0:2, 0:8, :] = near_ref[...]
+        frame_ref[6:8, 0:8, :] = far_ref[...]
+
+    @pl.when(jnp.logical_not(odd_row()))
+    def _():
+        frame_ref[0:2, 0:8, :] = far_ref[...]
+        frame_ref[6:8, 0:8, :] = near_ref[...]
+
     for x in range(8):
         frame_ref[x, 8:10, :] = right_ref[x]
         frame_ref[(x + 7) % 8, 14:16, :] = left_ref[x]
@@ -172,7 +185,9 @@
     return tiles
 
 
-def forward_z_body(field_ref, waves_ref, out_ref, head_ref, tail_ref, cells_ref, table_ref, sems):
+def forward_z_body(
+    field_ref, waves_ref, out_ref, near_ref, far_ref, first_ref, last_ref, cells_ref, table_ref, sems
+):
     groups = C // 4
     copies = [
         pltpu.make_async_copy(field_ref, cells_ref, sems.at[0]),
@@ -183,8 +198,20 @@
     for copy in copies:
         copy.wait()
     rows = cells_ref.shape[0]
-    head_ref[...] = cells_ref[0:2]
-    tail_ref[...] = cells_ref[rows - 2 : rows]
+    cols = cells_ref.shape[1]
+    first_ref[...] = cells_ref[:, 0:2, :]
+    last_ref[...] = cells_ref[:, cols - 2 : cols, :]
+
+    @pl.when(odd_row())
+    def _():
+        near_ref[...] = cells_ref[0:2]
+        far_ref[...] = cells_ref[rows - 2 : rows]
+
+    @pl.when(jnp.logical_not(odd_row()))
+    def _():
+        near_ref[...] = cells_ref[rows - 2 : rows]
+        far_ref[...] = cells_ref[0:2]
+
     stacked = jnp.concatenate(
         [cells_ref[:, :, g * 256 : (g + 1) * 256].reshape(32, 256) for g in range(groups)], axis=0
     )
@@ -379,8 +406,8 @@
 
     fast = (count_x, count_y, kept_x, kept_y) == (8, 4, 4, 8)
 
-    edge = (2, cols_here, C * Z)
-    columns, head, tail = local_call(
+    edge, side = (2, cols_here, C * Z), (rows_here, 2, C * Z)
+    columns, near, far, first, last = local_call(
         forward_z_body,
         (devices, 8, 128),
         [
@@ -392,10 +419,12 @@
         np.stack(halves(forward_z)),
         keep=False,
         remote=(0, 1),
-        more=(edge, edge),
+        more=(edge, edge, side, side),
     )
     columns = trade(columns)
-    top, bottom = shift(tail, "gx", True), shift(head, "gx", False)
+    ends = range(1, count_x - 1)
+    near = lax.ppermute(near, "gx", [(i, i ^ 1) for i in range(count_x) if i ^ 1 < count_x])
+    far = lax.ppermute(far, "gx", [(i, (i + 1 ^ 1) - 1) for i in ends])
 
     if fast:
         modes = local_call(
@@ -412,9 +441,14 @@
         modes = jnp.transpose(modes, (1, 3, 4, 0, 2, 5, 6))
         modes = modes.reshape(devices, kept_y, 2 * kept_x * 16)
     modes = trade(modes)
-    parts = (top, state_field, bottom)
-    last = jnp.concatenate([part[:, cols_here - 2 :] for part in parts], axis=0)
-    first = jnp.concatenate([part[:, :2] for part in parts], axis=0)
+    odd = lax.axis_index("gx") % 2 == 1
+
+    def framed(middle, low):
+        pair = near[:, low : low + 2], far[:, low : low + 2]
+        top, bottom = jnp.where(odd, pair[0], pair[1]), jnp.where(odd, pair[1], pair[0])
+        return jnp.concatenate([top, middle, bottom], axis=0)
+
+    last, first = framed(last, cols_here - 2), framed(first, 0)
     left, right = shift(last, "gy", True), shift(first, "gy", False)
     places = jnp.arange(128, dtype=jnp.int32)[None, :] + 2
     cell_x = row_start - 2 + places // 16
@@ -468,8 +502,8 @@
         ]
         + filters,
         state_field,
-        top,
-        bottom,
+        near,
+        far,
         left,
         right,
         conv_first,

time: 77.8 us -> 76.2 us (0.979)
  starting transfers between devices: 25.3 us -> 21.2 us
  waiting for transfers between devices: 24.2 us -> 27.8 us
  local copies, waits for them, and re-layouts: 2.07 us -> 0.92 us
    all_to_all x4, waiting for transfers between devices: 16.8 us -> 20.4 us  [trade(): return lax.all_to_all(block, both, 0, 0, tiled=True)]
    ppermute x4 -> x2, starting transfers between devices: 8.35 us -> 4.89 us  [shift(): lax.ppermute(block, axis, [(i, i + 1) if ahead else (i + 1, i) for i in s...]
    all_to_all x4, starting transfers between devices: 17 us -> 15.3 us  [trade(): return lax.all_to_all(block, both, 0, 0, tiled=True)]
    slice x3 -> x0, local copies, waits for them, and re-layouts: 1.15 us -> none  [on_device(): first = jnp.concatenate([part[:, :2] for part in parts], axis=0)]
    ppermute x0 -> x2, starting transfers between devices: none -> 0.97 us  [the longest x1 0.66 us: on_device(): far = lax.ppermute(far, 'gx', [(i, (i + 1 ^ 1) - 1) for i in ends])]
    ppermute x4 -> x2, waiting for transfers between devices: 7.37 us -> 7.36 us  [shift(): lax.ppermute(block, axis, [(i, i + 1) if ahead else (i + 1, i) for i in s...]
  transfers between devices with their start and end apart: 8 -> 8, of which waited for: 4 -> 4; matrix products, arithmetic and copies ran while one was open for 2% -> 0% of each run, Pallas kernels for 23% -> 24%
where the time goes in v4:
time: 76.2 us; the launch traced here: 75.8 us
  waiting for transfers between devices  27.8 us (36%)
  Pallas kernels  25.5 us (33%)
  starting transfers between devices  21.2 us (28%)
  local copies, waits for them, and re-layouts  0.92 us (1%)
    pallas_call x7, Pallas kernels, local_call(): pl.pallas_call(body, out_shape=[kind(shape, jnp.float32) for kind, shape...  25.5 us
    all_to_all x4, waiting for transfers between devices, trade(): return lax.all_to_all(block, both, 0, 0, tiled=True)  20.4 us
    all_to_all x4, starting transfers between devices, trade(): return lax.all_to_all(block, both, 0, 0, tiled=True)  15.3 us
    ppermute x2, waiting for transfers between devices, shift(): lax.ppermute(block, axis, [(i, i + 1) if ahead else (i + 1, i) for i in s...  7.36 us
    ppermute x2, starting transfers between devices, shift(): lax.ppermute(block, axis, [(i, i + 1) if ahead else (i + 1, i) for i in s...  4.89 us
  transfers between devices with their start and end apart: 8, of which 4 were waited for; matrix products, arithmetic and copies ran while one was open for 0% of the time, Pallas kernels for 24%

profile of v4, /device:TPU:0, one launch (start us, length us, event | category | flops | bytes accessed | tf_op | source)
XLA Modules:
  0.0 75.8 jit_solution(3995933315284995589)
XLA Ops:
  0.0 2.1 %shard_map.100 = (f32[32,8,128]{2,1,0:T(8,128)}, f32[2,8,2304]{2,1,0:T(8,128)S(1)}, f32[2,8,2304]{2,1,0:T(8,128)S(1)}, f32[4,2,2304]{2,1,0:T(2,128)S(1)}, f32[4,2,2304]{2,1,0:T(2,128)S(1)}) custom-call(f32[4,8,2304]{2,1,0:T(8,128)} %cells_ref.1, bf16[2,256,128]{2,1,0:T(8,128)(2,1)} %constant.69.clone.waves_ref), custom_call_target="tpu_custom_call" | custom-call | tf_op jit(solution)/shard_map/pallas_call | solution.py:343
  2.1 7.3 %all-to-all-start = ((f32[32,8,128]{2,1,0:T(8,128)}), f32[32,8,128]{2,1,0:T(8,128)S(1)}, u32[]{:S(2)}, u32[]{:S(2)}) async-start(f32[32,8,128]{2,1,0:T(8,128)} %get-tuple-element.10), calls=%async_computation | async-start | bytes 262144 | tf_op jit(solution)/shard_map/all_to_all | solution.py:401
  9.5 0.3 collective-permute-start
  9.8 0.7 collective-permute-start.1
  10.5 7.4 %all-to-all-done.in_ref = f32[32,8,128]{2,1,0:T(8,128)S(1)} async-done(((f32[32,8,128]{2,1,0:T(8,128)}), f32[32,8,128]{2,1,0:T(8,128)S(1)}, u32[]{:S(2)}, u32[]{:S(2)}) %all-to-all-start) | async-done | bytes 131104 | tf_op jit(solution)/shard_map/all_to_all | solution.py:401
  17.9 0.9 %copy-done.4 = bf16[2,192,128]{2,1,0:T(8,128)(2,1)S(1)} copy-done((bf16[2,192,128]{2,1,0:T(8,128)(2,1)S(1)}, bf16[2,192,128]{2,1,0:T(8,128)(2,1)}, u32[]{:S(2)}) %copy-start.4) | copy-done | bytes 98328
  18.8 1.6 %shard_map.101 = f32[32,8,128]{2,1,0:T(8,128)} custom-call(f32[32,8,128]{2,1,0:T(8,128)S(1)} %all-to-all-done.in_ref, bf16[2,192,128]{2,1,0:T(8,128)(2,1)S(1)} %copy-done.4), custom_call_target="tpu_custom_call" | custom-call | tf_op jit(solution)/shard_map/pallas_call | solution.py:343
  20.4 2.6 %all-to-all-start.1 = ((f32[32,8,128]{2,1,0:T(8,128)}), f32[32,8,128]{2,1,0:T(8,128)S(1)}, u32[]{:S(2)}, u32[]{:S(2)}) async-start(f32[32,8,128]{2,1,0:T(8,128)} %shard_map.101), calls=%async_computation.1 | async-start | bytes 262144 | tf_op jit(solution)/shard_map/all_to_all | solution.py:401
  23.0 8.3 %all-to-all-done.1.in_ref = f32[32,8,128]{2,1,0:T(8,128)S(1)} async-done(((f32[32,8,128]{2,1,0:T(8,128)}), f32[32,8,128]{2,1,0:T(8,128)S(1)}, u32[]{:S(2)}, u32[]{:S(2)}) %all-to-all-start.1) | async-done | bytes 131104 | tf_op jit(solution)/shard_map/all_to_all | solution.py:401
  31.4 4.2 %shard_map.102 = f32[32,8,128]{2,1,0:T(8,128)} custom-call(f32[32,8,128]{2,1,0:T(8,128)S(1)} %all-to-all-done.1.in_ref, f32[4,9,4,8,432]{4,3,2,1,0:T(8,128)} %bitcast.6, f32[4,9,4,8,432]{4,3,2,1,0:T(8,128)} %bitcast.7), custom_call_target="tpu_custom_call" | custom-call | tf_op jit(solution)/shard_map/pallas_call | solution.py:343
  35.6 0.0 copy-start.1
  35.6 2.7 %all-to-all-start.2 = ((f32[32,8,128]{2,1,0:T(8,128)}), f32[32,8,128]{2,1,0:T(8,128)S(1)}, u32[]{:S(2)}, u32[]{:S(2)}) async-start(f32[32,8,128]{2,1,0:T(8,128)} %shard_map.102), calls=%async_computation.2 | async-start | bytes 262144 | tf_op jit(solution)/shard_map/all_to_all | solution.py:401
  38.3 0.1 pad_maximum_fusion
  38.4 3.6 %collective-permute-start.2 = (f32[8,2,2304]{2,1,0:T(2,128)S(1)}, f32[8,2,2304]{2,1,0:T(2,128)S(1)}, u32[]{:S(2)}, u32[]{:S(2)}) collective-permute-start(f32[8,2,2304]{2,1,0:T(2,128)S(1)} %pad_maximum_fusion), channel_id=1, source_target_pairs={{0,1},{1,2},{2,3},{4,5},{5,6},{6,7},{8,9},{9,10},{10,11},{12,13},{... | collective-permute-start | bytes 442376 | tf_op jit(solution)/shard_map/ppermute | solution.py:405
  42.0 4.7 %all-to-all-done.2.in_ref = f32[32,8,128]{2,1,0:T(8,128)S(1)} async-done(((f32[32,8,128]{2,1,0:T(8,128)}), f32[32,8,128]{2,1,0:T(8,128)S(1)}, u32[]{:S(2)}, u32[]{:S(2)}) %all-to-all-start.2) | async-done | bytes 131104 | tf_op jit(solution)/shard_map/all_to_all | solution.py:401
  46.7 1.6 %shard_map.103 = f32[32,8,128]{2,1,0:T(8,128)} custom-call(f32[32,8,128]{2,1,0:T(8,128)S(1)} %all-to-all-done.2.in_ref, bf16[2,192,128]{2,1,0:T(8,128)(2,1)S(1)} %copy-done.3), custom_call_target="tpu_custom_call" | custom-call | tf_op jit(solution)/shard_map/pallas_call | solution.py:343
  48.4 2.7 %all-to-all-start.3 = ((f32[32,8,128]{2,1,0:T(8,128)}), f32[32,8,128]{2,1,0:T(8,128)S(1)}, u32[]{:S(2)}, u32[]{:S(2)}) async-start(f32[32,8,128]{2,1,0:T(8,128)} %shard_map.103), calls=%async_computation.3 | async-start | bytes 262144 | tf_op jit(solution)/shard_map/all_to_all | solution.py:401
  51.1 0.1 pad_maximum_fusion.1
  51.2 1.3 %collective-permute-start.3 = (f32[8,2,2304]{2,1,0:T(2,128)S(1)}, f32[8,2,2304]{2,1,0:T(2,128)S(1)}, u32[]{:S(2)}, u32[]{:S(2)}) collective-permute-start(f32[8,2,2304]{2,1,0:T(2,128)S(1)} %pad_maximum_fusion.1), channel_id=1, source_target_pairs={{1,0},{2,1},{3,2},{5,4},{6,5},{7,6},{9,8},{10,9},{11,10},{13,12},{... | collective-permute-start | bytes 442376 | tf_op jit(solution)/shard_map/ppermute | solution.py:405
  52.5 7.4 %collective-permute-done.3.right_ref = f32[8,2,2304]{2,1,0:T(2,128)S(1)} collective-permute-done((f32[8,2,2304]{2,1,0:T(2,128)S(1)}, f32[8,2,2304]{2,1,0:T(2,128)S(1)}, u32[]{:S(2)}, u32[]{:S(2)}) %collective-permute-start.3) | collective-permute-done | bytes 147488 | tf_op jit(solution)/shard_map/ppermute | solution.py:405
  59.9 7.8 %shard_map.104.data_ref = f32[2384,128]{1,0:T(8,128)S(1)} custom-call(f32[4,8,2304]{2,1,0:T(8,128)S(1)} %copy-done, f32[2,8,2304]{2,1,0:T(8,128)S(1)} %collective-permute-done.near_ref, f32[2,8,2304]{2,1,0:T(8,128)S(1)} %collective-permute-done.1.far_ref, f32[8,2,2304]{2,1,0:T(2,128)S(1)} %collective-permute-done.2.left_ref, ...), custom_call_target="tpu_custom_call" | custom-call | tf_op jit(solution)/shard_map/pallas_call | solution.py:343
  67.7 6.9 %shard_map.105.conv_ref = f32[4,8,2304]{2,1,0:T(8,128)S(1)} custom-call(f32[2384,128]{1,0:T(8,128)S(1)} %shard_map.104.data_ref, f32[3,3,36,108]{3,2,1,0:T(8,128)S(1)} %copy-done.1), custom_call_target="tpu_custom_call" | custom-call | tf_op jit(solution)/shard_map/pallas_call | solution.py:343
  74.6 0.0 all-to-all-done.3.in_ref
  74.6 1.1 %shard_map.106 = f32[4,8,2304]{2,1,0:T(8,128)} custom-call(f32[32,8,128]{2,1,0:T(8,128)S(1)} %all-to-all-done.3.in_ref, bf16[128,256]{1,0:T(8,128)(2,1)S(1)} %copy-done.6, bf16[128,256]{1,0:T(8,128)(2,1)S(1)} %copy-done.5, f32[4,8,2304]{2,1,0:T(8,128)S(1)} %shard_map.105.conv_ref), custom_call_target="tpu_custom_call" | custom-call | tf_op jit(solution)/shard_map/pallas_call | solution.py:343
  (17 shorter events, 0.1 us)
Async XLA Ops:
  2.1 15.7 %all-to-all-start = ((f32[32,8,128]{2,1,0:T(8,128)}), f32[32,8,128]{2,1,0:T(8,128)S(1)}, u32[]{:S(2)}, u32[]{:S(2)}) async-start(f32[32,8,128]{2,1,0:T(8,128)} %get-tuple-element.10), calls=%async_computation | async-start | bytes 262144 | tf_op jit(solution)/shard_map/all_to_all | solution.py:401
  9.5 13.5 %collective-permute-start = (f32[2,8,2304]{2,1,0:T(8,128)S(1)}, f32[2,8,2304]{2,1,0:T(8,128)S(1)}, u32[]{:S(2)}, u32[]{:S(2)}) collective-permute-start(f32[2,8,2304]{2,1,0:T(8,128)S(1)} %get-tuple-element.11), channel_id=1, source_target_pairs={{0,4},{4,0},{8,12},{12,8},{16,20},{20,16},{24,28},{28,24},{1,5},{5... | collective-permute-start | bytes 442376 | tf_op jit(solution)/shard_map/ppermute | solution.py:426
  9.8 13.2 %collective-permute-start.1 = (f32[2,8,2304]{2,1,0:T(8,128)S(1)}, f32[2,8,2304]{2,1,0:T(8,128)S(1)}, u32[]{:S(2)}, u32[]{:S(2)}) collective-permute-start(f32[2,8,2304]{2,1,0:T(8,128)S(1)} %get-tuple-element.12), channel_id=1, source_target_pairs={{4,8},{8,4},{12,16},{16,12},{20,24},{24,20},{5,9},{9,5},{13,17},{1... | collective-permute-start | bytes 442376 | tf_op jit(solution)/shard_map/ppermute | solution.py:427
  17.9 0.9 %copy-start.4 = (bf16[2,192,128]{2,1,0:T(8,128)(2,1)S(1)}, bf16[2,192,128]{2,1,0:T(8,128)(2,1)}, u32[]{:S(2)}) copy-start(bf16[2,192,128]{2,1,0:T(8,128)(2,1)} %constant.70.clone.table_ref) | copy-start | bytes 294916
  20.4 11.0 %all-to-all-start.1 = ((f32[32,8,128]{2,1,0:T(8,128)}), f32[32,8,128]{2,1,0:T(8,128)S(1)}, u32[]{:S(2)}, u32[]{:S(2)}) async-start(f32[32,8,128]{2,1,0:T(8,128)} %shard_map.101), calls=%async_computation.1 | async-start | bytes 262144 | tf_op jit(solution)/shard_map/all_to_all | solution.py:401
  31.3 15.4 %copy-start.3 = (bf16[2,192,128]{2,1,0:T(8,128)(2,1)S(1)}, bf16[2,192,128]{2,1,0:T(8,128)(2,1)}, u32[]{:S(2)}) copy-start(bf16[2,192,128]{2,1,0:T(8,128)(2,1)} %constant.71.clone.table_ref) | copy-start | bytes 294916
  31.3 28.5 %copy-start = (f32[4,8,2304]{2,1,0:T(8,128)S(1)}, f32[4,8,2304]{2,1,0:T(8,128)}, u32[]{:S(2)}) copy-start(f32[4,8,2304]{2,1,0:T(8,128)} %cells_ref.1) | copy-start | bytes 884740
  31.3 28.5 %copy-start.2 = (f32[3,3,36,108]{3,2,1,0:T(8,128)S(1)}, f32[3,3,36,108]{3,2,1,0:T(8,128)}, u32[]{:S(2)}) copy-start(f32[3,3,36,108]{3,2,1,0:T(8,128)} %filter_ref.2) | copy-start | bytes 419908
  35.6 32.0 %copy-start.1 = (f32[3,3,36,108]{3,2,1,0:T(8,128)S(1)}, f32[3,3,36,108]{3,2,1,0:T(8,128)}, u32[]{:S(2)}) copy-start(f32[3,3,36,108]{3,2,1,0:T(8,128)} %filter_ref.3) | copy-start | bytes 419908
  35.6 11.1 %all-to-all-start.2 = ((f32[32,8,128]{2,1,0:T(8,128)}), f32[32,8,128]{2,1,0:T(8,128)S(1)}, u32[]{:S(2)}, u32[]{:S(2)}) async-start(f32[32,8,128]{2,1,0:T(8,128)} %shard_map.102), calls=%async_computation.2 | async-start | bytes 262144 | tf_op jit(solution)/shard_map/all_to_all | solution.py:401
  38.4 14.1 %collective-permute-start.2 = (f32[8,2,2304]{2,1,0:T(2,128)S(1)}, f32[8,2,2304]{2,1,0:T(2,128)S(1)}, u32[]{:S(2)}, u32[]{:S(2)}) collective-permute-start(f32[8,2,2304]{2,1,0:T(2,128)S(1)} %pad_maximum_fusion), channel_id=1, source_target_pairs={{0,1},{1,2},{2,3},{4,5},{5,6},{6,7},{8,9},{9,10},{10,11},{12,13},{... | collective-permute-start | bytes 442376 | tf_op jit(solution)/shard_map/ppermute | solution.py:405
  48.4 26.2 %copy-start.5 = (bf16[128,256]{1,0:T(8,128)(2,1)S(1)}, bf16[128,256]{1,0:T(8,128)(2,1)}, u32[]{:S(2)}) copy-start(bf16[128,256]{1,0:T(8,128)(2,1)} %constant.73.clone.lo_ref) | copy-start | bytes 196612
  48.4 26.2 %copy-start.6 = (bf16[128,256]{1,0:T(8,128)(2,1)S(1)}, bf16[128,256]{1,0:T(8,128)(2,1)}, u32[]{:S(2)}) copy-start(bf16[128,256]{1,0:T(8,128)(2,1)} %constant.72.clone.hi_ref) | copy-start | bytes 196612
  48.4 26.2 %all-to-all-start.3 = ((f32[32,8,128]{2,1,0:T(8,128)}), f32[32,8,128]{2,1,0:T(8,128)S(1)}, u32[]{:S(2)}, u32[]{:S(2)}) async-start(f32[32,8,128]{2,1,0:T(8,128)} %shard_map.103), calls=%async_computation.3 | async-start | bytes 262144 | tf_op jit(solution)/shard_map/all_to_all | solution.py:401
  51.2 8.7 %collective-permute-start.3 = (f32[8,2,2304]{2,1,0:T(2,128)S(1)}, f32[8,2,2304]{2,1,0:T(2,128)S(1)}, u32[]{:S(2)}, u32[]{:S(2)}) collective-permute-start(f32[8,2,2304]{2,1,0:T(2,128)S(1)} %pad_maximum_fusion.1), channel_id=1, source_target_pairs={{1,0},{2,1},{3,2},{5,4},{6,5},{7,6},{9,8},{10,9},{11,10},{13,12},{... | collective-permute-start | bytes 442376 | tf_op jit(solution)/shard_map/ppermute | solution.py:405

commit v5 on v4

--- a/solution.py
+++ b/solution.py
@@ -30,6 +30,8 @@
 DEPTH = 224
 ROWS = Z * C
 BLOCK = STEP * C
+LATE = 1
+EARLY = ROWS - LATE * 2 * BLOCK
 
 
 def load_filters(filter_ref, wide_ref, hi_ref, lo_ref):
@@ -43,7 +45,7 @@
     hi_ref[...], lo_ref[...] = split(wide_ref[...])
 
 
-def convolve(data_ref, hi_ref, lo_ref, store):
+def convolve(data_ref, hi_ref, lo_ref, store, pairs):
     f32 = jnp.float32
 
     def step(g, carry):
@@ -69,7 +71,7 @@
             store(pl.multiple_of(at + h * BLOCK, 8), total[h])
         return carry
 
-    lax.fori_loop(0, Z // (2 * STEP), step, 0)
+    lax.fori_loop(0, pairs, step, 0)
 
 
 def odd_row():
@@ -78,7 +80,7 @@
 
 def first_conv_body(
     cells_ref, near_ref, far_ref, left_ref, right_ref, filter_ref, mask_ref,
-    out_ref, frame_ref, turn_ref, data_ref, wide_ref, hi_ref, lo_ref,
+    out_ref, tail_ref, frame_ref, turn_ref, data_ref, wide_ref, hi_ref, lo_ref,
 ):
     f32 = jnp.float32
     frame_ref[:, 8:16, :] = jnp.zeros((8, 8, C * Z), f32)
@@ -110,24 +112,85 @@
     def store(at, total):
         turn_ref[pl.ds(at, BLOCK), :] = gelu(total) * mask
 
-    convolve(data_ref, hi_ref, lo_ref, store)
+    tail_ref[...] = data_ref[EARLY:, :]
+    convolve(data_ref, hi_ref, lo_ref, store, EARLY // (2 * BLOCK))
     out_ref[0:TOP, :] = jnp.zeros((TOP, 128), f32)
-    out_ref[TOP + ROWS :, :] = jnp.zeros((TOP, 128), f32)
-    out_ref[TOP : TOP + ROWS, :] = turn_ref[...]
-
-
-def second_conv_body(data_ref, filter_ref, out_ref, turn_ref, wide_ref, hi_ref, lo_ref):
+    out_ref[TOP:, :] = turn_ref[0:EARLY, :]
+
+
+HALF = ROWS // 2
+PACKED = HALF + 2 * TOP
+
+
+def second_conv_body(
+    data_ref, tail_ref, mask_ref, first_ref, filter_ref, out_ref,
+    pack_hi_ref, pack_lo_ref, turn_ref, merge_ref, late_ref, wide_ref, hi_ref, lo_ref,
+):
+    f32 = jnp.float32
+    mask = mask_ref[0:1, :]
+
+    def store(at, total):
+        late_ref[pl.ds(at, BLOCK), :] = gelu(total) * mask
+
+    load_filters(first_ref, wide_ref, hi_ref, lo_ref)
+    convolve(tail_ref, hi_ref, lo_ref, store, LATE)
     load_filters(filter_ref, wide_ref, hi_ref, lo_ref)
-
-    def store(at, total):
-        turn_ref[pl.ds(at, BLOCK), :] = total
-
-    convolve(data_ref, hi_ref, lo_ref, store)
-    for j in range(C * Z // 128):
-        pieces = [turn_ref[pl.ds(2 * j + e, Z, stride=C), :] for e in range(2)]
+    source = lax.broadcasted_iota(jnp.int32, (256, 128), 0)
+    target = lax.broadcasted_iota(jnp.int32, (1, 128), 1)
+    place = target & 63
+    line = jnp.floor((place.astype(f32) + 0.5) * 0.1).astype(jnp.int32)
+    wanted = (target >= 64).astype(jnp.int32) * 128 + 16 * (line + 1) + place - 10 * line - 1
+    wanted = jnp.where(place < 60, wanted, -1)
+    select = jnp.where(source == wanted, 1.0, 0.0).astype(BF)
+    upper = [data_ref[HALF : TOP + EARLY, :], late_ref[...], jnp.zeros((TOP, 128), f32)]
+    whole = jnp.concatenate([data_ref[0:PACKED, :], jnp.concatenate(upper, axis=0)], axis=1)
+    for part, held_ref in zip(split(whole), (pack_hi_ref, pack_lo_ref)):
+        held_ref[...] = jnp.dot(part, select, preferred_element_type=f32).astype(BF)
+
+    def step(g, carry):
+        at = pl.multiple_of(g * BLOCK, 16)
+        later = pl.multiple_of(at + HALF // 2, 16)
+        data_hi, data_lo = [
+            jnp.concatenate([held[pl.ds(at, DEPTH), :], held[pl.ds(later, DEPTH), :]], axis=1)
+            for held in (pack_hi_ref, pack_lo_ref)
+        ]
+        total = None
+        for s in range(9):
+            hi = hi_ref[s * BLOCK : (s + 1) * BLOCK, :]
+            lo = lo_ref[s * BLOCK : (s + 1) * BLOCK, :]
+            part = jnp.dot(hi, data_hi, preferred_element_type=f32) + (
+                jnp.dot(lo, data_hi, preferred_element_type=f32)
+                + jnp.dot(hi, data_lo, preferred_element_type=f32)
+            )
+            sides = [part[:, :128], part[:, 128:]]
+            shift = (s // 3 - 1) * 10 + s % 3 - 1
+            if shift:
+                sides = [pltpu.roll(side, -shift % 128, 1) for side in sides]
+            total = sides if total is None else [u + v for u, v in zip(total, sides)]
+        turn_ref[pl.ds(at, BLOCK), :] = total[0]
+        turn_ref[pl.ds(later, BLOCK), :] = total[1]
+        return carry
+
+    lax.fori_loop(0, Z // (4 * STEP), step, 0)
+    quarter = lax.broadcasted_iota(jnp.int32, (64, 128), 1) >> 5
+    for four in range(C // 4):
+        pieces = [turn_ref[pl.ds(4 * four + e, Z // 2, stride=C), :] for e in range(4)]
         turned = jnp.concatenate(pieces, axis=0).T
-        for x in range(4):
-            out_ref[x, :, j * 128 : (j + 1) * 128] = turned[16 * x + 32 : 16 * x + 40, :]
+        early, late = turned[:64], turned[64:]
+        for pair in range(2):
+            turns = ((0, 32, 32, 64), (64, 96, 96, 0))[pair]
+            parts = [
+                pltpu.roll(side, turn, 1) if turn else side
+                for side, turn in zip((early, late, early, late), turns)
+            ]
+            merge_ref[pair] = jnp.where(
+                quarter < 2,
+                jnp.where(quarter < 1, parts[0], parts[1]),
+                jnp.where(quarter < 3, parts[2], parts[3]),
+            )
+            at = (2 * four + pair) * 128
+            for x in range(4):
+                out_ref[x, :, at : at + 128] = merge_ref[pair, 10 * x + 11 : 10 * x + 19, :]
 
 
 def dft_wave(freqs, length, sign):
@@ -186,15 +249,18 @@
 
 
 def forward_z_body(
-    field_ref, waves_ref, out_ref, near_ref, far_ref, first_ref, last_ref, cells_ref, table_ref, sems
+    field_ref, waves_ref, lines_ref, out_ref, near_ref, far_ref, first_ref, last_ref, held_ref,
+    cells_ref, table_ref, sems,
 ):
     groups = C // 4
     copies = [
         pltpu.make_async_copy(field_ref, cells_ref, sems.at[0]),
         pltpu.make_async_copy(waves_ref, table_ref, sems.at[1]),
     ]
+    later = pltpu.make_async_copy(lines_ref, held_ref, sems.at[2])
     for copy in copies:
         copy.start()
+    later.start()
     for copy in copies:
         copy.wait()
     rows = cells_ref.shape[0]
@@ -223,6 +289,7 @@
             out_ref[group * 3 + part] = tiles[part]
     for spare in range(3 * groups, out_ref.shape[0]):
         out_ref[spare] = jnp.zeros((8, 128), jnp.float32)
+    later.wait()
 
 
 def plane_body(in_ref, table_ref, out_ref, rows_ref):
@@ -257,12 +324,12 @@
     return jnp.floor((place.astype(jnp.float32) + 0.5) * (1.0 / C)).astype(jnp.int32)
 
 
-def mix_body(in_ref, real_hbm, imag_hbm, out_ref, left_ref, real_ref, imag_ref, sems):
+def mix_body(in_ref, real_hbm, imag_hbm, out_ref, left_ref, real_ref, imag_ref, sides_ref, sems):
     f32 = jnp.float32
     groups = C // 4
     copies = [
         [
-            pltpu.make_async_copy(source.at[:, :, k], held.at[k], sems.at[k, e])
+            pltpu.make_async_copy(source.at[k], held.at[k], sems.at[k, e])
             for e, (source, held) in enumerate(((real_hbm, real_ref), (imag_hbm, imag_ref)))
         ]
         for k in range(4)
@@ -271,9 +338,10 @@
         for copy in pair:
             copy.start()
     width = MZ * C
-    lane = lax.broadcasted_iota(jnp.int32, (256, width), 0) & 127
+    lane = lax.broadcasted_iota(jnp.int32, (128, width), 0)
     mode = mode_of(lax.broadcasted_iota(jnp.int32, (1, width), 1))
-    wanted = lane - ((mode >> 2) * 16 + (mode & 3))
+    table = jnp.where(lane == (mode >> 2) * 16 + (mode & 3), 1.0, 0.0).astype(BF)
+    table = jnp.concatenate([table, table], axis=0)
     place = lax.broadcasted_iota(jnp.int32, (width, 1), 0)
     mode = mode_of(place)
     channel = place - mode * C
@@ -286,24 +354,25 @@
         for m in range(4):
             at = (m * groups + group) * 8
             left_ref[at : at + 8, :] = tiles[m]
-    hi, lo = split(left_ref[...])
-    left = jnp.concatenate([hi, lo], axis=1)
+    left = left_ref[...]
     real = [jnp.zeros((8, MZ * C), f32) for _ in range(4)]
     imag = [jnp.zeros((8, MZ * C), f32) for _ in range(4)]
     for k in range(4):
-        sides = []
         for e in range(2):
-            table = jnp.where(wanted == e * 64 + k * 4, 1.0, 0.0).astype(BF)
-            sides.append(jnp.dot(left, table, preferred_element_type=f32))
-        for copy in copies[k]:
+            turn = -(e * 64 + k * 4) % 128
+            hi, lo = split(pltpu.roll(left, turn, 1) if turn else left)
+            turned = jnp.concatenate([hi, lo], axis=1)
+            sides_ref[2 * k + e] = jnp.dot(turned, table, preferred_element_type=f32)
+    for m in range(4):
+        for copy in copies[m]:
             copy.wait()
-        for m in range(4):
+        for k in range(4):
             for group in range(groups):
                 at = (m * groups + group) * 8
-                re = sides[0][at : at + 8]
-                im = sides[1][at : at + 8]
-                wr = real_ref[k, m, group]
-                wi = imag_ref[k, m, group]
+                re = sides_ref[2 * k, at : at + 8, :]
+                im = sides_ref[2 * k + 1, at : at + 8, :]
+                wr = real_ref[m, group * 4 + k]
+                wi = imag_ref[m, group * 4 + k]
                 real[m] = real[m] + (re * wr - im * wi)
                 imag[m] = imag[m] + (re * wi + im * wr)
     hi, lo = split(jnp.concatenate(real + imag, axis=0))
@@ -336,13 +405,13 @@
 
 
 def local_call(body, out_shape, scratch, *operands, keep=True, remote=(), more=()):
-    shapes = [out_shape, *more]
+    shapes = [jax.ShapeDtypeStruct(getattr(at, "shape", at), getattr(at, "dtype", jnp.float32)) for at in (out_shape, *more)]
     kinds = [pltpu.VMEM if keep else jax.ShapeDtypeStruct] + [pltpu.VMEM] * len(more)
     inside = pl.BlockSpec(memory_space=pltpu.VMEM)
     outside = pl.BlockSpec(memory_space=pltpu.HBM)
     results = pl.pallas_call(
         body,
-        out_shape=[kind(shape, jnp.float32) for kind, shape in zip(kinds, shapes)],
+        out_shape=[kind(at.shape, at.dtype) for kind, at in zip(kinds, shapes)],
         in_specs=[outside if at in remote else inside for at in range(len(operands))],
         out_specs=[inside] * len(shapes),
         scratch_shapes=scratch,
@@ -407,19 +476,21 @@
     fast = (count_x, count_y, kept_x, kept_y) == (8, 4, 4, 8)
 
     edge, side = (2, cols_here, C * Z), (rows_here, 2, C * Z)
-    columns, near, far, first, last = local_call(
+    lines = plane_table(line_table(forward_x, count_x, kept_x, count_x, rows_here), forward_y)
+    columns, near, far, first, last, lines = local_call(
         forward_z_body,
         (devices, 8, 128),
         [
             pltpu.VMEM((rows_here, cols_here, C * Z), f32),
             pltpu.VMEM((2, 4 * Z, 128), BF),
-            pltpu.SemaphoreType.DMA((2,)),
+            pltpu.SemaphoreType.DMA((3,)),
         ],
         state_field,
         np.stack(halves(forward_z)),
+        lines,
         keep=False,
-        remote=(0, 1),
-        more=(edge, edge, side, side),
+        remote=(0, 1, 2),
+        more=(edge, edge, side, side, lines),
     )
     columns = trade(columns)
     ends = range(1, count_x - 1)
@@ -432,7 +503,7 @@
             (devices, 8, 128),
             [pltpu.VMEM((256, 128), f32)],
             on_chip(columns),
-            plane_table(line_table(forward_x, count_x, kept_x, count_x, rows_here), forward_y),
+            on_chip(lines),
             keep=False,
         )
     else:
@@ -461,11 +532,12 @@
             mix_body,
             (devices, 8, 128),
             [pltpu.VMEM((32 * groups, 128), f32)]
-            + [pltpu.VMEM((4, kept_x, groups, kept_y, MZ * C), f32)] * 2
+            + [pltpu.VMEM((kept_x, C, kept_y, MZ * C), f32)] * 2
+            + [pltpu.VMEM((8, 32 * groups, MZ * C), f32)]
             + [pltpu.SemaphoreType.DMA((4, 2))],
             on_chip(modes),
             *[
-                jnp.transpose(spec, (0, 2, 1, 3)).reshape(kept_x, groups, 4, kept_y, MZ * C)
+                jnp.transpose(spec, (0, 2, 1, 3))
                 for spec in (spec_real, spec_imag)
             ],
             keep=False,
@@ -492,9 +564,9 @@
         mixed = jnp.pad(mixed, ((0, devices - owners), (0, 0), (0, 0)))
     mixed = trade(mixed)
     filters = [pltpu.VMEM((9 * BLOCK, DEPTH), f32)] + [pltpu.VMEM((9 * BLOCK, DEPTH), BF)] * 2
-    hidden = local_call(
+    hidden, rest = local_call(
         first_conv_body,
-        (ROWS + 2 * TOP, 128),
+        (TOP + EARLY, 128),
         [
             pltpu.VMEM((8, 16, C * Z), f32),
             pltpu.VMEM((ROWS, 128), f32),
@@ -508,6 +580,7 @@
         right,
         conv_first,
         mask,
+        more=((ROWS + 2 * TOP - EARLY, 128),),
     )
 
     if fast:
@@ -527,8 +600,18 @@
     conv_out = local_call(
         second_conv_body,
         (rows_here, cols_here, C * Z),
-        [pltpu.VMEM((ROWS, 128), f32)] + filters,
+        [
+            pltpu.VMEM((PACKED, 128), BF),
+            pltpu.VMEM((PACKED, 128), BF),
+            pltpu.VMEM((HALF, 128), f32),
+            pltpu.VMEM((2, 64, 128), f32),
+            pltpu.VMEM((ROWS - EARLY, 128), f32),
+        ]
+        + filters,
         on_chip(hidden),
+        on_chip(rest),
+        mask,
+        conv_first,
         conv_second,
     )
     return local_call(

time: 76.2 us -> 72.9 us (0.957)
  Pallas kernels: 25.5 us -> 23.2 us
  local copies, waits for them, and re-layouts: 0.92 us -> 0.03 us
    pallas_call x7, Pallas kernels: 25.5 us -> 23.2 us  [local_call(): pl.pallas_call(body, out_shape=[kind(at.shape, at.dtype) for kind, at in...]
    unnamed x14 -> x12, local copies, waits for them, and re-layouts: 0.92 us -> 0.03 us
  transfers between devices with their start and end apart: 8 -> 8, of which waited for: 4 -> 4; matrix products, arithmetic and copies ran while one was open for 0% -> 0% of each run, Pallas kernels for 24% -> 22%
where the time goes in v5:
time: 72.9 us; the launch traced here: 72.5 us
  waiting for transfers between devices  27.8 us (38%)
  Pallas kernels  23.2 us (32%)
  starting transfers between devices  21.1 us (29%)
    pallas_call x7, Pallas kernels, local_call(): pl.pallas_call(body, out_shape=[kind(at.shape, at.dtype) for kind, at in...  23.2 us
    all_to_all x4, waiting for transfers between devices, trade(): return lax.all_to_all(block, both, 0, 0, tiled=True)  20.4 us
    all_to_all x4, starting transfers between devices, trade(): return lax.all_to_all(block, both, 0, 0, tiled=True)  15.2 us
    ppermute x2, waiting for transfers between devices, shift(): lax.ppermute(block, axis, [(i, i + 1) if ahead else (i + 1, i) for i in s...  7.36 us
    ppermute x2, starting transfers between devices, shift(): lax.ppermute(block, axis, [(i, i + 1) if ahead else (i + 1, i) for i in s...  4.89 us
  transfers between devices with their start and end apart: 8, of which 4 were waited for; matrix products, arithmetic and copies ran while one was open for 0% of the time, Pallas kernels for 22%

profile of v5, /device:TPU:0, one launch (start us, length us, event | category | flops | bytes accessed | tf_op | source)
XLA Modules:
  0.0 72.5 jit_solution(7229406131647151989)
XLA Ops:
  0.0 2.1 %shard_map.100 = (f32[32,8,128]{2,1,0:T(8,128)}, f32[2,8,2304]{2,1,0:T(8,128)S(1)}, f32[2,8,2304]{2,1,0:T(8,128)S(1)}, f32[4,2,2304]{2,1,0:T(2,128)S(1)}, f32[4,...) custom-call(f32[4,8,2304]{2,1,0:T(8,128)} %cells_ref.1, bf16[2,256,128]{2,1,0:T(8,128)(2,1)} %constant.69.clone.waves_ref, ...), custom_call_target="tpu_custom_call" | custom-call | tf_op jit(solution)/shard_map/pallas_call | solution.py:412
  2.2 7.3 %all-to-all-start = ((f32[32,8,128]{2,1,0:T(8,128)}), f32[32,8,128]{2,1,0:T(8,128)S(1)}, u32[]{:S(2)}, u32[]{:S(2)}) async-start(f32[32,8,128]{2,1,0:T(8,128)} %get-tuple-element.13), calls=%async_computation | async-start | bytes 262144 | tf_op jit(solution)/shard_map/all_to_all | solution.py:470
  9.5 0.3 collective-permute-start
  9.8 0.7 collective-permute-start.1
  10.5 7.4 %all-to-all-done.in_ref = f32[32,8,128]{2,1,0:T(8,128)S(1)} async-done(((f32[32,8,128]{2,1,0:T(8,128)}), f32[32,8,128]{2,1,0:T(8,128)S(1)}, u32[]{:S(2)}, u32[]{:S(2)}) %all-to-all-start) | async-done | bytes 131104 | tf_op jit(solution)/shard_map/all_to_all | solution.py:470
  17.9 1.6 %shard_map.101 = f32[32,8,128]{2,1,0:T(8,128)} custom-call(f32[32,8,128]{2,1,0:T(8,128)S(1)} %all-to-all-done.in_ref, bf16[2,192,128]{2,1,0:T(8,128)(2,1)S(1)} %get-tuple-element.14.table_ref), custom_call_target="tpu_custom_call" | custom-call | tf_op jit(solution)/shard_map/pallas_call | solution.py:412
  19.5 2.6 %all-to-all-start.1 = ((f32[32,8,128]{2,1,0:T(8,128)}), f32[32,8,128]{2,1,0:T(8,128)S(1)}, u32[]{:S(2)}, u32[]{:S(2)}) async-start(f32[32,8,128]{2,1,0:T(8,128)} %shard_map.101), calls=%async_computation.1 | async-start | bytes 262144 | tf_op jit(solution)/shard_map/all_to_all | solution.py:470
  22.2 8.3 %all-to-all-done.1.in_ref = f32[32,8,128]{2,1,0:T(8,128)S(1)} async-done(((f32[32,8,128]{2,1,0:T(8,128)}), f32[32,8,128]{2,1,0:T(8,128)S(1)}, u32[]{:S(2)}, u32[]{:S(2)}) %all-to-all-start.1) | async-done | bytes 131104 | tf_op jit(solution)/shard_map/all_to_all | solution.py:470
  30.5 4.2 %shard_map.102 = f32[32,8,128]{2,1,0:T(8,128)} custom-call(f32[32,8,128]{2,1,0:T(8,128)S(1)} %all-to-all-done.1.in_ref, f32[4,36,8,432]{3,2,1,0:T(8,128)} %bitcast.2, f32[4,36,8,432]{3,2,1,0:T(8,128)} %bitcast.3), custom_call_target="tpu_custom_call" | custom-call | tf_op jit(solution)/shard_map/pallas_call | solution.py:412
  34.7 0.0 copy-start.2
  34.7 0.0 copy-start.4
  34.7 0.0 copy-start.5
  34.8 2.7 %all-to-all-start.2 = ((f32[32,8,128]{2,1,0:T(8,128)}), f32[32,8,128]{2,1,0:T(8,128)S(1)}, u32[]{:S(2)}, u32[]{:S(2)}) async-start(f32[32,8,128]{2,1,0:T(8,128)} %shard_map.102), calls=%async_computation.2 | async-start | bytes 262144 | tf_op jit(solution)/shard_map/all_to_all | solution.py:470
  37.5 0.1 pad_maximum_fusion
  37.6 3.6 %collective-permute-start.2 = (f32[8,2,2304]{2,1,0:T(2,128)S(1)}, f32[8,2,2304]{2,1,0:T(2,128)S(1)}, u32[]{:S(2)}, u32[]{:S(2)}) collective-permute-start(f32[8,2,2304]{2,1,0:T(2,128)S(1)} %pad_maximum_fusion), channel_id=1, source_target_pairs={{0,1},{1,2},{2,3},{4,5},{5,6},{6,7},{8,9},{9,10},{10,11},{12,13},{... | collective-permute-start | bytes 442376 | tf_op jit(solution)/shard_map/ppermute | solution.py:474
  41.2 4.7 %all-to-all-done.2.in_ref = f32[32,8,128]{2,1,0:T(8,128)S(1)} async-done(((f32[32,8,128]{2,1,0:T(8,128)}), f32[32,8,128]{2,1,0:T(8,128)S(1)}, u32[]{:S(2)}, u32[]{:S(2)}) %all-to-all-start.2) | async-done | bytes 131104 | tf_op jit(solution)/shard_map/all_to_all | solution.py:470
  45.9 1.6 %shard_map.103 = f32[32,8,128]{2,1,0:T(8,128)} custom-call(f32[32,8,128]{2,1,0:T(8,128)S(1)} %all-to-all-done.2.in_ref, bf16[2,192,128]{2,1,0:T(8,128)(2,1)S(1)} %copy-done.3), custom_call_target="tpu_custom_call" | custom-call | tf_op jit(solution)/shard_map/pallas_call | solution.py:412
  47.5 2.6 %all-to-all-start.3 = ((f32[32,8,128]{2,1,0:T(8,128)}), f32[32,8,128]{2,1,0:T(8,128)S(1)}, u32[]{:S(2)}, u32[]{:S(2)}) async-start(f32[32,8,128]{2,1,0:T(8,128)} %shard_map.103), calls=%async_computation.3 | async-start | bytes 262144 | tf_op jit(solution)/shard_map/all_to_all | solution.py:470
  50.1 0.1 pad_maximum_fusion.1
  50.1 1.3 %collective-permute-start.3 = (f32[8,2,2304]{2,1,0:T(2,128)S(1)}, f32[8,2,2304]{2,1,0:T(2,128)S(1)}, u32[]{:S(2)}, u32[]{:S(2)}) collective-permute-start(f32[8,2,2304]{2,1,0:T(2,128)S(1)} %pad_maximum_fusion.1), channel_id=1, source_target_pairs={{1,0},{2,1},{3,2},{5,4},{6,5},{7,6},{9,8},{10,9},{11,10},{13,12},{... | collective-permute-start | bytes 442376 | tf_op jit(solution)/shard_map/ppermute | solution.py:474
  51.5 7.4 %collective-permute-done.3.right_ref = f32[8,2,2304]{2,1,0:T(2,128)S(1)} collective-permute-done((f32[8,2,2304]{2,1,0:T(2,128)S(1)}, f32[8,2,2304]{2,1,0:T(2,128)S(1)}, u32[]{:S(2)}, u32[]{:S(2)}) %collective-permute-start.3) | collective-permute-done | bytes 147488 | tf_op jit(solution)/shard_map/ppermute | solution.py:474
  58.8 7.0 %shard_map.104 = (f32[2056,128]{1,0:T(8,128)S(1)}, f32[368,128]{1,0:T(8,128)S(1)}) custom-call(f32[4,8,2304]{2,1,0:T(8,128)S(1)} %copy-done, f32[2,8,2304]{2,1,0:T(8,128)S(1)} %collective-permute-done.near_ref, f32[2,8,2304]{2,1,0:T(8,128)S(1)} %collective-permute-done.1.far_ref, f32[8,2,2304]{2,1,0:T(2,128)S(1)} %collective-permute-done.2.left_ref, ...), custom_call_target="tpu_custom_call" | custom-call | tf_op jit(solution)/shard_map/pallas_call | solution.py:412
  65.9 5.4 %shard_map.105.conv_ref = f32[4,8,2304]{2,1,0:T(8,128)S(1)} custom-call(f32[2056,128]{1,0:T(8,128)S(1)} %get-tuple-element.19.data_ref, f32[368,128]{1,0:T(8,128)S(1)} %get-tuple-element.20.tail_ref, f32[1,128]{1,0:T(1,128)S(1)} %and_convert_fusion.mask_ref, f32[3,3,36,108]{3,2,1,0:T(8,128)S(1)} %copy-done.1, f32[3,3,36,108]{3,2,1,0:T(8,128)S(1)} %copy-done.2), custom_call_target="tpu_custom_call" | custom-call | tf_op jit(solution)/shard_map/pallas_call | solution.py:412
  71.3 1.1 %shard_map.106 = f32[4,8,2304]{2,1,0:T(8,128)} custom-call(f32[32,8,128]{2,1,0:T(8,128)S(1)} %all-to-all-done.3.in_ref, bf16[128,256]{1,0:T(8,128)(2,1)S(1)} %copy-done.5, bf16[128,256]{1,0:T(8,128)(2,1)S(1)} %copy-done.4, f32[4,8,2304]{2,1,0:T(8,128)S(1)} %shard_map.105.conv_ref), custom_call_target="tpu_custom_call" | custom-call | tf_op jit(solution)/shard_map/pallas_call | solution.py:412
  (15 shorter events, 0.1 us)
Async XLA Ops:
  2.2 15.7 %all-to-all-start = ((f32[32,8,128]{2,1,0:T(8,128)}), f32[32,8,128]{2,1,0:T(8,128)S(1)}, u32[]{:S(2)}, u32[]{:S(2)}) async-start(f32[32,8,128]{2,1,0:T(8,128)} %get-tuple-element.13), calls=%async_computation | async-start | bytes 262144 | tf_op jit(solution)/shard_map/all_to_all | solution.py:470
  9.5 12.6 %collective-permute-start = (f32[2,8,2304]{2,1,0:T(8,128)S(1)}, f32[2,8,2304]{2,1,0:T(8,128)S(1)}, u32[]{:S(2)}, u32[]{:S(2)}) collective-permute-start(f32[2,8,2304]{2,1,0:T(8,128)S(1)} %get-tuple-element.15), channel_id=1, source_target_pairs={{0,4},{4,0},{8,12},{12,8},{16,20},{20,16},{24,28},{28,24},{1,5},{5... | collective-permute-start | bytes 442376 | tf_op jit(solution)/shard_map/ppermute | solution.py:497
  9.8 12.3 %collective-permute-start.1 = (f32[2,8,2304]{2,1,0:T(8,128)S(1)}, f32[2,8,2304]{2,1,0:T(8,128)S(1)}, u32[]{:S(2)}, u32[]{:S(2)}) collective-permute-start(f32[2,8,2304]{2,1,0:T(8,128)S(1)} %get-tuple-element.16), channel_id=1, source_target_pairs={{4,8},{8,4},{12,16},{16,12},{20,24},{24,20},{5,9},{9,5},{13,17},{1... | collective-permute-start | bytes 442376 | tf_op jit(solution)/shard_map/ppermute | solution.py:498
  19.5 11.0 %all-to-all-start.1 = ((f32[32,8,128]{2,1,0:T(8,128)}), f32[32,8,128]{2,1,0:T(8,128)S(1)}, u32[]{:S(2)}, u32[]{:S(2)}) async-start(f32[32,8,128]{2,1,0:T(8,128)} %shard_map.101), calls=%async_computation.1 | async-start | bytes 262144 | tf_op jit(solution)/shard_map/all_to_all | solution.py:470
  30.5 15.4 %copy-start.3 = (bf16[2,192,128]{2,1,0:T(8,128)(2,1)S(1)}, bf16[2,192,128]{2,1,0:T(8,128)(2,1)}, u32[]{:S(2)}) copy-start(bf16[2,192,128]{2,1,0:T(8,128)(2,1)} %constant.71.clone.table_ref) | copy-start | bytes 294916
  30.5 28.4 %copy-start = (f32[4,8,2304]{2,1,0:T(8,128)S(1)}, f32[4,8,2304]{2,1,0:T(8,128)}, u32[]{:S(2)}) copy-start(f32[4,8,2304]{2,1,0:T(8,128)} %cells_ref.1) | copy-start | bytes 884740
  30.5 28.4 %copy-start.1 = (f32[3,3,36,108]{3,2,1,0:T(8,128)S(1)}, f32[3,3,36,108]{3,2,1,0:T(8,128)}, u32[]{:S(2)}) copy-start(f32[3,3,36,108]{3,2,1,0:T(8,128)} %first_ref.1) | copy-start | bytes 419908
  34.7 31.2 %copy-start.2 = (f32[3,3,36,108]{3,2,1,0:T(8,128)S(1)}, f32[3,3,36,108]{3,2,1,0:T(8,128)}, u32[]{:S(2)}) copy-start(f32[3,3,36,108]{3,2,1,0:T(8,128)} %filter_ref.3) | copy-start | bytes 419908
  34.7 36.6 %copy-start.4 = (bf16[128,256]{1,0:T(8,128)(2,1)S(1)}, bf16[128,256]{1,0:T(8,128)(2,1)}, u32[]{:S(2)}) copy-start(bf16[128,256]{1,0:T(8,128)(2,1)} %constant.73.clone.lo_ref) | copy-start | bytes 196612
  34.7 36.6 %copy-start.5 = (bf16[128,256]{1,0:T(8,128)(2,1)S(1)}, bf16[128,256]{1,0:T(8,128)(2,1)}, u32[]{:S(2)}) copy-start(bf16[128,256]{1,0:T(8,128)(2,1)} %constant.72.clone.hi_ref) | copy-start | bytes 196612
  34.8 11.1 %all-to-all-start.2 = ((f32[32,8,128]{2,1,0:T(8,128)}), f32[32,8,128]{2,1,0:T(8,128)S(1)}, u32[]{:S(2)}, u32[]{:S(2)}) async-start(f32[32,8,128]{2,1,0:T(8,128)} %shard_map.102), calls=%async_computation.2 | async-start | bytes 262144 | tf_op jit(solution)/shard_map/all_to_all | solution.py:470
  37.6 13.9 %collective-permute-start.2 = (f32[8,2,2304]{2,1,0:T(2,128)S(1)}, f32[8,2,2304]{2,1,0:T(2,128)S(1)}, u32[]{:S(2)}, u32[]{:S(2)}) collective-permute-start(f32[8,2,2304]{2,1,0:T(2,128)S(1)} %pad_maximum_fusion), channel_id=1, source_target_pairs={{0,1},{1,2},{2,3},{4,5},{5,6},{6,7},{8,9},{9,10},{10,11},{12,13},{... | collective-permute-start | bytes 442376 | tf_op jit(solution)/shard_map/ppermute | solution.py:474
  47.5 23.8 %all-to-all-start.3 = ((f32[32,8,128]{2,1,0:T(8,128)}), f32[32,8,128]{2,1,0:T(8,128)S(1)}, u32[]{:S(2)}, u32[]{:S(2)}) async-start(f32[32,8,128]{2,1,0:T(8,128)} %shard_map.103), calls=%async_computation.3 | async-start | bytes 262144 | tf_op jit(solution)/shard_map/all_to_all | solution.py:470
  50.1 8.7 %collective-permute-start.3 = (f32[8,2,2304]{2,1,0:T(2,128)S(1)}, f32[8,2,2304]{2,1,0:T(2,128)S(1)}, u32[]{:S(2)}, u32[]{:S(2)}) collective-permute-start(f32[8,2,2304]{2,1,0:T(2,128)S(1)} %pad_maximum_fusion.1), channel_id=1, source_target_pairs={{1,0},{2,1},{3,2},{5,4},{6,5},{7,6},{9,8},{10,9},{11,10},{13,12},{... | collective-permute-start | bytes 442376 | tf_op jit(solution)/shard_map/ppermute | solution.py:474

commit v6 on v5

--- a/solution.py
+++ b/solution.py
@@ -30,7 +30,7 @@
 DEPTH = 224
 ROWS = Z * C
 BLOCK = STEP * C
-LATE = 1
+LATE = 2
 EARLY = ROWS - LATE * 2 * BLOCK
 
 
@@ -71,7 +71,7 @@
             store(pl.multiple_of(at + h * BLOCK, 8), total[h])
         return carry
 
-    lax.fori_loop(0, pairs, step, 0)
+    lax.fori_loop(0, pairs, step, 0, unroll=2)
 
 
 def odd_row():
@@ -171,7 +171,7 @@
         turn_ref[pl.ds(later, BLOCK), :] = total[1]
         return carry
 
-    lax.fori_loop(0, Z // (4 * STEP), step, 0)
+    lax.fori_loop(0, Z // (4 * STEP), step, 0, unroll=2)
     quarter = lax.broadcasted_iota(jnp.int32, (64, 128), 1) >> 5
     for four in range(C // 4):
         pieces = [turn_ref[pl.ds(4 * four + e, Z // 2, stride=C), :] for e in range(4)]

time: 72.9 us -> 71.3 us (0.978)
  Pallas kernels: 23.2 us -> 21.7 us
    pallas_call x7, Pallas kernels: 23.2 us -> 21.7 us  [local_call(): pl.pallas_call(body, out_shape=[kind(at.shape, at.dtype) for kind, at in...]
  transfers between devices with their start and end apart: 8 -> 8, of which waited for: 4 -> 4; matrix products, arithmetic and copies ran while one was open for 0% -> 0% of each run, Pallas kernels for 22% -> 20%
where the time goes in v6:
time: 71.3 us; the launch traced here: 70.9 us
  waiting for transfers between devices  27.8 us (39%)
  Pallas kernels  21.7 us (30%)
  starting transfers between devices  21.1 us (30%)
    pallas_call x7, Pallas kernels, local_call(): pl.pallas_call(body, out_shape=[kind(at.shape, at.dtype) for kind, at in...  21.7 us
    all_to_all x4, waiting for transfers between devices, trade(): return lax.all_to_all(block, both, 0, 0, tiled=True)  20.4 us
    all_to_all x4, starting transfers between devices, trade(): return lax.all_to_all(block, both, 0, 0, tiled=True)  15.2 us
    ppermute x2, waiting for transfers between devices, shift(): lax.ppermute(block, axis, [(i, i + 1) if ahead else (i + 1, i) for i in s...  7.36 us
    ppermute x2, starting transfers between devices, shift(): lax.ppermute(block, axis, [(i, i + 1) if ahead else (i + 1, i) for i in s...  4.89 us
  transfers between devices with their start and end apart: 8, of which 4 were waited for; matrix products, arithmetic and copies ran while one was open for 0% of the time, Pallas kernels for 20%

profile of v6, /device:TPU:0, one launch (start us, length us, event | category | flops | bytes accessed | tf_op | source)
XLA Modules:
  0.0 70.9 jit_solution(7283203902356244657)
XLA Ops:
  0.0 2.1 %shard_map.100 = (f32[32,8,128]{2,1,0:T(8,128)}, f32[2,8,2304]{2,1,0:T(8,128)S(1)}, f32[2,8,2304]{2,1,0:T(8,128)S(1)}, f32[4,2,2304]{2,1,0:T(2,128)S(1)}, f32[4,...) custom-call(f32[4,8,2304]{2,1,0:T(8,128)} %cells_ref.1, bf16[2,256,128]{2,1,0:T(8,128)(2,1)} %constant.69.clone.waves_ref, ...), custom_call_target="tpu_custom_call" | custom-call | tf_op jit(solution)/shard_map/pallas_call | solution.py:412
  2.2 7.3 %all-to-all-start = ((f32[32,8,128]{2,1,0:T(8,128)}), f32[32,8,128]{2,1,0:T(8,128)S(1)}, u32[]{:S(2)}, u32[]{:S(2)}) async-start(f32[32,8,128]{2,1,0:T(8,128)} %get-tuple-element.13), calls=%async_computation | async-start | bytes 262144 | tf_op jit(solution)/shard_map/all_to_all | solution.py:470
  9.5 0.3 collective-permute-start
  9.8 0.7 collective-permute-start.1
  10.5 7.4 %all-to-all-done.in_ref = f32[32,8,128]{2,1,0:T(8,128)S(1)} async-done(((f32[32,8,128]{2,1,0:T(8,128)}), f32[32,8,128]{2,1,0:T(8,128)S(1)}, u32[]{:S(2)}, u32[]{:S(2)}) %all-to-all-start) | async-done | bytes 131104 | tf_op jit(solution)/shard_map/all_to_all | solution.py:470
  17.9 1.6 %shard_map.101 = f32[32,8,128]{2,1,0:T(8,128)} custom-call(f32[32,8,128]{2,1,0:T(8,128)S(1)} %all-to-all-done.in_ref, bf16[2,192,128]{2,1,0:T(8,128)(2,1)S(1)} %get-tuple-element.14.table_ref), custom_call_target="tpu_custom_call" | custom-call | tf_op jit(solution)/shard_map/pallas_call | solution.py:412
  19.5 2.6 %all-to-all-start.1 = ((f32[32,8,128]{2,1,0:T(8,128)}), f32[32,8,128]{2,1,0:T(8,128)S(1)}, u32[]{:S(2)}, u32[]{:S(2)}) async-start(f32[32,8,128]{2,1,0:T(8,128)} %shard_map.101), calls=%async_computation.1 | async-start | bytes 262144 | tf_op jit(solution)/shard_map/all_to_all | solution.py:470
  22.2 8.3 %all-to-all-done.1.in_ref = f32[32,8,128]{2,1,0:T(8,128)S(1)} async-done(((f32[32,8,128]{2,1,0:T(8,128)}), f32[32,8,128]{2,1,0:T(8,128)S(1)}, u32[]{:S(2)}, u32[]{:S(2)}) %all-to-all-start.1) | async-done | bytes 131104 | tf_op jit(solution)/shard_map/all_to_all | solution.py:470
  30.5 4.2 %shard_map.102 = f32[32,8,128]{2,1,0:T(8,128)} custom-call(f32[32,8,128]{2,1,0:T(8,128)S(1)} %all-to-all-done.1.in_ref, f32[4,36,8,432]{3,2,1,0:T(8,128)} %bitcast.2, f32[4,36,8,432]{3,2,1,0:T(8,128)} %bitcast.3), custom_call_target="tpu_custom_call" | custom-call | tf_op jit(solution)/shard_map/pallas_call | solution.py:412
  34.7 0.0 copy-start.2
  34.7 0.0 copy-start.4
  34.7 0.0 copy-start.5
  34.8 2.7 %all-to-all-start.2 = ((f32[32,8,128]{2,1,0:T(8,128)}), f32[32,8,128]{2,1,0:T(8,128)S(1)}, u32[]{:S(2)}, u32[]{:S(2)}) async-start(f32[32,8,128]{2,1,0:T(8,128)} %shard_map.102), calls=%async_computation.2 | async-start | bytes 262144 | tf_op jit(solution)/shard_map/all_to_all | solution.py:470
  37.5 0.1 pad_maximum_fusion
  37.6 3.6 %collective-permute-start.2 = (f32[8,2,2304]{2,1,0:T(2,128)S(1)}, f32[8,2,2304]{2,1,0:T(2,128)S(1)}, u32[]{:S(2)}, u32[]{:S(2)}) collective-permute-start(f32[8,2,2304]{2,1,0:T(2,128)S(1)} %pad_maximum_fusion), channel_id=1, source_target_pairs={{0,1},{1,2},{2,3},{4,5},{5,6},{6,7},{8,9},{9,10},{10,11},{12,13},{... | collective-permute-start | bytes 442376 | tf_op jit(solution)/shard_map/ppermute | solution.py:474
  41.2 4.7 %all-to-all-done.2.in_ref = f32[32,8,128]{2,1,0:T(8,128)S(1)} async-done(((f32[32,8,128]{2,1,0:T(8,128)}), f32[32,8,128]{2,1,0:T(8,128)S(1)}, u32[]{:S(2)}, u32[]{:S(2)}) %all-to-all-start.2) | async-done | bytes 131104 | tf_op jit(solution)/shard_map/all_to_all | solution.py:470
  45.9 1.6 %shard_map.103 = f32[32,8,128]{2,1,0:T(8,128)} custom-call(f32[32,8,128]{2,1,0:T(8,128)S(1)} %all-to-all-done.2.in_ref, bf16[2,192,128]{2,1,0:T(8,128)(2,1)S(1)} %copy-done.3), custom_call_target="tpu_custom_call" | custom-call | tf_op jit(solution)/shard_map/pallas_call | solution.py:412
  47.5 2.6 %all-to-all-start.3 = ((f32[32,8,128]{2,1,0:T(8,128)}), f32[32,8,128]{2,1,0:T(8,128)S(1)}, u32[]{:S(2)}, u32[]{:S(2)}) async-start(f32[32,8,128]{2,1,0:T(8,128)} %shard_map.103), calls=%async_computation.3 | async-start | bytes 262144 | tf_op jit(solution)/shard_map/all_to_all | solution.py:470
  50.1 0.1 pad_maximum_fusion.1
  50.1 1.3 %collective-permute-start.3 = (f32[8,2,2304]{2,1,0:T(2,128)S(1)}, f32[8,2,2304]{2,1,0:T(2,128)S(1)}, u32[]{:S(2)}, u32[]{:S(2)}) collective-permute-start(f32[8,2,2304]{2,1,0:T(2,128)S(1)} %pad_maximum_fusion.1), channel_id=1, source_target_pairs={{1,0},{2,1},{3,2},{5,4},{6,5},{7,6},{9,8},{10,9},{11,10},{13,12},{... | collective-permute-start | bytes 442376 | tf_op jit(solution)/shard_map/ppermute | solution.py:474
  51.5 7.4 %collective-permute-done.3.right_ref = f32[8,2,2304]{2,1,0:T(2,128)S(1)} collective-permute-done((f32[8,2,2304]{2,1,0:T(2,128)S(1)}, f32[8,2,2304]{2,1,0:T(2,128)S(1)}, u32[]{:S(2)}, u32[]{:S(2)}) %collective-permute-start.3) | collective-permute-done | bytes 147488 | tf_op jit(solution)/shard_map/ppermute | solution.py:474
  58.8 5.5 %shard_map.104 = (f32[1768,128]{1,0:T(8,128)S(1)}, f32[656,128]{1,0:T(8,128)S(1)}) custom-call(f32[4,8,2304]{2,1,0:T(8,128)S(1)} %copy-done, f32[2,8,2304]{2,1,0:T(8,128)S(1)} %collective-permute-done.near_ref, f32[2,8,2304]{2,1,0:T(8,128)S(1)} %collective-permute-done.1.far_ref, f32[8,2,2304]{2,1,0:T(2,128)S(1)} %collective-permute-done.2.left_ref, ...), custom_call_target="tpu_custom_call" | custom-call | tf_op jit(solution)/shard_map/pallas_call | solution.py:412
  64.4 5.4 %shard_map.105.conv_ref = f32[4,8,2304]{2,1,0:T(8,128)S(1)} custom-call(f32[1768,128]{1,0:T(8,128)S(1)} %get-tuple-element.19.data_ref, f32[656,128]{1,0:T(8,128)S(1)} %get-tuple-element.20.tail_ref, f32[1,128]{1,0:T(1,128)S(1)} %and_convert_fusion.mask_ref, f32[3,3,36,108]{3,2,1,0:T(8,128)S(1)} %copy-done.1, f32[3,3,36,108]{3,2,1,0:T(8,128)S(1)} %copy-done.2), custom_call_target="tpu_custom_call" | custom-call | tf_op jit(solution)/shard_map/pallas_call | solution.py:412
  69.8 1.1 %shard_map.106 = f32[4,8,2304]{2,1,0:T(8,128)} custom-call(f32[32,8,128]{2,1,0:T(8,128)S(1)} %all-to-all-done.3.in_ref, bf16[128,256]{1,0:T(8,128)(2,1)S(1)} %copy-done.5, bf16[128,256]{1,0:T(8,128)(2,1)S(1)} %copy-done.4, f32[4,8,2304]{2,1,0:T(8,128)S(1)} %shard_map.105.conv_ref), custom_call_target="tpu_custom_call" | custom-call | tf_op jit(solution)/shard_map/pallas_call | solution.py:412
  (15 shorter events, 0.1 us)
Async XLA Ops:
  2.2 15.7 %all-to-all-start = ((f32[32,8,128]{2,1,0:T(8,128)}), f32[32,8,128]{2,1,0:T(8,128)S(1)}, u32[]{:S(2)}, u32[]{:S(2)}) async-start(f32[32,8,128]{2,1,0:T(8,128)} %get-tuple-element.13), calls=%async_computation | async-start | bytes 262144 | tf_op jit(solution)/shard_map/all_to_all | solution.py:470
  9.5 12.6 %collective-permute-start = (f32[2,8,2304]{2,1,0:T(8,128)S(1)}, f32[2,8,2304]{2,1,0:T(8,128)S(1)}, u32[]{:S(2)}, u32[]{:S(2)}) collective-permute-start(f32[2,8,2304]{2,1,0:T(8,128)S(1)} %get-tuple-element.15), channel_id=1, source_target_pairs={{0,4},{4,0},{8,12},{12,8},{16,20},{20,16},{24,28},{28,24},{1,5},{5... | collective-permute-start | bytes 442376 | tf_op jit(solution)/shard_map/ppermute | solution.py:497
  9.8 12.3 %collective-permute-start.1 = (f32[2,8,2304]{2,1,0:T(8,128)S(1)}, f32[2,8,2304]{2,1,0:T(8,128)S(1)}, u32[]{:S(2)}, u32[]{:S(2)}) collective-permute-start(f32[2,8,2304]{2,1,0:T(8,128)S(1)} %get-tuple-element.16), channel_id=1, source_target_pairs={{4,8},{8,4},{12,16},{16,12},{20,24},{24,20},{5,9},{9,5},{13,17},{1... | collective-permute-start | bytes 442376 | tf_op jit(solution)/shard_map/ppermute | solution.py:498
  19.5 11.0 %all-to-all-start.1 = ((f32[32,8,128]{2,1,0:T(8,128)}), f32[32,8,128]{2,1,0:T(8,128)S(1)}, u32[]{:S(2)}, u32[]{:S(2)}) async-start(f32[32,8,128]{2,1,0:T(8,128)} %shard_map.101), calls=%async_computation.1 | async-start | bytes 262144 | tf_op jit(solution)/shard_map/all_to_all | solution.py:470
  30.5 15.4 %copy-start.3 = (bf16[2,192,128]{2,1,0:T(8,128)(2,1)S(1)}, bf16[2,192,128]{2,1,0:T(8,128)(2,1)}, u32[]{:S(2)}) copy-start(bf16[2,192,128]{2,1,0:T(8,128)(2,1)} %constant.71.clone.table_ref) | copy-start | bytes 294916
  30.5 28.4 %copy-start = (f32[4,8,2304]{2,1,0:T(8,128)S(1)}, f32[4,8,2304]{2,1,0:T(8,128)}, u32[]{:S(2)}) copy-start(f32[4,8,2304]{2,1,0:T(8,128)} %cells_ref.1) | copy-start | bytes 884740
  30.5 28.4 %copy-start.1 = (f32[3,3,36,108]{3,2,1,0:T(8,128)S(1)}, f32[3,3,36,108]{3,2,1,0:T(8,128)}, u32[]{:S(2)}) copy-start(f32[3,3,36,108]{3,2,1,0:T(8,128)} %first_ref.1) | copy-start | bytes 419908
  34.7 29.6 %copy-start.2 = (f32[3,3,36,108]{3,2,1,0:T(8,128)S(1)}, f32[3,3,36,108]{3,2,1,0:T(8,128)}, u32[]{:S(2)}) copy-start(f32[3,3,36,108]{3,2,1,0:T(8,128)} %filter_ref.3) | copy-start | bytes 419908
  34.7 35.0 %copy-start.4 = (bf16[128,256]{1,0:T(8,128)(2,1)S(1)}, bf16[128,256]{1,0:T(8,128)(2,1)}, u32[]{:S(2)}) copy-start(bf16[128,256]{1,0:T(8,128)(2,1)} %constant.73.clone.lo_ref) | copy-start | bytes 196612
  34.7 35.0 %copy-start.5 = (bf16[128,256]{1,0:T(8,128)(2,1)S(1)}, bf16[128,256]{1,0:T(8,128)(2,1)}, u32[]{:S(2)}) copy-start(bf16[128,256]{1,0:T(8,128)(2,1)} %constant.72.clone.hi_ref) | copy-start | bytes 196612
  34.8 11.1 %all-to-all-start.2 = ((f32[32,8,128]{2,1,0:T(8,128)}), f32[32,8,128]{2,1,0:T(8,128)S(1)}, u32[]{:S(2)}, u32[]{:S(2)}) async-start(f32[32,8,128]{2,1,0:T(8,128)} %shard_map.102), calls=%async_computation.2 | async-start | bytes 262144 | tf_op jit(solution)/shard_map/all_to_all | solution.py:470
  37.6 13.9 %collective-permute-start.2 = (f32[8,2,2304]{2,1,0:T(2,128)S(1)}, f32[8,2,2304]{2,1,0:T(2,128)S(1)}, u32[]{:S(2)}, u32[]{:S(2)}) collective-permute-start(f32[8,2,2304]{2,1,0:T(2,128)S(1)} %pad_maximum_fusion), channel_id=1, source_target_pairs={{0,1},{1,2},{2,3},{4,5},{5,6},{6,7},{8,9},{9,10},{10,11},{12,13},{... | collective-permute-start | bytes 442376 | tf_op jit(solution)/shard_map/ppermute | solution.py:474
  47.5 22.3 %all-to-all-start.3 = ((f32[32,8,128]{2,1,0:T(8,128)}), f32[32,8,128]{2,1,0:T(8,128)S(1)}, u32[]{:S(2)}, u32[]{:S(2)}) async-start(f32[32,8,128]{2,1,0:T(8,128)} %shard_map.103), calls=%async_computation.3 | async-start | bytes 262144 | tf_op jit(solution)/shard_map/all_to_all | solution.py:470
  50.1 8.7 %collective-permute-start.3 = (f32[8,2,2304]{2,1,0:T(2,128)S(1)}, f32[8,2,2304]{2,1,0:T(2,128)S(1)}, u32[]{:S(2)}, u32[]{:S(2)}) collective-permute-start(f32[8,2,2304]{2,1,0:T(2,128)S(1)} %pad_maximum_fusion.1), channel_id=1, source_target_pairs={{1,0},{2,1},{3,2},{5,4},{6,5},{7,6},{9,8},{10,9},{11,10},{13,12},{... | collective-permute-start | bytes 442376 | tf_op jit(solution)/shard_map/ppermute | solution.py:474
